TPU v7x, 32 devices: a whole 2x2x4 slice. The times are simulated.
32 devices in a mesh: group: 8 (over z, y), lat: 2 (over x), rad: 2 (over core).
Axes of the slice: x: 2, y: 2, z: 4, core: 2. Of those that a mesh axis runs over, the one named last changes fastest.
Arguments:
- displacement_prev: float32 [3, 4, 128, 256], P(None, 'rad', 'group', 'lat'), may hold values from -2.5 to 2.5
- shear_modulus: float32 [4, 128, 256], P('rad', 'group', 'lat'), may hold values from 1 to 10
- viscosity: float32 [4, 128, 256], P('rad', 'group', 'lat'), may hold values from 0.5 to 20
- element_matrix: float32 [24, 24], replicated, as said below
- regrid_index: int32 [128, 2, 4], P('group', 'lat'), may hold values from 0 to 63
- regrid_weight: float32 [128, 2, 4], P('group', 'lat'), may hold values from 0.1 to 0.6
- ice_thickness: float32 [32, 256], P('lat'), may hold values from 0.5 to 4
- bed_elevation: float32 [32, 256], P('lat'), may hold values from -3 to 3
- basal_friction: float32 [32, 256], P('lat'), may hold values from 0.2 to 5
- ice_mask: int32 [32, 256], P('lat'), may hold values 0 or 1
- speed_guess: float32 [16, 32, 256], P(None, 'lat'), may hold values from -3 to 3
Outputs:
- displacement: float32 [3, 4, 128, 256], P(None, 'rad', 'group', 'lat')
- bed_new: float32 [32, 256], P('lat')
Inputs may be any that keep to these rules, and one draw needn't show every extreme that they name: `regrid_index`: names a block of the ice map: block b is row b // 2, columns 128 * (b % 2) to 128 * (b % 2) + 127. `element_matrix`: symmetric positive definite.
All inputs are finite; a program needn't handle non-finite values. No bound on the sum of `ice_mask` on one device may be relied on, other than what follows from the above.
Results may differ from a plain program's by a relative error of at most 0.0019.
Values may be sent and summed in bfloat16 or wider, within the bound.
No kernel may reach another device: no remote copies, remote signals or barrier semaphores. Data moves between devices by JAX's collectives and lax.ppermute only.
A program may use at most 64 MiB of HBM per device.

v0:
```python
import jax
import jax.numpy as jnp
from jax import lax
from jax.sharding import PartitionSpec as P

BLOCK = 128
SWEEPS = 6
ITERS = 4


LOAD_SCALE = 20.0
UPLIFT_SCALE = 0.5
TIME_SCALE = 1.0
ICE_STEP = 0.5
ASPECT = 0.01
STRAIN_FLOOR = 0.01
CORNERS = [
    (layer_bit, row_bit, col_bit)
    for layer_bit in (0, 1)
    for row_bit in (0, 1)
    for col_bit in (0, 1)
]


def padded(cells, sides, width):
    for axis, dim in sides:
        count = lax.axis_size(axis)
        ends = count - 1
        head = lax.slice_in_dim(cells, 0, width, axis=dim)
        tail = lax.slice_in_dim(cells, cells.shape[dim] - width, cells.shape[dim], axis=dim)
        cells = jnp.concatenate(
            [
                lax.ppermute(tail, axis, [(i, (i + 1) % count) for i in range(ends)]),
                cells,
                lax.ppermute(head, axis, [((i + 1) % count, i) for i in range(ends)]),
            ],
            axis=dim,
        )
    return cells


def broadcast(value, axis, source):
    kept = jnp.where(lax.axis_index(axis) == source, value, 0).astype(value.dtype)
    return lax.psum(kept, axis)


def corner_mean(padded_coef):
    layer_count = padded_coef.shape[0] - 1
    col_count = padded_coef.shape[1] - 1
    depth_count = padded_coef.shape[2] - 1
    summed = jnp.zeros((layer_count, col_count, depth_count), jnp.float32)
    for layer_bit, row_bit, col_bit in CORNERS:
        summed = (
            summed
            + padded_coef[
                layer_bit : layer_bit + layer_count,
                row_bit : row_bit + col_count,
                col_bit : col_bit + depth_count,
            ]
        )
    return summed / 8.0


def element_apply(padded_field, element_coef, kernel):
    layer_count, col_count, depth_count = element_coef.shape
    pieces = [
        padded_field[
            :,
            layer_bit : layer_bit + layer_count,
            row_bit : row_bit + col_count,
            col_bit : col_bit + depth_count,
        ]
        for layer_bit, row_bit, col_bit in CORNERS
    ]
    stacked = jnp.concatenate(pieces, 0)
    forces = (
        jnp.einsum("pq,qrab->prab", kernel, stacked, precision=lax.Precision.HIGHEST) * element_coef
    )
    summed = jnp.zeros((3, layer_count - 1, col_count - 1, depth_count - 1), jnp.float32)
    for corner_id, (layer_bit, row_bit, col_bit) in enumerate(CORNERS):
        summed = (
            summed
            + forces[
                3 * corner_id : 3 * corner_id + 3,
                1 - layer_bit : layer_count - layer_bit,
                1 - row_bit : col_count - row_bit,
                1 - col_bit : depth_count - col_bit,
            ]
        )
    return summed


def column_neighbours(values):
    zero_col = jnp.zeros_like(values[..., :1])
    east_side = jnp.concatenate([values[..., 1:], zero_col], -1)
    west_side = jnp.concatenate([zero_col, values[..., :-1]], -1)
    return (east_side, west_side)


def ice_sweep(velocity, padded_speed, thickness, friction, driving):
    levels = velocity.shape[0]
    north_side = padded_speed[:, 2:, :]
    south_side = padded_speed[:, :-2, :]
    east_side, west_side = column_neighbours(velocity)
    inverse = (levels - 1) / thickness
    slope_rows = 0.5 * (north_side - south_side)
    slope_cols = 0.5 * (east_side - west_side)
    slope_levels = (
        jnp.concatenate(
            [
                velocity[1:2] - velocity[0:1],
                0.5 * (velocity[2:] - velocity[:-2]),
                velocity[-1:] - velocity[-2:-1],
            ],
            0,
        )
        * inverse
    )
    strain = slope_rows**2 + 0.25 * slope_cols**2 + 0.25 * slope_levels**2 + STRAIN_FLOOR
    stiffness = 0.5 * strain ** (-1.0 / 3.0)
    vertical = ASPECT * inverse**2 * 0.5 * (stiffness[1:] + stiffness[:-1])
    neighbours = stiffness * (north_side + south_side + east_side + west_side)
    factors = []
    upper_prev = None
    values_prev = None
    for level_id in range(levels):
        diagonal = 4.0 * stiffness[level_id]
        if level_id > 0:
            diagonal = diagonal + vertical[level_id - 1]
        if level_id < levels - 1:
            diagonal = diagonal + vertical[level_id]
        if level_id == 0:
            diagonal = diagonal + friction
        right_side = driving + neighbours[level_id]
        if level_id > 0:
            lower_coef = -vertical[level_id - 1]
            diagonal = diagonal - lower_coef * upper_prev
            right_side = right_side - lower_coef * values_prev
        upper_prev = -vertical[level_id] / diagonal if level_id < levels - 1 else None
        values_prev = right_side / diagonal
        factors.append((upper_prev, values_prev))
    solution = [None] * levels
    solution[levels - 1] = factors[levels - 1][1]
    for level_id in range(levels - 2, -1, -1):
        solution[level_id] = factors[level_id][1] - factors[level_id][0] * solution[level_id + 1]
    return jnp.stack(solution, 0)


def ice_tile_load(is_ice, ice_thickness, bed_elevation, basal_friction, ice_mask, speed_guess):
    ice_present = ice_mask.astype(jnp.float32)
    surface = bed_elevation + ice_thickness
    padded_surface = padded(surface, (("lat", 0),), 1)
    driving = -ice_present * ice_thickness * 0.5 * (padded_surface[2:] - padded_surface[:-2])
    velocity = speed_guess
    for sweep_id in range(SWEEPS):
        padded_speed = padded(velocity, (("lat", 1),), 1)

        def run_sweep(operands):
            return ice_sweep(operands[0], operands[1], ice_thickness, basal_friction, driving)

        def keep_speed(operands):
            return operands[0]

        velocity = lax.cond(is_ice, run_sweep, keep_speed, (velocity, padded_speed))
    ice_flux = ice_thickness * jnp.mean(velocity, 0)
    padded_flux = padded(ice_flux, (("lat", 0),), 1)
    new_thickness = ice_thickness - ICE_STEP * 0.5 * (padded_flux[2:] - padded_flux[:-2])
    ice_load = (ice_present * new_thickness).astype(jnp.bfloat16)
    return jnp.where(is_ice, ice_load, jnp.zeros_like(ice_load))


def per_device(
    displacement_prev,
    shear_modulus,
    viscosity,
    element_matrix,
    regrid_index,
    regrid_weight,
    ice_thickness,
    bed_elevation,
    basal_friction,
    ice_mask,
    speed_guess,
):
    ice_root = lax.axis_size("group") - 1
    is_ice = lax.axis_index("group") == ice_root
    shell_group = (lax.axis_index("group") < ice_root).astype(jnp.float32)
    top_core = (lax.axis_index("rad") == 0).astype(jnp.float32)
    relax_ratio = TIME_SCALE * shear_modulus / viscosity
    modulus = shell_group * shear_modulus / (1.0 + relax_ratio)
    relaxed = modulus * relax_ratio / (1.0 + relax_ratio)
    start_field = displacement_prev * shell_group
    joined = jnp.concatenate([start_field, modulus[None], relaxed[None]], 0)
    padded_all = padded(joined, (("group", 2), ("lat", 3), ("rad", 1)), 1)
    coef_main = corner_mean(padded_all[3])
    coef_relax = corner_mean(padded_all[4])
    ice_load = ice_tile_load(
        is_ice, ice_thickness, bed_elevation, basal_friction, ice_mask, speed_guess
    )

    def skip_shell(unused):
        return jnp.zeros(start_field.shape, jnp.float32)

    def shell_branch(unused):
        return element_apply(padded_all[:3], coef_relax, element_matrix) * shell_group

    relax_force = lax.cond(is_ice, skip_shell, shell_branch, 0)
    shell_tile = broadcast(ice_load, "group", ice_root)
    ice_field = lax.all_gather(shell_tile, "lat", axis=0, tiled=True)
    row_count = regrid_index.shape[0]
    flat_index = regrid_index.reshape(-1)
    weights = regrid_weight.reshape(row_count, -1)
    blocks = ice_field.reshape(-1, BLOCK)
    picked = jnp.take(blocks, flat_index, axis=0).astype(jnp.float32).reshape(row_count, -1, BLOCK)
    surface_thickness = jnp.sum(weights[..., None] * picked, 1)
    load_field = (
        jnp.zeros(start_field.shape, jnp.float32)
        .at[2, 0]
        .set(-LOAD_SCALE * surface_thickness * top_core * shell_group)
    )
    residual = load_field - relax_force

    def global_norm(values):
        return lax.psum(jnp.sum(values * values), ("group", "lat", "rad"))

    solution = start_field
    direction = residual
    norm_now = global_norm(residual)
    for iter_id in range(ITERS):
        padded_field = padded(direction, (("group", 2), ("lat", 3), ("rad", 1)), 1)
        mapped = element_apply(padded_field, coef_main, element_matrix) * shell_group
        step_size = norm_now / lax.psum(jnp.sum(direction * mapped), ("group", "lat", "rad"))
        solution = solution + step_size * direction
        residual = residual - step_size * mapped
        norm_next = global_norm(residual)
        direction = residual + norm_next / norm_now * direction
        norm_now = norm_next
    layer_total = solution.shape[1] * lax.axis_size("rad")
    surface_lift = jnp.sum(solution[2], 0) / layer_total
    contrib = (weights[..., None] * surface_lift[:, None, :]).reshape(-1, BLOCK)
    tile_height = 2 * ice_thickness.shape[0]
    targets = lax.broadcasted_iota(
        jnp.int32, (tile_height * lax.axis_size("lat"), flat_index.shape[0]), 0
    )
    selector = (targets == flat_index[None, :]).astype(jnp.float32)
    all_lift = lax.psum(
        jnp.dot(
            selector, contrib, precision=lax.Precision.HIGHEST, preferred_element_type=jnp.float32
        ),
        ("group", "lat", "rad"),
    )
    own_lift = lax.dynamic_slice_in_dim(
        all_lift, lax.axis_index("lat") * tile_height, tile_height, 0
    )
    bed_new = bed_elevation + UPLIFT_SCALE * own_lift.reshape(bed_elevation.shape)
    return (solution, bed_new)


def solution(mesh):
    in_specs = (
        P(None, "rad", "group", "lat"),
        P("rad", "group", "lat"),
        P("rad", "group", "lat"),
        P(),
        P("group", "lat", None),
        P("group", "lat", None),
        P("lat", None),
        P("lat", None),
        P("lat", None),
        P("lat", None),
        P(None, "lat", None),
    )
    out_specs = (P(None, "rad", "group", "lat"), P("lat", None))
    return jax.shard_map(
        per_device, mesh=mesh, in_specs=in_specs, out_specs=out_specs, check_vma=False
    )
```

profile of v0, /device:TPU:0, one launch (start us, length us, event | category | flops | bytes accessed | tf_op | source)
XLA Modules:
  0.0 650.5 jit_solution(13611516230514924410)
XLA Ops:
  0.7 1.7 copy.132
  5.3 5.5 collective-permute-start.16
  13.8 4.5 collective-permute-start.3
  21.3 4.5 collective-permute-start
  30.6 4.5 collective-permute-start.4
  40.4 4.5 collective-permute-start.6
  45.1 1.3 collective-permute-done.6
  49.7 4.5 collective-permute-start.8
  55.7 4.6 collective-permute-start.18
  63.6 4.5 collective-permute-start.10
  72.9 4.5 collective-permute-start.12
  78.8 3.0 collective-permute-start.20
  85.8 1.9 collective-permute-start.15
  89.9 7.3 %conditional.13 = (f32[3,2,16,128]{3,0,2,1:T(4,128)S(1)}) conditional(s32[]{:T(128)} %convert_element_type.28, (f32[5,4,18,130]{3,0,2,1:T(8,128)S(1)}, f32[24,24]{1,0:T(8,128)S(1)}, f32[3,17,129]{2,0,1:T(4,128)}, f32[]{:T(128)}) %tuple.375, () %tuple.72), branch_computations={%region_15.16_spmd, %region_16.17_spmd} | conditional | flops 45782880 | bytes 5078236 | solution.py:207
  90.4 4.3 concatenate.158
  98.1 87.5 %psum.70 = bf16[16,256]{1,0:T(8,128)(2,1)S(1)} all-reduce(bf16[16,256]{1,0:T(8,128)(2,1)S(1)} %select_select_fusion), channel_id=1, replica_groups=mesh['group'=8,'lat'=2,'rad'=2] {'group'}, use_global_device_ids=true, to_apply=%region_13.14 | all-reduce | flops 4096 | bytes 16384 | tf_op jit(solution)/shard_map/psum | solution.py:44
  185.6 4.4 all_gather.3
  192.9 4.5 collective-permute-start.22
  197.5 1.3 collective-permute-done.22
  200.2 4.5 collective-permute-start.24
  205.1 1.6 collective-permute-done.24
  208.2 3.0 collective-permute-start.26
  213.0 4.3 concatenate.211
  219.4 40.3 %all-reduce.13 = (f32[]{:T(128)}, f32[]{:T(128)}) all-reduce(f32[]{:T(128)} %get-tuple-element.190, f32[]{:T(128)} %get-tuple-element.189), channel_id=1, replica_groups=mesh['group'=8,'lat'=2,'rad'=2] {'group','lat','rad'}, use_global_device_ids=true, to_apply=%region_18.19 | all-reduce | flops 2 | bytes 16 | tf_op jit(solution)/shard_map/psum | solution.py:224
  261.7 40.9 %psum.73 = f32[]{:T(128)} all-reduce(f32[]{:T(128)} %multiply_reduce_fusion.4), channel_id=1, replica_groups=mesh['group'=8,'lat'=2,'rad'=2] {'group','lat','rad'}, use_global_device_ids=true, to_apply=%region_22.23 | all-reduce | flops 1 | bytes 8 | tf_op jit(solution)/shard_map/psum | solution.py:224
  305.2 5.0 collective-permute-start.28
  310.3 1.3 collective-permute-done.28
  313.0 4.5 collective-permute-start.30
  317.9 1.6 collective-permute-done.30
  321.0 3.3 collective-permute-start.32
  325.8 4.3 concatenate.216
  332.2 43.2 %psum.74 = f32[]{:T(128)} all-reduce(f32[]{:T(128)} %get-tuple-element.399), channel_id=1, replica_groups=mesh['group'=8,'lat'=2,'rad'=2] {'group','lat','rad'}, use_global_device_ids=true, to_apply=%region_24.25 | all-reduce | flops 1 | bytes 8 | tf_op jit(solution)/shard_map/psum | solution.py:232
  377.3 40.4 %psum.75 = f32[]{:T(128)} all-reduce(f32[]{:T(128)} %get-tuple-element.397), channel_id=1, replica_groups=mesh['group'=8,'lat'=2,'rad'=2] {'group','lat','rad'}, use_global_device_ids=true, to_apply=%region_26.27 | all-reduce | flops 1 | bytes 8 | tf_op jit(solution)/shard_map/psum | solution.py:224
  420.4 5.0 collective-permute-start.34
  425.4 1.3 collective-permute-done.34
  428.1 4.5 collective-permute-start.36
  433.1 1.6 collective-permute-done.36
  436.2 3.0 collective-permute-start.38
  441.0 4.3 concatenate.221
  447.3 43.4 %psum.76 = f32[]{:T(128)} all-reduce(f32[]{:T(128)} %get-tuple-element.395), channel_id=1, replica_groups=mesh['group'=8,'lat'=2,'rad'=2] {'group','lat','rad'}, use_global_device_ids=true, to_apply=%region_28.29 | all-reduce | flops 1 | bytes 8 | tf_op jit(solution)/shard_map/psum | solution.py:232
  492.7 41.1 %psum.77 = f32[]{:T(128)} all-reduce(f32[]{:T(128)} %multiply_reduce_fusion), channel_id=1, replica_groups=mesh['group'=8,'lat'=2,'rad'=2] {'group','lat','rad'}, use_global_device_ids=true, to_apply=%region_30.31 | all-reduce | flops 1 | bytes 8 | tf_op jit(solution)/shard_map/psum | solution.py:224
  536.5 5.0 collective-permute-start.40
  544.3 4.5 collective-permute-start.42
  549.2 1.6 collective-permute-done.42
  552.3 3.3 collective-permute-start.44
  557.1 4.3 concatenate.226
  563.5 43.2 %psum.78 = f32[]{:T(128)} all-reduce(f32[]{:T(128)} %fusion.707), channel_id=1, replica_groups=mesh['group'=8,'lat'=2,'rad'=2] {'group','lat','rad'}, use_global_device_ids=true, to_apply=%region_32.33 | all-reduce | flops 1 | bytes 8 | tf_op jit(solution)/shard_map/psum | solution.py:232
  609.0 40.8 %psum.79 = f32[64,128]{1,0:T(8,128)S(1)} all-reduce(f32[64,128]{1,0:T(8,128)S(1)} %fusion.711), channel_id=1, replica_groups=mesh['group'=8,'lat'=2,'rad'=2] {'group','lat','rad'}, use_global_device_ids=true, to_apply=%region_34.35 | all-reduce | flops 8192 | bytes 65536 | tf_op jit(solution)/shard_map/psum | solution.py:246
  (188 shorter events, 83.1 us)
Async XLA Ops:
  4.0 41.0 %collective-permute-start.17 = (f32[5,2,1,128]{3,0,2,1:T(8,128)S(1)}, f32[5,2,1,128]{3,0,2,1:T(8,128)S(1)}, u32[]{:S(2)}, u32[]{:S(2)}) collective-permute-start(f32[5,2,1,128]{3,0,2,1:T(8,128)S(1)} %get-tuple-element.513), channel_id=1, source_target_pairs={{4,0},{8,4},{12,8},{16,12},{20,16},{24,20},{28,24},{5,1},{9,5},{13... | collective-permute-start | bytes 15368 | tf_op jit(solution)/shard_map/ppermute | solution.py:35
  5.3 39.7 %collective-permute-start.16 = (f32[5,2,1,128]{3,0,2,1:T(8,128)S(1)}, f32[5,2,1,128]{3,0,2,1:T(8,128)S(1)}, u32[]{:S(2)}, u32[]{:S(2)}) collective-permute-start(f32[5,2,1,128]{3,0,2,1:T(8,128)S(1)} %get-tuple-element.512), channel_id=1, source_target_pairs={{0,4},{4,8},{8,12},{12,16},{16,20},{20,24},{24,28},{1,5},{5,9},{9,... | collective-permute-start | bytes 15368 | tf_op jit(solution)/shard_map/ppermute | solution.py:33
  11.8 14.8 %collective-permute-start.1 = (f32[16,1,256]{2,1,0:T(1,128)S(1)}, f32[16,1,256]{2,1,0:T(1,128)S(1)}, u32[]{:S(2)}, u32[]{:S(2)}) collective-permute-start(f32[16,1,256]{2,1,0:T(1,128)S(1)} %get-tuple-element.461), channel_id=1, source_target_pairs={{2,0},{3,1},{6,4},{7,5},{10,8},{11,9},{14,12},{15,13},{18,16},{19,... | collective-permute-start | bytes 49160 | tf_op jit(solution)/shard_map/ppermute | solution.py:35
  13.8 7.4 %collective-permute-start.3 = (f32[1,256]{1,0:T(1,128)S(1)}, f32[1,256]{1,0:T(1,128)S(1)}, u32[]{:S(2)}, u32[]{:S(2)}) collective-permute-start(f32[1,256]{1,0:T(1,128)S(1)} %get-tuple-element.533), channel_id=1, source_target_pairs={{0,2},{1,3},{4,6},{5,7},{8,10},{9,11},{12,14},{13,15},{16,18},{17,... | collective-permute-start | bytes 3080 | tf_op jit(solution)/shard_map/ppermute | solution.py:33
  18.4 7.4 %collective-permute-start.2 = (f32[1,256]{1,0:T(1,128)S(1)}, f32[1,256]{1,0:T(1,128)S(1)}, u32[]{:S(2)}, u32[]{:S(2)}) collective-permute-start(f32[1,256]{1,0:T(1,128)S(1)} %get-tuple-element.532), channel_id=1, source_target_pairs={{2,0},{3,1},{6,4},{7,5},{10,8},{11,9},{14,12},{15,13},{18,16},{19,... | collective-permute-start | bytes 3080 | tf_op jit(solution)/shard_map/ppermute | solution.py:35
  21.3 6.0 collective-permute-start
  29.3 7.8 %collective-permute-start.5 = (f32[16,1,256]{2,1,0:T(1,128)S(1)}, f32[16,1,256]{2,1,0:T(1,128)S(1)}, u32[]{:S(2)}, u32[]{:S(2)}) collective-permute-start(f32[16,1,256]{2,1,0:T(1,128)S(1)} %get-tuple-element.459), channel_id=1, source_target_pairs={{2,0},{3,1},{6,4},{7,5},{10,8},{11,9},{14,12},{15,13},{18,16},{19,... | collective-permute-start | bytes 49160 | tf_op jit(solution)/shard_map/ppermute | solution.py:35
  30.6 6.5 %collective-permute-start.4 = (f32[16,1,256]{2,1,0:T(1,128)S(1)}, f32[16,1,256]{2,1,0:T(1,128)S(1)}, u32[]{:S(2)}, u32[]{:S(2)}) collective-permute-start(f32[16,1,256]{2,1,0:T(1,128)S(1)} %get-tuple-element.458), channel_id=1, source_target_pairs={{0,2},{1,3},{4,6},{5,7},{8,10},{9,11},{12,14},{13,15},{16,18},{17,... | collective-permute-start | bytes 49160 | tf_op jit(solution)/shard_map/ppermute | solution.py:33
  39.1 5.9 collective-permute-start.7
  40.4 6.0 collective-permute-start.6
  48.4 11.8 %collective-permute-start.9 = (f32[16,1,256]{2,1,0:T(1,128)S(1)}, f32[16,1,256]{2,1,0:T(1,128)S(1)}, u32[]{:S(2)}, u32[]{:S(2)}) collective-permute-start(f32[16,1,256]{2,1,0:T(1,128)S(1)} %get-tuple-element.455), channel_id=1, source_target_pairs={{2,0},{3,1},{6,4},{7,5},{10,8},{11,9},{14,12},{15,13},{18,16},{19,... | collective-permute-start | bytes 49160 | tf_op jit(solution)/shard_map/ppermute | solution.py:35
  49.7 10.5 %collective-permute-start.8 = (f32[16,1,256]{2,1,0:T(1,128)S(1)}, f32[16,1,256]{2,1,0:T(1,128)S(1)}, u32[]{:S(2)}, u32[]{:S(2)}) collective-permute-start(f32[16,1,256]{2,1,0:T(1,128)S(1)} %get-tuple-element.454), channel_id=1, source_target_pairs={{0,2},{1,3},{4,6},{5,7},{8,10},{9,11},{12,14},{13,15},{16,18},{17,... | collective-permute-start | bytes 49160 | tf_op jit(solution)/shard_map/ppermute | solution.py:33
  54.4 13.8 %collective-permute-start.19 = (f32[5,2,18,1]{3,0,2,1:T(8,128)S(1)}, f32[5,2,18,1]{3,0,2,1:T(8,128)S(1)}, u32[]{:S(2)}, u32[]{:S(2)}) collective-permute-start(f32[5,2,18,1]{3,0,2,1:T(8,128)S(1)} %get-tuple-element.511), channel_id=1, source_target_pairs={{2,0},{3,1},{6,4},{7,5},{10,8},{11,9},{14,12},{15,13},{18,16},{19,... | collective-permute-start | bytes 2168 | tf_op jit(solution)/shard_map/ppermute | solution.py:35
  55.7 12.5 %collective-permute-start.18 = (f32[5,2,18,1]{3,0,2,1:T(8,128)S(1)}, f32[5,2,18,1]{3,0,2,1:T(8,128)S(1)}, u32[]{:S(2)}, u32[]{:S(2)}) collective-permute-start(f32[5,2,18,1]{3,0,2,1:T(8,128)S(1)} %get-tuple-element.510), channel_id=1, source_target_pairs={{0,2},{1,3},{4,6},{5,7},{8,10},{9,11},{12,14},{13,15},{16,18},{17,... | collective-permute-start | bytes 2168 | tf_op jit(solution)/shard_map/ppermute | solution.py:33
  62.3 6.2 collective-permute-start.11
  63.6 6.0 collective-permute-start.10
  71.6 10.2 %collective-permute-start.13 = (f32[16,1,256]{2,1,0:T(1,128)S(1)}, f32[16,1,256]{2,1,0:T(1,128)S(1)}, u32[]{:S(2)}, u32[]{:S(2)}) collective-permute-start(f32[16,1,256]{2,1,0:T(1,128)S(1)} %get-tuple-element.451), channel_id=1, source_target_pairs={{2,0},{3,1},{6,4},{7,5},{10,8},{11,9},{14,12},{15,13},{18,16},{19,... | collective-permute-start | bytes 49160 | tf_op jit(solution)/shard_map/ppermute | solution.py:35
  72.9 8.9 %collective-permute-start.12 = (f32[16,1,256]{2,1,0:T(1,128)S(1)}, f32[16,1,256]{2,1,0:T(1,128)S(1)}, u32[]{:S(2)}, u32[]{:S(2)}) collective-permute-start(f32[16,1,256]{2,1,0:T(1,128)S(1)} %get-tuple-element.450), channel_id=1, source_target_pairs={{0,2},{1,3},{4,6},{5,7},{8,10},{9,11},{12,14},{13,15},{16,18},{17,... | collective-permute-start | bytes 49160 | tf_op jit(solution)/shard_map/ppermute | solution.py:33
  77.5 11.5 %collective-permute-start.21 = (f32[5,1,18,130]{3,0,2,1:T(8,128)S(1)}, f32[5,1,18,130]{3,0,2,1:T(8,128)S(1)}, u32[]{:S(2)}, u32[]{:S(2)}) collective-permute-start(f32[5,1,18,130]{3,0,2,1:T(8,128)S(1)} %get-tuple-element.449), channel_id=1, source_target_pairs={{1,0},{3,2},{5,4},{7,6},{9,8},{11,10},{13,12},{15,14},{17,16},{19,... | collective-permute-start | bytes 140408 | tf_op jit(solution)/shard_map/ppermute | solution.py:35
  78.8 10.2 %collective-permute-start.20 = (f32[5,1,18,130]{3,0,2,1:T(8,128)S(1)}, f32[5,1,18,130]{3,0,2,1:T(8,128)S(1)}, u32[]{:S(2)}, u32[]{:S(2)}) collective-permute-start(f32[5,1,18,130]{3,0,2,1:T(8,128)S(1)} %get-tuple-element.448), channel_id=1, source_target_pairs={{0,1},{2,3},{4,5},{6,7},{8,9},{10,11},{12,13},{14,15},{16,17},{18,... | collective-permute-start | bytes 140408 | tf_op jit(solution)/shard_map/ppermute | solution.py:33
  85.8 11.4 %collective-permute-start.15 = (f32[1,256]{1,0:T(1,128)}, f32[1,256]{1,0:T(1,128)}, u32[]{:S(2)}, u32[]{:S(2)}) collective-permute-start(f32[1,256]{1,0:T(1,128)} %get-tuple-element.531), channel_id=1, source_target_pairs={{0,2},{1,3},{4,6},{5,7},{8,10},{9,11},{12,14},{13,15},{16,18},{17,... | collective-permute-start | bytes 3080 | tf_op jit(solution)/shard_map/ppermute | solution.py:33
  87.6 9.6 %collective-permute-start.14 = (f32[1,256]{1,0:T(1,128)}, f32[1,256]{1,0:T(1,128)}, u32[]{:S(2)}, u32[]{:S(2)}) collective-permute-start(f32[1,256]{1,0:T(1,128)} %get-tuple-element.530), channel_id=1, source_target_pairs={{2,0},{3,1},{6,4},{7,5},{10,8},{11,9},{14,12},{15,13},{18,16},{19,... | collective-permute-start | bytes 3080 | tf_op jit(solution)/shard_map/ppermute | solution.py:35
  191.6 5.9 collective-permute-start.23
  192.9 5.9 collective-permute-start.22
  198.9 6.2 collective-permute-start.25
  200.2 6.5 %collective-permute-start.24 = (f32[3,2,18,1]{3,0,2,1:T(4,128)S(1)}, f32[3,2,18,1]{3,0,2,1:T(4,128)S(1)}, u32[]{:S(2)}, u32[]{:S(2)}) collective-permute-start(f32[3,2,18,1]{3,0,2,1:T(4,128)S(1)} %get-tuple-element.520), channel_id=1, source_target_pairs={{0,2},{1,3},{4,6},{5,7},{8,10},{9,11},{12,14},{13,15},{16,18},{17,... | collective-permute-start | bytes 1304 | tf_op jit(solution)/shard_map/ppermute | solution.py:33
  206.9 4.6 collective-permute-start.27
  208.2 3.9 collective-permute-start.26
  303.9 6.3 collective-permute-start.29
  305.2 6.3 collective-permute-start.28
  311.7 6.2 collective-permute-start.31
  313.0 6.5 %collective-permute-start.30 = (f32[3,2,18,1]{3,0,2,1:T(4,128)S(1)}, f32[3,2,18,1]{3,0,2,1:T(4,128)S(1)}, u32[]{:S(2)}, u32[]{:S(2)}) collective-permute-start(f32[3,2,18,1]{3,0,2,1:T(4,128)S(1)} %get-tuple-element.518), channel_id=1, source_target_pairs={{0,2},{1,3},{4,6},{5,7},{8,10},{9,11},{12,14},{13,15},{16,18},{17,... | collective-permute-start | bytes 1304 | tf_op jit(solution)/shard_map/ppermute | solution.py:33
  319.7 4.6 collective-permute-start.33
  321.0 3.9 collective-permute-start.32
  419.1 6.3 collective-permute-start.35
  420.4 6.3 collective-permute-start.34
  426.8 6.2 collective-permute-start.37
  428.1 6.5 %collective-permute-start.36 = (f32[3,2,18,1]{3,0,2,1:T(4,128)S(1)}, f32[3,2,18,1]{3,0,2,1:T(4,128)S(1)}, u32[]{:S(2)}, u32[]{:S(2)}) collective-permute-start(f32[3,2,18,1]{3,0,2,1:T(4,128)S(1)} %get-tuple-element.516), channel_id=1, source_target_pairs={{0,2},{1,3},{4,6},{5,7},{8,10},{9,11},{12,14},{13,15},{16,18},{17,... | collective-permute-start | bytes 1304 | tf_op jit(solution)/shard_map/ppermute | solution.py:33
  434.9 4.3 collective-permute-start.39
  436.2 3.9 collective-permute-start.38
  535.2 6.3 collective-permute-start.41
  536.5 6.3 collective-permute-start.40
  543.0 6.2 collective-permute-start.43
  544.3 6.5 %collective-permute-start.42 = (f32[3,2,18,1]{3,0,2,1:T(4,128)S(1)}, f32[3,2,18,1]{3,0,2,1:T(4,128)S(1)}, u32[]{:S(2)}, u32[]{:S(2)}) collective-permute-start(f32[3,2,18,1]{3,0,2,1:T(4,128)S(1)} %get-tuple-element.514), channel_id=1, source_target_pairs={{0,2},{1,3},{4,6},{5,7},{8,10},{9,11},{12,14},{13,15},{16,18},{17,... | collective-permute-start | bytes 1304 | tf_op jit(solution)/shard_map/ppermute | solution.py:33
  551.0 4.9 collective-permute-start.45
  552.3 3.9 collective-permute-start.44
  561.4 46.6 %copy-start.4 = (f32[3,2,16,128]{3,2,1,0:T(8,128)S(1)}, f32[3,2,16,128]{3,2,1,0:T(8,128)}, u32[]{:S(2)}) copy-start(f32[3,2,16,128]{3,2,1,0:T(8,128)} %param.27) | copy-start | bytes 147460
  562.7 87.2 %copy-start.5 = (f32[16,256]{1,0:T(8,128)S(1)}, f32[16,256]{1,0:T(8,128)}, u32[]{:S(2)}) copy-start(f32[16,256]{1,0:T(8,128)} %param.34) | copy-start | bytes 49156
  (5 other events, 69.6 us)
where the time goes:
time: 655 us; the launch traced here: 650 us
  blocking collectives  425 us (65%)
  starting transfers between devices  127 us (19%)
  local copies, waits for them, and re-layouts  39.4 us (6%)
  other arithmetic  22.9 us (3%)
  waiting for transfers between devices  18.6 us (3%)
  between operations  11.2 us (2%)
    psum x4, blocking collectives, global_norm(): return lax.psum(jnp.sum(values * values), ('group', 'lat', 'rad'))  163 us
    psum x3, blocking collectives, per_device(): lax.psum(jnp.sum(direction * mapped), ('group', 'lat', 'rad'))  130 us
    ppermute x23, starting transfers between devices, padded(): lax.ppermute(tail, axis, [(i, (i + 1) % count) for i in range(ends)])  97.1 us
    psum x1, blocking collectives, broadcast(): return lax.psum(kept, axis)  87.5 us
    psum x1, blocking collectives, per_device(): lax.psum(jnp.dot(selector, contrib, precision=lax.Precision.HIGHEST, pref...  40.8 us
    ppermute x23, starting transfers between devices, padded(): lax.ppermute(head, axis, [((i + 1) % count, i) for i in range(ends)])  29.7 us
    concatenate x5, local copies, waits for them, and re-layouts, element_apply(): stacked = jnp.concatenate(pieces, 0)  21.6 us
    ppermute x23, waiting for transfers between devices, padded(): lax.ppermute(tail, axis, [(i, (i + 1) % count) for i in range(ends)])  17.1 us
  transfers between devices with their start and end apart: 46, of which 19 were waited for; matrix products, arithmetic and copies ran while one was open for 4% of the time, Pallas kernels for 0%

commit v1 on v0

v1 whole, which is shorter than its diff:
```python
import functools

import jax
import jax.numpy as jnp
import numpy as np
from jax import lax
from jax.experimental import pallas as pl
from jax.experimental.pallas import tpu as pltpu
from jax.sharding import PartitionSpec as P

SWEEPS = 6
ITERS = 4
HALO = 8
COMPS = 3
LAYERS = 4
PAIR = 2 * LAYERS
VEC = COMPS * PAIR
LOAD_SCALE = 20.0
UPLIFT_SCALE = 0.5
ASPECT = 0.01
STRAIN_FLOOR = 0.01
TYPICAL_MODULUS = 2.2

F32 = jnp.float32
BF16 = jnp.bfloat16


def vmem():
    return pl.BlockSpec(memory_space=pltpu.VMEM)


def iota(shape, dim):
    return lax.broadcasted_iota(jnp.int32, shape, dim)


def shift_lanes(x, step):
    size = x.shape[1]
    lanes = iota(x.shape, 1)
    edge = size - 1 if step == 1 else 0
    return jnp.where(lanes == edge, 0.0, pltpu.roll(x, size - 1 if step == 1 else 1, 1))


def ice_kernel(*refs, masked):
    if masked:
        speed, thick, bed, fric, mask, before, after, out, S, PL, ST, RH = refs
    else:
        speed, thick, bed, fric, mask, halo, out, S, PL, ST, RH = refs
    levels, own_rows, cols = speed.shape
    lat = lax.axis_index("lat")
    window = ST.shape[1]
    planes = (thick, bed, fric, mask)
    S[:, 0:HALO, :] = jnp.zeros((levels, HALO, cols), F32)
    S[:, HALO + window :, :] = jnp.zeros((levels, HALO, cols), F32)
    PL[:, 0:HALO, :] = jnp.zeros((5, HALO, cols), F32)
    PL[:, HALO + window :, :] = jnp.zeros((5, HALO, cols), F32)

    def place(start, speeds, four):
        rows = pl.ds(pl.multiple_of(HALO + start, 8), speeds.shape[1])
        S[:, rows, :] = speeds
        for n in range(4):
            PL[n, rows, :] = four[n]

    own_four = [thick[...], bed[...], fric[...], mask[...].astype(F32)]
    if masked:
        own_at = HALO
        place(own_at, speed[...], own_four)
        place(0, before[:levels], [before[levels + n] for n in range(4)])
        place(HALO + own_rows, after[:levels], [after[levels + n] for n in range(4)])
    else:
        own_at = lat * HALO
        place(own_at, speed[...], own_four)
        place((1 - lat) * own_rows, halo[:levels], [halo[levels + n] for n in range(4)])
    tiles = range(window // 8)

    def rows_of(t, by=0):
        return slice(HALO + 8 * t + by, HALO + 8 * t + 8 + by)

    PL[4, HALO : HALO + window] = (
        PL[0, HALO : HALO + window] + PL[1, HALO : HALO + window]
    )
    for t in tiles:
        thickness = PL[0, rows_of(t)]
        PL[1, rows_of(t)] = (
            -0.5 * PL[3, rows_of(t)] * thickness * (PL[4, rows_of(t, 1)] - PL[4, rows_of(t, -1)])
        )
    if masked:
        count = lax.axis_size("lat")

        def inside(t):
            row = iota((8, cols), 0) + (8 * t - HALO)
            top = jnp.where(lat == 0, 0, -HALO)
            end = jnp.where(lat == count - 1, own_rows, own_rows + HALO)
            return jnp.logical_and(row >= top, row < end)

    def inverse_of(t):
        thickness = PL[0, rows_of(t)]
        if masked:
            thickness = jnp.where(inside(t), thickness, 1.0)
        return (levels - 1) / thickness

    lanes = iota((8, cols), 1)
    first, last = lanes == 0, lanes == cols - 1

    def sweep(_, carry):
        for t in tiles:
            inverse = inverse_of(t)
            driving = PL[1, rows_of(t)]
            for k in range(levels):
                here = S[k, rows_of(t)]
                north = S[k, rows_of(t, 1)]
                south = S[k, rows_of(t, -1)]
                east = jnp.where(last, 0.0, pltpu.roll(here, cols - 1, 1))
                west = jnp.where(first, 0.0, pltpu.roll(here, 1, 1))
                above = S[min(k + 1, levels - 1), rows_of(t)]
                below = S[max(k - 1, 0), rows_of(t)]
                by_level = (above - below) * inverse
                if k in (0, levels - 1):
                    by_level = 2.0 * by_level
                by_row = north - south
                by_col = east - west
                strain = (
                    0.25 * (by_row * by_row)
                    + 0.0625 * (by_col * by_col + by_level * by_level)
                    + STRAIN_FLOOR
                )
                stiffness = 0.5 * jnp.exp(jnp.log(strain) * (-1.0 / 3.0))
                ST[k, 8 * t : 8 * t + 8] = stiffness
                RH[k, 8 * t : 8 * t + 8] = driving + stiffness * (
                    (north + south) + (east + west)
                )
        scale = [(0.5 * ASPECT) * inverse_of(t) * inverse_of(t) for t in tiles]
        upper, value, vertical, stiff = {}, {}, {}, {}
        for k in range(levels):
            for t in tiles:
                rows = slice(8 * t, 8 * t + 8)
                current = ST[0, rows] if k == 0 else stiff[t]
                diagonal = 4.0 * current
                right = RH[k, rows]
                if k == 0:
                    diagonal = diagonal + PL[2, rows_of(t)]
                else:
                    diagonal = diagonal + vertical[t] * (1.0 - upper[t])
                    right = right + vertical[t] * value[t]
                if k < levels - 1:
                    stiff[t] = ST[k + 1, rows]
                    vertical[t] = scale[t] * (current + stiff[t])
                    diagonal = diagonal + vertical[t]
                invert = 1.0 / diagonal
                value[t] = right * invert
                RH[k, rows] = value[t]
                if k < levels - 1:
                    upper[t] = vertical[t] * invert
                    ST[k, rows] = upper[t]
        for k in range(levels - 1, -1, -1):
            for t in tiles:
                rows = slice(8 * t, 8 * t + 8)
                if k < levels - 1:
                    value[t] = RH[k, rows] + ST[k, rows] * value[t]
                fresh = value[t]
                if masked:
                    fresh = jnp.where(inside(t), fresh, 0.0)
                    value[t] = fresh
                S[k, rows_of(t)] = fresh
        return carry

    lax.fori_loop(0, SWEEPS, sweep, 0)
    for t in tiles:
        total = S[0, rows_of(t)]
        for k in range(1, levels):
            total = total + S[k, rows_of(t)]
        PL[4, rows_of(t)] = PL[0, rows_of(t)] * total * (1.0 / levels)
    for t in tiles:
        fresh = PL[0, rows_of(t)] - 0.25 * (PL[4, rows_of(t, 1)] - PL[4, rows_of(t, -1)])
        PL[1, rows_of(t)] = PL[3, rows_of(t)] * fresh
    out[...] = PL[1, pl.ds(pl.multiple_of(HALO + own_at, 8), own_rows), :].astype(BF16)


def ice_load_of(speed, thick, bed, fric, mask):
    levels, own_rows, cols = speed.shape
    count = lax.axis_size("lat")

    def edge(at):
        return jnp.concatenate(
            [
                speed[:, at : at + HALO],
                thick[None, at : at + HALO],
                bed[None, at : at + HALO],
                fric[None, at : at + HALO],
                mask[None, at : at + HALO].astype(F32),
            ],
            0,
        )

    low, high = edge(0), edge(own_rows - HALO)
    if count == 2:
        sent = jnp.where(lax.axis_index("lat") == 0, high, low)
        halos = [lax.ppermute(sent, "lat", [(0, 1), (1, 0)])]
        window = own_rows + HALO
    else:
        halos = [
            lax.ppermute(high, "lat", [(i, i + 1) for i in range(count - 1)]),
            lax.ppermute(low, "lat", [(i + 1, i) for i in range(count - 1)]),
        ]
        window = own_rows + 2 * HALO
    return pl.pallas_call(
        functools.partial(ice_kernel, masked=count != 2),
        out_shape=jax.ShapeDtypeStruct((own_rows, cols), BF16),
        in_specs=[vmem()] * (5 + len(halos)),
        out_specs=vmem(),
        scratch_shapes=[
            pltpu.VMEM((levels, window + 2 * HALO, cols), F32),
            pltpu.VMEM((5, window + 2 * HALO, cols), F32),
            pltpu.VMEM((levels, window, cols), F32),
            pltpu.VMEM((levels, window, cols), F32),
        ],
        name="ice",
    )(speed, thick, bed, fric, mask, *halos)


def stencil_tables():
    pick_row = np.zeros((32 * COMPS, 24), np.float32)
    pick_col = np.zeros((4, 24, 3 * VEC), np.float32)
    keep = np.zeros((4, 32 * COMPS, 3 * VEC), np.float32)
    for c in range(COMPS):
        for p in range(2):
            for s in range(2):
                for q in range(2):
                    for layer in range(LAYERS):
                        m = ((c * 2 + p) * 2 + s) * PAIR + q * LAYERS + layer
                        pick_row[m, 3 * (4 * p + 2 * q + s) + c] = 1.0
                        for dj in range(3):
                            for c2 in range(COMPS):
                                for q2 in range(2):
                                    for l2 in range(LAYERS):
                                        n = dj * VEC + c2 * PAIR + q2 * LAYERS + l2
                                        p2 = l2 - layer + p
                                        s2 = dj - 1 + s
                                        if p2 in (0, 1) and s2 in (0, 1):
                                            keep[2 * p2 + s2, m, n] = 1.0
    for p2 in range(2):
        for s2 in range(2):
            for dj in range(3):
                for c2 in range(COMPS):
                    for q2 in range(2):
                        for l2 in range(LAYERS):
                            n = dj * VEC + c2 * PAIR + q2 * LAYERS + l2
                            pick_col[2 * p2 + s2, 3 * (4 * p2 + 2 * q2 + s2) + c2, n] = 1.0
    return pick_row, pick_col, keep


def stencil_kernel(matrix, pick_row, pick_col, keep, out, theta):
    exact = functools.partial(
        jnp.dot, precision=lax.Precision.HIGHEST, preferred_element_type=F32
    )
    entries = matrix[...]
    rows = exact(pick_row[...], entries)
    full = jnp.zeros((rows.shape[0], 3 * VEC), F32)
    for n in range(4):
        full = full + keep[n] * exact(rows, pick_col[n])
    high = full.astype(BF16).astype(F32)
    low = full - high
    blank = jnp.zeros((rows.shape[0], PAIR), F32)
    parts = []
    for dj in range(3):
        cut = slice(dj * VEC, (dj + 1) * VEC)
        parts += [high[:, cut], high[:, cut], low[:, cut], blank]
    out[...] = jnp.concatenate(parts, 1).astype(BF16)
    square = iota(entries.shape, 0) == iota(entries.shape, 1)
    trace = jnp.sum(jnp.where(square, entries, 0.0), keepdims=True)
    theta[...] = jnp.broadcast_to(trace * (8.0 * TYPICAL_MODULUS / 24.0), (8, 128))


def stencil_of(matrix):
    tables = [jnp.asarray(t) for t in stencil_tables()]
    return pl.pallas_call(
        stencil_kernel,
        out_shape=(
            jax.ShapeDtypeStruct((32 * COMPS, 3 * (3 * VEC + PAIR)), BF16),
            jax.ShapeDtypeStruct((8, 128), F32),
        ),
        in_specs=[vmem()] * 4,
        out_specs=(vmem(), vmem()),
        name="stencil",
    )(matrix, *tables)


def element_force(vector, stencil, coef):
    parts = []
    for moved in (shift_lanes(vector, -1), vector, shift_lanes(vector, 1)):
        high = moved.astype(BF16).astype(F32)
        low = moved - high
        parts += [high, low, high, low[:PAIR]]
    stacked = jnp.concatenate(parts, 0).astype(BF16)
    force = jnp.dot(stencil, stacked, preferred_element_type=F32)
    sums = []
    for c in range(COMPS):
        total = None
        for n in range(4):
            piece = force[(c * 4 + n) * PAIR : (c * 4 + n + 1) * PAIR] * coef(n)
            total = piece if total is None else total + piece
        sums.append(total)
    return jnp.concatenate(sums, 0)


def swap_rows(x):
    return jnp.concatenate(
        [pltpu.roll(x[c * PAIR : (c + 1) * PAIR], LAYERS, 0) for c in range(COMPS)], 0
    )


def at(base, size, index):
    start = index * size
    if not isinstance(index, int):
        start = pl.multiple_of(start, 8)
    return base.at[pl.ds(start, size)]


def apply_rows(source, coefs, stencil, forces, start, stop, width, store):
    blocks = -(-(stop - start + 2) // width)
    low = min(start - 1, 32 - blocks * width)
    weights = stencil[...]

    def force_block(n, carry):
        base = low + n * width
        for w in range(width):
            pair = base + w
            vector = at(source, VEC, pair)[...]
            coef = at(coefs, 4 * PAIR, pair)
            at(forces, VEC, pair)[...] = element_force(
                vector, weights, lambda n: coef[n * PAIR : (n + 1) * PAIR]
            )
        return carry

    lax.fori_loop(0, blocks, force_block, 0)
    front = iota((VEC, source.shape[1]), 0) % PAIR < LAYERS

    def store_block(n, carry):
        pair = start + n
        before = at(forces, VEC, pair - 1)[...]
        after = at(forces, VEC, pair + 1)[...]
        total = at(forces, VEC, pair)[...] + swap_rows(jnp.where(front, after, before))
        store(pair, total)
        return carry

    lax.fori_loop(0, stop - start, store_block, 0)


def domain_of(pair, cols, group, own_rows, sub):
    row = (pair - 1 - HALO) + group * own_rows + (sub % PAIR) // LAYERS
    shell = (lax.axis_size("group") - 1) * own_rows
    return jnp.where(jnp.logical_and(row >= 0, row < shell), 1.0, 0.0)


def relax_kernel(*refs, pieces):
    E = refs[:pieces]
    stencil, theta = refs[pieces : pieces + 2]
    r_out, c_out, x_out, lw_out, ut_out = refs[pieces + 2 : pieces + 7]
    XP, CR, FO, XS, SH, VI, IW = refs[pieces + 7 :]
    group, lat, rad = (lax.axis_index(n) for n in ("group", "lat", "rad"))
    lat_count = lax.axis_size("lat")
    rows, width = E[0].shape[-2:]
    own_rows = rows - 2 * HALO
    cols = XP.shape[1]
    rad_layers = LAYERS // 2
    planes = COMPS * rad_layers

    def block(lb, rb, plane):
        if pieces == 1:
            return E[0][lb * 2 + rb, plane]
        near, far = [
            jnp.where(rad == rb, E[n][plane], E[n + 1][plane]) for n in (0, 2)
        ]
        return jnp.where(lat == lb, near, far)

    for lb in range(lat_count):
        for rb in range(2):
            for k in range(rad_layers):
                layer = rb * rad_layers + k
                for c in range(COMPS):
                    value = block(lb, rb, c * rad_layers + k)
                    for q in range(2):
                        first = (1 - q) * VEC + c * PAIR + q * LAYERS + layer
                        XS[lb, pl.ds(first, rows, VEC), :] = value
                for ref, plane in ((SH, planes + k), (VI, planes + rad_layers + k)):
                    value = block(lb, rb, plane)
                    for q in range(2):
                        first = (1 - q) * PAIR + q * LAYERS + layer
                        ref[lb, pl.ds(first, rows, PAIR), :] = value
        value = block(lb, 0, planes + 2 * rad_layers)
        for q in range(2):
            for layer in range(LAYERS):
                first = (1 - q) * PAIR + q * LAYERS + layer
                IW[lb, pl.ds(first, rows, PAIR), :] = value

    sub8 = iota((PAIR, cols), 0)
    sub24 = iota((VEC, cols), 0)
    layer8 = sub8 % LAYERS
    shrink = 1.0 / theta[0:1, 0:1]

    def corner_means(nodal):
        both = nodal + pltpu.roll(nodal, LAYERS, 0)
        up = jnp.where(layer8 == LAYERS - 1, 0.0, pltpu.roll(both, PAIR - 1, 0))
        down = jnp.where(layer8 == 0, 0.0, pltpu.roll(both, 1, 0))
        result = []
        for side in (both + up, both + down):
            for step in (1, -1):
                result.append(0.125 * (side + shift_lanes(side, step)))
        return result

    def coef_rows(pair, carry):
        domain = domain_of(pair, cols, group, own_rows, sub8)
        shear, viscosity, vector = [
            jnp.concatenate([at(ref.at[lb], size, pair)[...] for lb in range(lat_count)], 1)
            for ref, size in ((SH, PAIR), (VI, PAIR), (XS, VEC))
        ]
        ratio = shear / viscosity
        damp = 1.0 / (1.0 + ratio)
        modulus = domain * shear * damp
        relaxed = modulus * ratio * damp
        main, relax = corner_means(modulus * shrink), corner_means(relaxed)
        main_ref, relax_ref = at(c_out, 4 * PAIR, pair), at(CR, 4 * PAIR, pair)
        for n in range(4):
            main_ref[n * PAIR : (n + 1) * PAIR] = main[n]
            relax_ref[n * PAIR : (n + 1) * PAIR] = relax[n]
        at(XP, VEC, pair)[...] = vector * domain_of(pair, cols, group, own_rows, sub24)
        return carry

    lax.fori_loop(1, 32, coef_rows, 0)

    def store(pair, total):
        at(r_out, VEC, pair)[...] = -domain_of(pair, cols, group, own_rows, sub24) * total

    apply_rows(XP, CR, stencil, FO, 5, 28, 5, store)
    for t in range(own_rows // 2):
        x_out[t * VEC : (t + 1) * VEC] = XP[(HALO + 1 + 2 * t) * VEC : (HALO + 2 + 2 * t) * VEC]

    blocks = lw_out.shape[2] // 3
    map_rows = blocks // 2
    tile_rows = ut_out.shape[1] // 2
    pair_rows = 32 * PAIR
    row = iota((pair_rows, 1), 0)
    is_top = jnp.where(row % LAYERS == 0, -LOAD_SCALE, 0.0)
    top_scale = is_top * domain_of(row // PAIR, 1, group, own_rows, row)
    for lb in range(lat_count):
        table = IW[lb, 0:pair_rows]
        spots = iota((pair_rows, blocks), 1)
        spread = jnp.zeros((pair_rows, blocks), F32)
        for k in range(4):
            index = table[:, k : k + 1].astype(jnp.int32)
            spot = (index % 2) * map_rows + index // 2
            spread = spread + jnp.where(spots == spot, table[:, 4 + k : 5 + k], 0.0)
        loads = spread * top_scale
        high = loads.astype(BF16).astype(F32)
        middle = (loads - high).astype(BF16).astype(F32)
        low = loads - high - middle
        lw_out[lb] = jnp.concatenate([high, middle, low], 1).astype(BF16)
        own = []
        for t in range(own_rows // 2):
            first = (HALO + 1 + 2 * t) * PAIR
            own.append(table[first : first + PAIR])
        own = jnp.concatenate(own, 0)
        spots = iota((own.shape[0], 2 * tile_rows), 1)
        spread = jnp.zeros((own.shape[0], 2 * tile_rows), F32)
        for k in range(4):
            index = own[:, k : k + 1].astype(jnp.int32)
            near = index // 2 - lat * tile_rows
            spot = (index % 2) * tile_rows + near
            spot = jnp.where(jnp.logical_and(near >= 0, near < tile_rows), spot, -1)
            spread = spread + jnp.where(spots == spot, own[:, 4 + k : 5 + k], 0.0)
        ut_out[lb * own.shape[0] : (lb + 1) * own.shape[0]] = spread * (1.0 / LAYERS)


def krylov_kernel(*refs, loads):
    load_refs = refs[:loads]
    stencil, r_in, coefs, x_own, lw, ut = refs[loads : loads + 6]
    payload, v_out = refs[loads + 6 : loads + 8]
    V, FO = refs[loads + 8 :]
    group, lat = lax.axis_index("group"), lax.axis_index("lat")
    lat_count = lax.axis_size("lat")
    cols = r_in.shape[1]
    width = cols // lat_count
    pairs = x_own.shape[0] // VEC
    own_rows = 2 * pairs
    sub24 = iota((VEC, cols), 0)
    if loads == 2:
        own, other = load_refs[0][...], load_refs[1][...]
        own, other = own.astype(F32), other.astype(F32)
        tiles = [jnp.where(lat == 0, own, other), jnp.where(lat == 0, other, own)]
        field = jnp.concatenate(tiles, 0)
    else:
        field = load_refs[0][...].astype(F32)
    half = field.shape[1] // 2
    blocks = jnp.concatenate([field[:, :half], field[:, half:]], 0)
    blocks = jnp.concatenate([blocks] * 3, 0).astype(BF16)
    count = 32 * PAIR
    for lb in range(lat_count):
        top = jnp.dot(lw[lb], blocks, preferred_element_type=F32)
        FO[0:count, lb * width : (lb + 1) * width] = top

    def start(pair, carry):
        vector = at(r_in, VEC, pair)[...]
        top = at(FO, PAIR, pair)[...]
        vector = jnp.concatenate([vector[: 2 * PAIR], vector[2 * PAIR :] + top], 0)
        at(V.at[0], VEC, pair)[...] = vector
        return carry

    lax.fori_loop(5, 28, start, 0)
    for ref in (V.at[0],):
        ref[0 : 5 * VEC] = jnp.zeros((5 * VEC, cols), F32)
        ref[28 * VEC :] = jnp.zeros((5 * VEC, cols), F32)
    for n in range(ITERS):
        low, high = 6 + n, 27 - n
        if n < ITERS - 1:
            for ref in (V.at[n + 1],):
                ref[(low - 2) * VEC : low * VEC] = jnp.zeros((2 * VEC, cols), F32)
                ref[high * VEC : (high + 2) * VEC] = jnp.zeros((2 * VEC, cols), F32)

        def store(pair, total, n=n):
            domain = domain_of(pair, cols, group, own_rows, sub24)
            fresh = domain * total - at(V.at[n], VEC, pair)[...]
            at(V.at[n + 1], VEC, pair)[...] = fresh

        apply_rows(V.at[n], coefs, stencil, FO, low, high, 5 - n % 2, store)

    def fold(x):
        total = None
        for r in range(x.shape[0] // 8):
            for c in range(x.shape[1] // 128):
                piece = x[8 * r : 8 * r + 8, 128 * c : 128 * c + 128]
                total = piece if total is None else total + piece
        return total

    def products(t, sums):
        pair = HALO + 1 + 2 * t
        values = [at(V.at[n], VEC, pair)[...] for n in range(ITERS + 1)]
        return tuple(
            total + fold(values[k // 2] * values[(k + 1) // 2]) for k, total in enumerate(sums)
        )

    sums = lax.fori_loop(
        0, pairs, products, tuple(jnp.zeros((8, 128), F32) for _ in range(2 * ITERS))
    )
    for k in range(2 * ITERS):
        payload[k : k + 1] = jnp.sum(sums[k], 0, keepdims=True)
    fields = []
    for lb in range(lat_count):
        lanes = slice(lb * width, (lb + 1) * width)
        row = [
            jnp.concatenate(
                [x_own[t * VEC + 2 * PAIR : (t + 1) * VEC, lanes] for t in range(pairs)], 0
            )
        ]
        for n in range(ITERS):
            row.append(
                jnp.concatenate(
                    [
                        V[n, (HALO + 1 + 2 * t) * VEC + 2 * PAIR : (HALO + 2 + 2 * t) * VEC, lanes]
                        for t in range(pairs)
                    ],
                    0,
                )
            )
        fields.append(jnp.concatenate(row, 1))
    fields = jnp.concatenate(fields, 0)
    lift = lax.dot_general(
        ut[...],
        fields,
        (((0,), (0,)), ((), ())),
        precision=lax.Precision.HIGHEST,
        preferred_element_type=F32,
    )
    spots = ut.shape[1]
    for n in range(ITERS + 1):
        payload[2 * ITERS + n * spots : 2 * ITERS + (n + 1) * spots] = lift[
            :, n * width : (n + 1) * width
        ]
    own = pl.ds(pl.multiple_of(lat * width, 128), width)
    for n in range(ITERS):
        for t in range(pairs):
            pair = HALO + 1 + 2 * t
            v_out[n, t * VEC : (t + 1) * VEC] = V[n, pair * VEC : (pair + 1) * VEC, own]
    v_out[ITERS] = x_own[:, own]


def finish_kernel(payload, theta, v, bed, disp_out, bed_out, X):
    rad = lax.axis_index("rad")
    moment = [
        jnp.broadcast_to(jnp.sum(payload[k : k + 1], 1, keepdims=True), (8, 128))
        for k in range(2 * ITERS)
    ]

    def product(left, right, size=False):
        by_degree = {}
        for i, a in enumerate(left):
            for j, b in enumerate(right):
                term = a * b
                if size:
                    term = jnp.abs(term)
                by_degree[i + j] = by_degree[i + j] + term if i + j in by_degree else term
        total = None
        for k, weight in by_degree.items():
            term = weight * (jnp.abs(moment[k]) if size else moment[k])
            total = term if total is None else total + term
        return total

    def shifted(poly):
        result = list(poly) + [jnp.zeros((8, 128), F32)]
        for i, a in enumerate(poly):
            result[i + 1] = result[i + 1] + a
        return result

    one, zero = jnp.ones((8, 128), F32), jnp.zeros((8, 128), F32)
    residual, direction, answer = [one], [one], [zero] * ITERS
    norm = moment[0]
    live = None
    for n in range(ITERS):
        image = shifted(direction)
        step = norm / product(direction, image)
        if live is not None:
            step = jnp.where(live, step, 0.0)
        for i, a in enumerate(direction):
            answer[i] = answer[i] + step * a
        if n == ITERS - 1:
            break
        residual = [
            (residual[i] if i < len(residual) else zero) - step * a for i, a in enumerate(image)
        ]
        fresh = product(residual, residual)
        above = fresh > 1e-7 * product(residual, residual, True)
        live = above if live is None else jnp.logical_and(live, above)
        ratio = jnp.where(live, fresh / norm, 0.0)
        direction = [
            a + (ratio * direction[i] if i < len(direction) else zero)
            for i, a in enumerate(residual)
        ]
        norm = jnp.where(live, fresh, 1.0)
    raw = [a[0:1] for a in answer]
    answer = [a / theta[0:1] for a in raw]
    total = v[ITERS]
    for n in range(ITERS):
        total = total + answer[n] * v[n]
    X[...] = total
    layers = disp_out.shape[1]
    pairs = disp_out.shape[2] // 2
    for c in range(COMPS):
        for k in range(layers):
            for q in range(2):
                lower = X[pl.ds(c * PAIR + q * LAYERS + k, pairs, VEC), :]
                upper = X[pl.ds(c * PAIR + q * LAYERS + layers + k, pairs, VEC), :]
                disp_out[c, k, pl.ds(q, pairs, 2), :] = jnp.where(rad == 0, lower, upper)
    rows, cols = bed.shape
    spots = 2 * rows
    base = 2 * ITERS
    lift = payload[base : base + spots]
    for n in range(ITERS):
        lift = lift + answer[n] * payload[base + (n + 1) * spots : base + (n + 2) * spots]
    for h in range(2):
        lanes = slice(h * cols // 2, (h + 1) * cols // 2)
        bed_out[:, lanes] = bed[:, lanes] + UPLIFT_SCALE * lift[h * rows : (h + 1) * rows]


def per_device(
    displacement_prev,
    shear_modulus,
    viscosity,
    element_matrix,
    regrid_index,
    regrid_weight,
    ice_thickness,
    bed_elevation,
    basal_friction,
    ice_mask,
    speed_guess,
):
    groups, lats = lax.axis_size("group"), lax.axis_size("lat")
    rad_layers, own_rows, width = shear_modulus.shape
    tile_rows, map_cols = ice_thickness.shape
    cols = lats * width
    blocks = 2 * tile_rows * lats
    table = jnp.concatenate(
        [
            regrid_index[:, 0].astype(F32),
            regrid_weight[:, 0],
            jnp.zeros((own_rows, width - 8), F32),
        ],
        1,
    )
    packed = jnp.concatenate(
        [
            displacement_prev.reshape(COMPS * rad_layers, own_rows, width),
            shear_modulus,
            viscosity,
            table[None],
        ],
        0,
    )
    ring = [(i, (i + 1) % groups) for i in range(groups)]
    back = [(i, (i - 1) % groups) for i in range(groups)]
    north = lax.ppermute(packed[:, own_rows - HALO :], "group", ring)
    south = lax.ppermute(packed[:, :HALO], "group", back)
    stencil, theta = stencil_of(element_matrix)
    region = jnp.concatenate([north, packed, south], 1)
    if lats == 2:
        pieces = [
            region,
            lax.ppermute(region, "rad", [(0, 1), (1, 0)]),
            lax.ppermute(region, "lat", [(0, 1), (1, 0)]),
            lax.ppermute(region, ("lat", "rad"), [(i, i ^ 3) for i in range(4)]),
        ]
    else:
        pieces = [lax.all_gather(region, ("lat", "rad"))]
    ice_load = ice_load_of(
        speed_guess, ice_thickness, bed_elevation, basal_friction, ice_mask
    )
    if lats == 2:
        loads = [ice_load, lax.ppermute(ice_load, "lat", [(0, 1), (1, 0)])]
    else:
        loads = [lax.all_gather(ice_load, "lat", axis=0, tiled=True)]
    pairs = own_rows // 2
    r_start, coefs, x_own, lw, ut = pl.pallas_call(
        functools.partial(relax_kernel, pieces=len(pieces)),
        out_shape=(
            jax.ShapeDtypeStruct((33 * VEC, cols), F32),
            jax.ShapeDtypeStruct((33 * 4 * PAIR, cols), F32),
            jax.ShapeDtypeStruct((pairs * VEC, cols), F32),
            jax.ShapeDtypeStruct((lats, 32 * PAIR, 3 * blocks), BF16),
            jax.ShapeDtypeStruct((lats * pairs * PAIR, 2 * tile_rows), F32),
        ),
        in_specs=[vmem()] * (len(pieces) + 2),
        out_specs=(vmem(),) * 5,
        scratch_shapes=[
            pltpu.VMEM((33 * VEC, cols), F32),
            pltpu.VMEM((33 * 4 * PAIR, cols), F32),
            pltpu.VMEM((33 * VEC, cols), F32),
            pltpu.VMEM((lats, 33 * VEC, width), F32),
            pltpu.VMEM((lats, 33 * PAIR, width), F32),
            pltpu.VMEM((lats, 33 * PAIR, width), F32),
            pltpu.VMEM((lats, 33 * PAIR, width), F32),
        ],
        name="relax",
    )(*pieces, stencil, theta)
    spots = 2 * tile_rows
    payload, vectors = pl.pallas_call(
        functools.partial(krylov_kernel, loads=len(loads)),
        out_shape=(
            jax.ShapeDtypeStruct((2 * ITERS + (ITERS + 1) * spots, width), F32),
            jax.ShapeDtypeStruct((ITERS + 1, pairs * VEC, width), F32),
        ),
        in_specs=[vmem()] * (len(loads) + 6),
        out_specs=(vmem(), vmem()),
        scratch_shapes=[
            pltpu.VMEM((ITERS + 1, 33 * VEC, cols), F32),
            pltpu.VMEM((33 * VEC, cols), F32),
        ],
        name="krylov",
    )(*loads, stencil, r_start, coefs, x_own, lw, ut)
    step = 1
    while step < groups:
        payload = payload + lax.ppermute(
            payload, "group", [(i, i ^ step) for i in range(groups)]
        )
        step *= 2
    displacement, bed_new = pl.pallas_call(
        finish_kernel,
        out_shape=(
            jax.ShapeDtypeStruct((COMPS, rad_layers, own_rows, width), F32),
            jax.ShapeDtypeStruct((tile_rows, map_cols), F32),
        ),
        in_specs=[vmem()] * 4,
        out_specs=(vmem(), vmem()),
        scratch_shapes=[pltpu.VMEM((pairs * VEC, width), F32)],
        name="finish",
    )(payload, theta, vectors, bed_elevation)
    return displacement, bed_new


def solution(mesh):
    in_specs = (
        P(None, "rad", "group", "lat"),
        P("rad", "group", "lat"),
        P("rad", "group", "lat"),
        P(),
        P("group", "lat", None),
        P("group", "lat", None),
        P("lat", None),
        P("lat", None),
        P("lat", None),
        P("lat", None),
        P(None, "lat", None),
    )
    out_specs = (P(None, "rad", "group", "lat"), P("lat", None))
    return jax.shard_map(
        per_device, mesh=mesh, in_specs=in_specs, out_specs=out_specs, check_vma=False
    )
```

time: 655 us -> 78.7 us (0.12)
  blocking collectives: 425 us -> 0 us
  starting transfers between devices: 127 us -> 11.2 us
  local copies, waits for them, and re-layouts: 39.4 us -> 6.14 us
  Pallas kernels: 0 us -> 30.8 us
  other arithmetic: 22.9 us -> 3.93 us
  between operations: 11.2 us -> 0.78 us
    psum x9 -> x0, blocking collectives: 421 us -> none  [the longest x4 163 us: global_norm(): return lax.psum(jnp.sum(values * values), ('group', 'lat', 'rad'))]
    ppermute x46 -> x10, starting transfers between devices: 127 us -> 11.2 us  [the longest x1 3.1 us: per_device(): south = lax.ppermute(packed[:, :HALO], 'group', back)]
    pallas_call x0 -> x5, Pallas kernels: none -> 30.8 us  [the longest x1 10.4 us: per_device(): pl.pallas_call(functools.partial(krylov_kernel, loads=len(loads)), out_sh...]
    concatenate x5 -> x1, local copies, waits for them, and re-layouts: 21.6 us -> 0.08 us  [per_device(): jnp.concatenate([regrid_index[:, 0].astype(F32), regrid_weight[:, 0], jnp...]
    slice x32 -> x1, local copies, waits for them, and re-layouts: 10.7 us -> 0.01 us  [per_device(): north = lax.ppermute(packed[:, own_rows - HALO:], 'group', ring)]
    concatenate x21 -> x3, other arithmetic: 8.72 us -> 1.57 us  [the longest x1 0.84 us: per_device(): jnp.concatenate([displacement_prev.reshape(COMPS * rad_layers, own_rows,...]
    reduce_sum x10 -> x0, other arithmetic: 7 us -> none  [the longest x4 3.26 us: per_device(): jnp.sum(direction * mapped)]
    ppermute x46 -> x10, waiting for transfers between devices: 18.6 us -> 25.1 us  [the longest x3 14.4 us: per_device(): lax.ppermute(payload, 'group', [(i, i ^ step) for i in range(groups)])]
  transfers between devices with their start and end apart: 46 -> 10, of which waited for: 19 -> 4; matrix products, arithmetic and copies ran while one was open for 4% -> 5% of each run, Pallas kernels for 0% -> 24%
where the time goes in v1:
time: 78.7 us; the launch traced here: 77.9 us
  Pallas kernels  30.8 us (39%)
  waiting for transfers between devices  25.1 us (32%)
  starting transfers between devices  11.2 us (14%)
  local copies, waits for them, and re-layouts  6.14 us (8%)
  other arithmetic  3.93 us (5%)
    ppermute x3, waiting for transfers between devices, per_device(): lax.ppermute(payload, 'group', [(i, i ^ step) for i in range(groups)])  14.4 us
    ppermute x1, waiting for transfers between devices, ice_load_of(): halos = [lax.ppermute(sent, 'lat', [(0, 1), (1, 0)])]  10.7 us
    pallas_call x1, Pallas kernels, per_device(): pl.pallas_call(functools.partial(krylov_kernel, loads=len(loads)), out_sh...  10.4 us
    pallas_call x1, Pallas kernels, per_device(): pl.pallas_call(functools.partial(relax_kernel, pieces=len(pieces)), out_s...  8.89 us
    pallas_call x1, Pallas kernels, ice_load_of(): pl.pallas_call(functools.partial(ice_kernel, masked=count != 2), out_shap...  7.25 us
    unnamed x22, local copies, waits for them, and re-layouts  5.21 us
    ppermute x1, starting transfers between devices, per_device(): south = lax.ppermute(packed[:, :HALO], 'group', back)  3.1 us
    ppermute x1, starting transfers between devices, per_device(): north = lax.ppermute(packed[:, own_rows - HALO:], 'group', ring)  3.05 us
  transfers between devices with their start and end apart: 10, of which 4 were waited for; matrix products, arithmetic and copies ran while one was open for 5% of the time, Pallas kernels for 24%

profile of v1, /device:TPU:0, one launch (start us, length us, event | category | flops | bytes accessed | tf_op | source)
XLA Modules:
  0.0 77.9 jit_solution(8811485656547740100)
XLA Ops:
  0.6 0.0 copy-start.6
  0.6 0.0 copy-start.7
  0.7 0.0 copy-start.1
  0.7 0.7 convert_bitcast_fusion
  1.4 0.1 copy.16
  1.5 0.8 copy.17
  2.2 0.1 pad.12.clone
  2.3 0.1 maximum_bitcast_fusion
  2.4 0.8 %pad_maximum_fusion.1 = f32[11,16,128]{2,1,0:T(8,128)S(1)} fusion(f32[1,16,128]{2,1,0:T(8,128)S(1)} %maximum_bitcast_fusion, f32[2,16,128]{2,1,0:T(8,128)} %param.16, f32[2,16,128]{2,1,0:T(8,128)} %param.15, f32[6,16,128]{2,1,0:T(8,128)} %bitcast.22), kind=kLoop, calls=%fused_computation.3 | loop fusion | flops 67584 | bytes 180224 | tf_op jit(solution)/shard_map/concatenate | solution.py:688
  3.2 3.0 %collective-permute-start.2 = (f32[11,8,128]{2,1,0:T(8,128)S(1)}, f32[11,8,128]{2,1,0:T(8,128)S(1)}, u32[]{:S(2)}, u32[]{:S(2)}) collective-permute-start(f32[11,8,128]{2,1,0:T(8,128)S(1)} %get-tuple-element.22), channel_id=1, source_target_pairs={{0,4},{4,8},{8,12},{12,16},{16,20},{20,24},{24,28},{28,0},{1,5},{5... | collective-permute-start | bytes 135176 | tf_op jit(solution)/shard_map/ppermute | solution.py:699
  6.3 3.1 %collective-permute-start.3 = (f32[11,8,128]{2,1,0:T(8,128)S(1)}, f32[11,8,128]{2,1,0:T(8,128)S(1)}, u32[]{:S(2)}, u32[]{:S(2)}) collective-permute-start(f32[11,8,128]{2,1,0:T(8,128)S(1)} %get-tuple-element.23), channel_id=1, source_target_pairs={{0,28},{4,0},{8,4},{12,8},{16,12},{20,16},{24,20},{28,24},{1,29},{... | collective-permute-start | bytes 135176 | tf_op jit(solution)/shard_map/ppermute | solution.py:700
  9.4 1.0 %slice_dynamic-update-slice_fusion = (f32[20,8,256]{2,1,0:T(8,128)S(1)}, f32[20,8,256]{2,1,0:T(8,128)S(1)}) fusion(f32[16,16,256]{2,1,0:T(8,128)} %refs_0_.1), kind=kLoop, calls=%fused_computation.1 | loop fusion | bytes 524288
  10.4 0.7 constant_dynamic-update-slice_fusion.7
  11.1 0.7 constant_dynamic-update-slice_fusion.6
  11.8 0.7 constant_dynamic-update-slice_fusion.5
  12.5 0.7 constant_dynamic-update-slice_fusion.4
  13.2 0.0 collective-permute-done.2
  13.2 0.0 collective-permute-done.3
  13.2 0.0 copy-done.6
  13.3 0.0 copy-done.7
  13.3 0.7 collective-permute-start.6
  14.0 1.0 %collective-permute-start.5 = (f32[11,32,128]{2,1,0:T(8,128)S(1)}, f32[11,32,128]{2,1,0:T(8,128)S(1)}, u32[]{:S(2)}, u32[]{:S(2)}) collective-permute-start(f32[11,32,128]{2,1,0:T(8,128)S(1)} %pad_maximum_fusion.refs_0_), channel_id=1, source_target_pairs={{0,2},{2,0},{1,3},{3,1},{4,6},{6,4},{5,7},{7,5},{8,10},{10,8},{9,1... | collective-permute-start | bytes 540680 | tf_op jit(solution)/shard_map/ppermute | solution.py:707
  15.0 0.2 collective-permute-start.4
  15.3 1.7 %collective-permute-start = (f32[20,8,256]{2,1,0:T(8,128)S(1)}, f32[20,8,256]{2,1,0:T(8,128)S(1)}, u32[]{:S(2)}, u32[]{:S(2)}) collective-permute-start(f32[20,8,256]{2,1,0:T(8,128)S(1)} %broadcast_select_fusion), channel_id=1, source_target_pairs={{0,2},{2,0},{1,3},{3,1},{4,6},{6,4},{5,7},{7,5},{8,10},{10,8},{9,1... | collective-permute-start | bytes 491528 | tf_op jit(solution)/shard_map/ppermute | solution.py:197
  16.9 10.7 %collective-permute-done.refs_5_ = f32[20,8,256]{2,1,0:T(8,128)S(1)} collective-permute-done((f32[20,8,256]{2,1,0:T(8,128)S(1)}, f32[20,8,256]{2,1,0:T(8,128)S(1)}, u32[]{:S(2)}, u32[]{:S(2)}) %collective-permute-start) | collective-permute-done | bytes 163872 | tf_op jit(solution)/shard_map/ppermute | solution.py:197
  27.6 0.7 copy-done.5
  28.3 7.3 %ice.1.refs_0_ = bf16[16,256]{1,0:T(8,128)(2,1)} custom-call(f32[16,16,256]{2,1,0:T(8,128)} %refs_0_.1, f32[16,256]{1,0:T(8,128)} %refs_1_.1, f32[16,256]{1,0:T(8,128)} %bed.1, f32[16,256]{1,0:T(8,128)} %refs_3_.1, s32[16,256]{1,0:T(8,128)} %refs_4_.1, f32[20,8,256]{2,1,0:T(8,128)} %copy-done.5), custom_call_target="tpu_custom_call" | custom-call | tf_op jit(solution)/shard_map/ice/pallas_call | solution.py:205
  35.5 0.9 %collective-permute-start.1 = (bf16[16,256]{1,0:T(8,128)(2,1)}, bf16[16,256]{1,0:T(8,128)(2,1)S(1)}, u32[]{:S(2)}, u32[]{:S(2)}) collective-permute-start(bf16[16,256]{1,0:T(8,128)(2,1)} %ice.1.refs_0_), channel_id=1, source_target_pairs={{0,2},{2,0},{1,3},{3,1},{4,6},{6,4},{5,7},{7,5},{8,10},{10,8},{9,1... | collective-permute-start | bytes 24584 | tf_op jit(solution)/shard_map/ppermute | solution.py:716
  36.4 2.2 %stencil.1 = (bf16[96,240]{1,0:T(8,128)(2,1)}, f32[8,128]{1,0:T(8,128)}) custom-call(f32[24,24]{1,0:T(8,128)} %matrix.1, f32[96,24]{1,0:T(8,128)} %constant.14.clone.pick_row, f32[4,24,72]{2,1,0:T(8,128)} %constant.15.clone.pick_col, f32[4,96,72]{2,1,0:T(8,128)} %constant.16.clone.keep), custom_call_target="tpu_custom_call" | custom-call | tf_op jit(solution)/shard_map/stencil/pallas_call | solution.py:275
  38.6 0.0 collective-permute-done.6.refs_3_
  38.6 0.0 collective-permute-done.5.refs_2_
  38.6 0.0 collective-permute-done.4.refs_1_
  38.7 0.6 copy-done.2
  39.3 0.1 copy-done.3
  39.4 0.1 copy-done.4
  39.4 8.9 %relax.1 = (f32[792,256]{1,0:T(8,128)}, f32[1056,256]{1,0:T(8,128)}, f32[192,256]{1,0:T(8,128)}, bf16[2,256,192]{2,1,0:T(8,128)(2,1)}, f32[128,32]{1,0:T(8,128)}) custom-call(f32[11,32,128]{2,1,0:T(8,128)} %copy-done, f32[11,32,128]{2,1,0:T(8,128)} %copy-done.4, f32[11,32,128]{2,1,0:T(8,128)} %copy-done.3, f32[11,32,128]{2,1,0:T(8,128)} %copy-done.2, ...), custom_call_target="tpu_custom_call" | custom-call | tf_op jit(solution)/shard_map/relax/pallas_call | solution.py:720
  48.3 0.0 collective-permute-done.1.refs_1_
  48.3 0.6 copy-done.8
  48.9 10.4 %krylov.1 = (f32[168,128]{1,0:T(8,128)}, f32[5,192,128]{2,1,0:T(8,128)}) custom-call(bf16[16,256]{1,0:T(8,128)(2,1)} %ice.1.refs_0_, bf16[16,256]{1,0:T(8,128)(2,1)} %copy-done.8, bf16[96,240]{1,0:T(8,128)(2,1)} %get-tuple-element.11.refs_4_.refs_2_, f32[792,256]{1,0:T(8,128)} %get-tuple-element.13.refs_3_, f32[1056,256]{1,0:T(8,128)} %get-tuple-element.14.refs_4_, ...), custom_call_target="tpu_custom_call" | custom-call | tf_op jit(solution)/shard_map/krylov/pallas_call | solution.py:743
  59.4 0.0 collective-permute-start.7
  59.4 4.7 %collective-permute-done.7 = f32[168,128]{1,0:T(8,128)S(1)} collective-permute-done((f32[168,128]{1,0:T(8,128)}, f32[168,128]{1,0:T(8,128)S(1)}, u32[]{:S(2)}, u32[]{:S(2)}) %collective-permute-start.7) | collective-permute-done | bytes 86048 | tf_op jit(solution)/shard_map/ppermute | solution.py:759
  64.1 0.9 %add.9 = f32[168,128]{1,0:T(8,128)S(1)} add(f32[168,128]{1,0:T(8,128)} %get-tuple-element.18, f32[168,128]{1,0:T(8,128)S(1)} %collective-permute-done.7) | non-fusion elementwise | flops 21504 | bytes 258048 | tf_op jit(solution)/shard_map/add | solution.py:759
  65.0 0.1 collective-permute-start.8
  65.1 4.5 %collective-permute-done.8 = f32[168,128]{1,0:T(8,128)S(1)} collective-permute-done((f32[168,128]{1,0:T(8,128)S(1)}, f32[168,128]{1,0:T(8,128)S(1)}, u32[]{:S(2)}, u32[]{:S(2)}) %collective-permute-start.8) | collective-permute-done | bytes 86048 | tf_op jit(solution)/shard_map/ppermute | solution.py:759
  69.5 0.5 collective-permute-start.9
  70.1 5.3 %collective-permute-done.9 = f32[168,128]{1,0:T(8,128)S(1)} collective-permute-done((f32[168,128]{1,0:T(8,128)S(1)}, f32[168,128]{1,0:T(8,128)S(1)}, u32[]{:S(2)}, u32[]{:S(2)}) %collective-permute-start.9) | collective-permute-done | bytes 86048 | tf_op jit(solution)/shard_map/ppermute | solution.py:759
  75.4 0.6 add.11.payload
  76.0 1.9 %finish.1 = (f32[3,2,16,128]{3,2,1,0:T(8,128)}, f32[16,256]{1,0:T(8,128)}) custom-call(f32[168,128]{1,0:T(8,128)} %add.11.payload, f32[8,128]{1,0:T(8,128)} %get-tuple-element.12.refs_5_.theta, f32[5,192,128]{2,1,0:T(8,128)} %get-tuple-element.19.v, f32[16,256]{1,0:T(8,128)} %bed.1), custom_call_target="tpu_custom_call" | custom-call | tf_op jit(solution)/shard_map/finish/pallas_call | solution.py:763
  (13 shorter events, 0.1 us)
Async XLA Ops:
  0.6 12.6 %copy-start.6 = (f32[2,16,128]{2,1,0:T(8,128)S(1)}, f32[2,16,128]{2,1,0:T(8,128)}, u32[]{:S(2)}) copy-start(f32[2,16,128]{2,1,0:T(8,128)} %param.16) | copy-start | bytes 49156
  0.6 12.6 %copy-start.7 = (f32[2,16,128]{2,1,0:T(8,128)S(1)}, f32[2,16,128]{2,1,0:T(8,128)}, u32[]{:S(2)}) copy-start(f32[2,16,128]{2,1,0:T(8,128)} %param.15) | copy-start | bytes 49156
  0.7 12.6 %copy-start.1 = (f32[3,2,16,128]{3,2,1,0:T(8,128)S(1)}, f32[3,2,16,128]{3,2,1,0:T(8,128)}, u32[]{:S(2)}) copy-start(f32[3,2,16,128]{3,2,1,0:T(8,128)} %param.14) | copy-start | bytes 147460
  3.2 10.0 %collective-permute-start.2 = (f32[11,8,128]{2,1,0:T(8,128)S(1)}, f32[11,8,128]{2,1,0:T(8,128)S(1)}, u32[]{:S(2)}, u32[]{:S(2)}) collective-permute-start(f32[11,8,128]{2,1,0:T(8,128)S(1)} %get-tuple-element.22), channel_id=1, source_target_pairs={{0,4},{4,8},{8,12},{12,16},{16,20},{20,24},{24,28},{28,0},{1,5},{5... | collective-permute-start | bytes 135176 | tf_op jit(solution)/shard_map/ppermute | solution.py:699
  6.3 7.0 %collective-permute-start.3 = (f32[11,8,128]{2,1,0:T(8,128)S(1)}, f32[11,8,128]{2,1,0:T(8,128)S(1)}, u32[]{:S(2)}, u32[]{:S(2)}) collective-permute-start(f32[11,8,128]{2,1,0:T(8,128)S(1)} %get-tuple-element.23), channel_id=1, source_target_pairs={{0,28},{4,0},{8,4},{12,8},{16,12},{20,16},{24,20},{28,24},{1,29},{... | collective-permute-start | bytes 135176 | tf_op jit(solution)/shard_map/ppermute | solution.py:700
  13.3 25.4 %copy-start = (f32[11,32,128]{2,1,0:T(8,128)}, f32[11,32,128]{2,1,0:T(8,128)S(1)}, u32[]{:S(2)}) copy-start(f32[11,32,128]{2,1,0:T(8,128)S(1)} %pad_maximum_fusion.refs_0_) | copy-start | bytes 540676
  13.3 25.3 %collective-permute-start.6 = (f32[11,32,128]{2,1,0:T(8,128)S(1)}, f32[11,32,128]{2,1,0:T(8,128)S(1)}, u32[]{:S(2)}, u32[]{:S(2)}) collective-permute-start(f32[11,32,128]{2,1,0:T(8,128)S(1)} %pad_maximum_fusion.refs_0_), channel_id=1, source_target_pairs={{0,3},{1,2},{2,1},{3,0},{4,7},{5,6},{6,5},{7,4},{8,11},{9,10},{10,... | collective-permute-start | bytes 540680 | tf_op jit(solution)/shard_map/ppermute | solution.py:708
  14.0 24.6 %collective-permute-start.5 = (f32[11,32,128]{2,1,0:T(8,128)S(1)}, f32[11,32,128]{2,1,0:T(8,128)S(1)}, u32[]{:S(2)}, u32[]{:S(2)}) collective-permute-start(f32[11,32,128]{2,1,0:T(8,128)S(1)} %pad_maximum_fusion.refs_0_), channel_id=1, source_target_pairs={{0,2},{2,0},{1,3},{3,1},{4,6},{6,4},{5,7},{7,5},{8,10},{10,8},{9,1... | collective-permute-start | bytes 540680 | tf_op jit(solution)/shard_map/ppermute | solution.py:707
  15.0 23.6 %collective-permute-start.4 = (f32[11,32,128]{2,1,0:T(8,128)S(1)}, f32[11,32,128]{2,1,0:T(8,128)S(1)}, u32[]{:S(2)}, u32[]{:S(2)}) collective-permute-start(f32[11,32,128]{2,1,0:T(8,128)S(1)} %pad_maximum_fusion.refs_0_), channel_id=1, source_target_pairs={{0,1},{1,0},{2,3},{3,2},{4,5},{5,4},{6,7},{7,6},{8,9},{9,8},{10,11... | collective-permute-start | bytes 540680 | tf_op jit(solution)/shard_map/ppermute | solution.py:706
  15.3 12.3 %collective-permute-start = (f32[20,8,256]{2,1,0:T(8,128)S(1)}, f32[20,8,256]{2,1,0:T(8,128)S(1)}, u32[]{:S(2)}, u32[]{:S(2)}) collective-permute-start(f32[20,8,256]{2,1,0:T(8,128)S(1)} %broadcast_select_fusion), channel_id=1, source_target_pairs={{0,2},{2,0},{1,3},{3,1},{4,6},{6,4},{5,7},{7,5},{8,10},{10,8},{9,1... | collective-permute-start | bytes 491528 | tf_op jit(solution)/shard_map/ppermute | solution.py:197
  27.6 0.7 copy-start.5
  35.5 12.8 %collective-permute-start.1 = (bf16[16,256]{1,0:T(8,128)(2,1)}, bf16[16,256]{1,0:T(8,128)(2,1)S(1)}, u32[]{:S(2)}, u32[]{:S(2)}) collective-permute-start(bf16[16,256]{1,0:T(8,128)(2,1)} %ice.1.refs_0_), channel_id=1, source_target_pairs={{0,2},{2,0},{1,3},{3,1},{4,6},{6,4},{5,7},{7,5},{8,10},{10,8},{9,1... | collective-permute-start | bytes 24584 | tf_op jit(solution)/shard_map/ppermute | solution.py:716
  38.6 0.7 copy-start.2
  38.6 0.7 copy-start.3
  38.6 0.8 %copy-start.4 = (f32[11,32,128]{2,1,0:T(8,128)}, f32[11,32,128]{2,1,0:T(8,128)S(1)}, u32[]{:S(2)}) copy-start(f32[11,32,128]{2,1,0:T(8,128)S(1)} %collective-permute-done.4.refs_1_) | copy-start | bytes 540676
  48.3 0.6 copy-start.8
  59.4 4.7 %collective-permute-start.7 = (f32[168,128]{1,0:T(8,128)}, f32[168,128]{1,0:T(8,128)S(1)}, u32[]{:S(2)}, u32[]{:S(2)}) collective-permute-start(f32[168,128]{1,0:T(8,128)} %get-tuple-element.18), channel_id=1, source_target_pairs={{0,4},{4,0},{8,12},{12,8},{16,20},{20,16},{24,28},{28,24},{1,5},{5... | collective-permute-start | bytes 258056 | tf_op jit(solution)/shard_map/ppermute | solution.py:759
  65.0 4.5 %collective-permute-start.8 = (f32[168,128]{1,0:T(8,128)S(1)}, f32[168,128]{1,0:T(8,128)S(1)}, u32[]{:S(2)}, u32[]{:S(2)}) collective-permute-start(f32[168,128]{1,0:T(8,128)S(1)} %add.9), channel_id=1, source_target_pairs={{0,8},{4,12},{8,0},{12,4},{16,24},{20,28},{24,16},{28,20},{1,9},{5... | collective-permute-start | bytes 258056 | tf_op jit(solution)/shard_map/ppermute | solution.py:759
  69.5 5.8 %collective-permute-start.9 = (f32[168,128]{1,0:T(8,128)S(1)}, f32[168,128]{1,0:T(8,128)S(1)}, u32[]{:S(2)}, u32[]{:S(2)}) collective-permute-start(f32[168,128]{1,0:T(8,128)S(1)} %add.10), channel_id=1, source_target_pairs={{0,16},{4,20},{8,24},{12,28},{16,0},{20,4},{24,8},{28,12},{1,17},{... | collective-permute-start | bytes 258056 | tf_op jit(solution)/shard_map/ppermute | solution.py:759

commit v2 on v1

v2 whole, which is shorter than its diff:
```python
import functools

import jax
import jax.numpy as jnp
import numpy as np
from jax import lax
from jax.experimental import pallas as pl
from jax.experimental.pallas import tpu as pltpu
from jax.sharding import PartitionSpec as P

SWEEPS = 6
ITERS = 4
HALO = 8
COMPS = 3
LAYERS = 4
PAIR = 2 * LAYERS
VEC = COMPS * PAIR
LOAD_SCALE = 20.0
UPLIFT_SCALE = 0.5
ASPECT = 0.01
STRAIN_FLOOR = 0.01
TYPICAL_MODULUS = 2.2

F32 = jnp.float32
BF16 = jnp.bfloat16


def vmem():
    return pl.BlockSpec(memory_space=pltpu.VMEM)


def keep(*arrays):
    return [pltpu.with_memory_space_constraint(a, pltpu.VMEM) for a in arrays]


def call(body, name, out, inputs, scratch=(), specs=None):
    lats = lax.axis_size("lat")
    return pl.pallas_call(
        body,
        out_shape=out,
        in_specs=specs or [vmem()] * len(inputs),
        out_specs=jax.tree.map(lambda _: vmem(), out),
        scratch_shapes=list(scratch),
        compiler_params=pltpu.CompilerParams(vmem_limit_bytes=(8 if lats == 2 else 40) << 20),
        name=name,
    )(*inputs)


def iota(shape, dim):
    return lax.broadcasted_iota(jnp.int32, shape, dim)


def shift_lanes(x, step):
    zero = jnp.zeros((x.shape[0], 1), x.dtype)
    if step == 1:
        return jnp.concatenate([x[:, 1:], zero], 1)
    return jnp.concatenate([zero, x[:, :-1]], 1)


def ice_kernel(*refs, masked):
    if masked:
        speed, thick, bed, fric, mask, before, after, out, S, PL, ST, RH = refs
    else:
        speed, thick, bed, fric, mask, halo, out, S, PL, ST, RH = refs
    levels, own_rows, cols = speed.shape
    lat = lax.axis_index("lat")
    window = ST.shape[1]
    planes = (thick, bed, fric, mask)
    S[:, 0:HALO, :] = jnp.zeros((levels, HALO, cols), F32)
    S[:, HALO + window :, :] = jnp.zeros((levels, HALO, cols), F32)
    PL[:, 0:HALO, :] = jnp.zeros((5, HALO, cols), F32)
    PL[:, HALO + window :, :] = jnp.zeros((5, HALO, cols), F32)

    def place(start, speeds, four):
        rows = pl.ds(pl.multiple_of(HALO + start, 8), speeds.shape[1])
        S[:, rows, :] = speeds
        for n in range(4):
            PL[n, rows, :] = four[n]

    own_four = [thick[...], bed[...], fric[...], mask[...].astype(F32)]
    if masked:
        own_at = HALO
        place(own_at, speed[...], own_four)
        place(0, before[:levels], [before[levels + n] for n in range(4)])
        place(HALO + own_rows, after[:levels], [after[levels + n] for n in range(4)])
    else:
        own_at = lat * HALO
        place(own_at, speed[...], own_four)
        place((1 - lat) * own_rows, halo[:levels], [halo[levels + n] for n in range(4)])
    tiles = range(window // 8)

    def rows_of(t):
        return slice(HALO + 8 * t, HALO + 8 * t + 8)

    sub = iota((8, cols), 0)
    top_row, bottom_row = sub == 0, sub == 7

    def north_of(ref, t, here):
        joined = jnp.where(top_row, ref[rows_of(t + 1)], here)
        return pltpu.roll(joined, 7, 0)

    def south_of(ref, t, here):
        joined = jnp.where(bottom_row, ref[rows_of(t - 1)], here)
        return pltpu.roll(joined, 1, 0)

    factor = 0.5 * 0.25 ** (-1.0 / 3.0)
    PL[4, HALO : HALO + window] = (
        PL[0, HALO : HALO + window] + PL[1, HALO : HALO + window]
    )
    for t in tiles:
        here = PL[4, rows_of(t)]
        PL[1, rows_of(t)] = (
            (-0.5 / factor)
            * PL[3, rows_of(t)]
            * PL[0, rows_of(t)]
            * (north_of(PL.at[4], t, here) - south_of(PL.at[4], t, here))
        )
        PL[2, rows_of(t)] = PL[2, rows_of(t)] * (1.0 / factor)
    if masked:
        count = lax.axis_size("lat")

        def inside(t):
            row = iota((8, cols), 0) + (8 * t - HALO)
            top = jnp.where(lat == 0, 0, -HALO)
            end = jnp.where(lat == count - 1, own_rows, own_rows + HALO)
            return jnp.logical_and(row >= top, row < end)

    def inverse_of(t):
        thickness = PL[0, rows_of(t)]
        if masked:
            thickness = jnp.where(inside(t), thickness, 1.0)
        return (levels - 1) / thickness

    def sweep(_, carry):
        for t in tiles:
            inverse = 0.5 * inverse_of(t)
            driving = PL[1, rows_of(t)]
            for k in range(levels):
                here = S[k, rows_of(t)]
                north, south = north_of(S.at[k], t, here), south_of(S.at[k], t, here)
                east, west = shift_lanes(here, 1), shift_lanes(here, -1)
                above = S[min(k + 1, levels - 1), rows_of(t)]
                below = S[max(k - 1, 0), rows_of(t)]
                by_level = (above - below) * inverse
                if k in (0, levels - 1):
                    by_level = 2.0 * by_level
                by_row = north - south
                by_col = east - west
                strain = (by_row * by_row + 4.0 * STRAIN_FLOOR) + (
                    0.25 * (by_col * by_col) + by_level * by_level
                )
                stiffness = jnp.exp2(jnp.log2(strain) * (-1.0 / 3.0))
                ST[k, 8 * t : 8 * t + 8] = stiffness
                RH[k, 8 * t : 8 * t + 8] = driving + stiffness * (
                    (north + south) + (east + west)
                )
        scale = [(0.5 * ASPECT) * inverse_of(t) * inverse_of(t) for t in tiles]
        upper, value, vertical, stiff, rest = {}, {}, {}, {}, {}
        for k in range(levels):
            for t in tiles:
                rows = slice(8 * t, 8 * t + 8)
                current = ST[0, rows] if k == 0 else stiff[t]
                partial = 4.0 * current
                right = RH[k, rows]
                if k == 0:
                    partial = partial + PL[2, rows_of(t)]
                else:
                    partial = partial + vertical[t] * rest[t]
                    right = right + vertical[t] * value[t]
                diagonal = partial
                if k < levels - 1:
                    stiff[t] = ST[k + 1, rows]
                    vertical[t] = scale[t] * (current + stiff[t])
                    diagonal = partial + vertical[t]
                invert = 1.0 / diagonal
                value[t] = right * invert
                RH[k, rows] = value[t]
                if k < levels - 1:
                    rest[t] = partial * invert
                    ST[k, rows] = vertical[t] * invert
        for k in range(levels - 1, -1, -1):
            for t in tiles:
                rows = slice(8 * t, 8 * t + 8)
                if k < levels - 1:
                    value[t] = RH[k, rows] + ST[k, rows] * value[t]
                fresh = value[t]
                if masked:
                    fresh = jnp.where(inside(t), fresh, 0.0)
                    value[t] = fresh
                S[k, rows_of(t)] = fresh
        return carry

    lax.fori_loop(0, SWEEPS, sweep, 0)
    for t in tiles:
        total = S[0, rows_of(t)]
        for k in range(1, levels):
            total = total + S[k, rows_of(t)]
        PL[4, rows_of(t)] = PL[0, rows_of(t)] * total * (1.0 / levels)
    for t in tiles:
        here = PL[4, rows_of(t)]
        change = north_of(PL.at[4], t, here) - south_of(PL.at[4], t, here)
        fresh = PL[0, rows_of(t)] - 0.25 * change
        PL[1, rows_of(t)] = PL[3, rows_of(t)] * fresh
    out[...] = PL[1, pl.ds(pl.multiple_of(HALO + own_at, 8), own_rows), :].astype(BF16)


def edge_kernel(speed, thick, bed, fric, mask, *rest, masked):
    outs, sems = rest[:-1], rest[-1]
    levels, own_rows, cols = speed.shape
    top = own_rows - HALO
    if masked:
        starts = [0, top]
    else:
        starts = [jnp.where(lax.axis_index("lat") == 0, top, 0)]
    copies = []
    for n, (start, out) in enumerate(zip(starts, outs)):
        rows = pl.ds(start if masked else pl.multiple_of(start, 8), HALO)
        copies.append(
            pltpu.make_async_copy(speed.at[:, rows, :], out.at[0:levels], sems.at[4 * n])
        )
        for m, plane in enumerate((thick, bed, fric)):
            copies.append(
                pltpu.make_async_copy(
                    plane.at[rows, :], out.at[levels + m], sems.at[4 * n + 1 + m]
                )
            )
    for copy in copies:
        copy.start()
    for start, out in zip(starts, outs):
        rows = pl.ds(start if masked else pl.multiple_of(start, 8), HALO)
        out[levels + 3] = mask[rows, :].astype(F32)
    for copy in copies:
        copy.wait()


def ice_edges(speed, thick, bed, fric, mask):
    levels, _, cols = speed.shape
    masked = lax.axis_size("lat") != 2
    count = 2 if masked else 1
    return call(
        functools.partial(edge_kernel, masked=masked),
        "edge",
        (pltpu.VMEM((levels + 4, HALO, cols), F32),) * count,
        (speed, thick, bed, fric, mask),
        [pltpu.SemaphoreType.DMA((4 * count,))],
        [pl.BlockSpec(memory_space=pl.ANY)] * 4 + [vmem()],
    )


def ice_load_of(speed, thick, bed, fric, mask, halos):
    levels, own_rows, cols = speed.shape
    window = own_rows + HALO * (1 if len(halos) == 1 else 2)
    return call(
        functools.partial(ice_kernel, masked=len(halos) != 1),
        "ice",
        pltpu.VMEM((own_rows, cols), BF16),
        (speed, thick, bed, fric, mask, *keep(*halos)),
        [
            pltpu.VMEM((levels, window + 2 * HALO, cols), F32),
            pltpu.VMEM((5, window + 2 * HALO, cols), F32),
            pltpu.VMEM((levels, window, cols), F32),
            pltpu.VMEM((levels, window, cols), F32),
        ],
    )


def stencil_tables():
    pick_row = np.zeros((32 * COMPS, 24), np.float32)
    pick_col = np.zeros((4, 24, 3 * VEC), np.float32)
    keep = np.zeros((4, 32 * COMPS, 3 * VEC), np.float32)
    for c in range(COMPS):
        for p in range(2):
            for s in range(2):
                for q in range(2):
                    for layer in range(LAYERS):
                        m = ((c * 2 + p) * 2 + s) * PAIR + q * LAYERS + layer
                        pick_row[m, 3 * (4 * p + 2 * q + s) + c] = 1.0
                        for dj in range(3):
                            for c2 in range(COMPS):
                                for q2 in range(2):
                                    for l2 in range(LAYERS):
                                        n = dj * VEC + c2 * PAIR + q2 * LAYERS + l2
                                        p2 = l2 - layer + p
                                        s2 = dj - 1 + s
                                        if p2 in (0, 1) and s2 in (0, 1):
                                            keep[2 * p2 + s2, m, n] = 1.0
    for p2 in range(2):
        for s2 in range(2):
            for dj in range(3):
                for c2 in range(COMPS):
                    for q2 in range(2):
                        for l2 in range(LAYERS):
                            n = dj * VEC + c2 * PAIR + q2 * LAYERS + l2
                            pick_col[2 * p2 + s2, 3 * (4 * p2 + 2 * q2 + s2) + c2, n] = 1.0
    return pick_row, pick_col, keep


def stencil_kernel(matrix, pick_row, pick_col, keep, out, theta):
    exact = functools.partial(
        jnp.dot, precision=lax.Precision.HIGHEST, preferred_element_type=F32
    )
    entries = matrix[...]
    rows = exact(pick_row[...], entries)
    full = jnp.zeros((rows.shape[0], 3 * VEC), F32)
    for n in range(4):
        full = full + keep[n] * exact(rows, pick_col[n])
    high = full.astype(BF16).astype(F32)
    low = full - high
    blank = jnp.zeros((rows.shape[0], PAIR), F32)
    parts = []
    for dj in range(3):
        cut = slice(dj * VEC, (dj + 1) * VEC)
        parts += [high[:, cut], high[:, cut], low[:, cut], blank]
    out[...] = jnp.concatenate(parts, 1).astype(BF16)
    square = iota(entries.shape, 0) == iota(entries.shape, 1)
    trace = jnp.sum(jnp.where(square, entries, 0.0), keepdims=True)
    theta[...] = jnp.broadcast_to(trace * (8.0 * TYPICAL_MODULUS / 24.0), (8, 128))


def stencil_of(matrix):
    tables = [jnp.asarray(t) for t in stencil_tables()]
    return call(
        stencil_kernel,
        "stencil",
        (
            pltpu.VMEM((32 * COMPS, 3 * (3 * VEC + PAIR)), BF16),
            pltpu.VMEM((8, 128), F32),
        ),
        (matrix, *tables),
    )


def pack_kernel(disp, shear, visc, index, weight, low, high, TS, *, map_rows):
    layers = shear.shape[0]
    count = COMPS * layers
    spot = index[...]
    TS[0:4, 0 : 2 * HALO] = ((spot % 2) * map_rows + spot // 2).astype(F32)
    TS[4:8, 0 : 2 * HALO] = weight[...]
    table = jnp.transpose(TS[...])
    for n, out in enumerate((low, high)):
        rows = slice(n * HALO, (n + 1) * HALO)
        for c in range(COMPS):
            for k in range(layers):
                out[c * layers + k] = disp[c, k, rows]
        for k in range(layers):
            out[count + k] = shear[k, rows]
            out[count + layers + k] = visc[k, rows]
        out[count + 2 * layers, :, 0:8] = table[rows]


def region_kernel(north, low, high, south, out):
    for n, piece in enumerate((north, low, high, south)):
        out[:, n * HALO : (n + 1) * HALO] = piece[...]


def at(base, size, index):
    return base.at[pl.ds(index * size, size)]


def element_force(vector, stencil, coef):
    high = vector.astype(BF16).astype(F32)
    split = jnp.concatenate([high, vector - high], 0).astype(BF16)
    parts = []
    for moved in (shift_lanes(split, -1), split, shift_lanes(split, 1)):
        parts += [moved, moved[: VEC + PAIR]]
    force = jnp.dot(stencil, jnp.concatenate(parts, 0), preferred_element_type=F32)
    sums = []
    for c in range(COMPS):
        total = None
        for n in range(4):
            first = (c * 4 + n) * PAIR
            piece = force[first : first + PAIR] * coef[n * PAIR : (n + 1) * PAIR]
            total = piece if total is None else total + piece
        sums.append(total)
    return sums


def apply_rows(source, coefs, stencil, start, stop, store):
    weights = stencil[...]
    front = iota((PAIR, source.shape[1]), 0) < LAYERS
    forces = {}
    for pair in range(start - 1, stop + 1):
        forces[pair] = element_force(
            at(source, VEC, pair)[...], weights, at(coefs, 4 * PAIR, pair)[...]
        )
        done = pair - 1
        if done >= start:
            sums = []
            for c in range(COMPS):
                swapped = jnp.where(front, forces[pair][c], forces[done - 1][c])
                sums.append(forces[done][c] + pltpu.roll(swapped, LAYERS, 0))
            store(done, sums)
            del forces[done - 1]


def domain_of(own_rows, cols):
    shell = (lax.axis_size("group") - 1) * own_rows
    base = iota((PAIR, 128), 0) // LAYERS + lax.axis_index("group") * own_rows

    def mask(pair):
        offset = pair - 1 - HALO
        live = jnp.logical_and(base >= -offset, base < shell - offset)
        one = jnp.where(live, 1.0, 0.0)
        return jnp.concatenate([one] * (cols // 128), 1)

    return mask


def relax_kernel(*refs, pieces):
    E = refs[:pieces]
    stencil, theta = refs[pieces : pieces + 2]
    r_out, c_out, x_out, lw_out, ut_out = refs[pieces + 2 : pieces + 7]
    XP, CR, XS, SH, VI = refs[pieces + 7 :]
    group, lat, rad = (lax.axis_index(n) for n in ("group", "lat", "rad"))
    lat_count = lax.axis_size("lat")
    rows, width = E[0].shape[-2:]
    own_rows = rows - 2 * HALO
    cols = XP.shape[1]
    rad_layers = LAYERS // 2
    planes = COMPS * rad_layers

    def block(lb, rb, plane):
        if pieces == 1:
            return E[0][lb * 2 + rb, plane]
        near, far = [
            jnp.where(rad == rb, E[n][plane], E[n + 1][plane]) for n in (0, 2)
        ]
        return jnp.where(lat == lb, near, far)

    for lb in range(lat_count):
        for rb in range(2):
            for k in range(rad_layers):
                layer = rb * rad_layers + k
                for c in range(COMPS):
                    value = block(lb, rb, c * rad_layers + k)
                    for q in range(2):
                        first = (1 - q) * VEC + c * PAIR + q * LAYERS + layer
                        XS[lb, pl.ds(first, rows, VEC), :] = value
                for ref, plane in ((SH, planes + k), (VI, planes + rad_layers + k)):
                    value = block(lb, rb, plane)
                    for q in range(2):
                        first = (1 - q) * PAIR + q * LAYERS + layer
                        ref[lb, pl.ds(first, rows, PAIR), :] = value

    mask = domain_of(own_rows, cols)
    layer8 = iota((PAIR, cols), 0) % LAYERS
    top_layer, last_layer = layer8 == 0, layer8 == LAYERS - 1
    shrink = 1.0 / theta[0:1, 0:1]
    eighth = 0.125 * shrink

    def corner_means(nodal, scale):
        both = nodal + pltpu.roll(nodal, LAYERS, 0)
        up = jnp.where(last_layer, 0.0, pltpu.roll(both, PAIR - 1, 0))
        down = jnp.where(top_layer, 0.0, pltpu.roll(both, 1, 0))
        result = []
        for side in (both + up, both + down):
            side = scale * side
            for step in (1, -1):
                result.append(side + shift_lanes(side, step))
        return jnp.concatenate(result, 0)

    for pair in range(4, 29):
        domain = mask(pair)
        shear, viscosity, vector = [
            jnp.concatenate([at(ref.at[lb], size, pair)[...] for lb in range(lat_count)], 1)
            for ref, size in ((SH, PAIR), (VI, PAIR), (XS, VEC))
        ]
        ratio = shear / viscosity
        damp = 1.0 / (1.0 + ratio)
        modulus = domain * shear * damp
        relaxed = modulus * ratio * damp
        at(c_out, 4 * PAIR, pair)[...] = corner_means(modulus, eighth)
        at(CR, 4 * PAIR, pair)[...] = corner_means(relaxed, 0.125)
        at(XP, VEC, pair)[...] = vector * jnp.concatenate([domain] * COMPS, 0)

    def store(pair, sums):
        domain = mask(pair)
        at(r_out, VEC, pair)[...] = jnp.concatenate([-domain * x for x in sums], 0)

    apply_rows(XP, CR, stencil, 5, 28, store)
    for t in range(own_rows // 2):
        x_out[t * VEC : (t + 1) * VEC] = at(XP, VEC, HALO + 1 + 2 * t)[...]

    blocks = lw_out.shape[2] // 3
    map_rows = blocks // 2
    tile_rows = map_rows // lat_count
    row = iota((rows, 1), 0) - HALO + group * own_rows
    shell = (lax.axis_size("group") - 1) * own_rows
    scale = jnp.where(jnp.logical_and(row >= 0, row < shell), -LOAD_SCALE, 0.0)
    own = slice(HALO, HALO + own_rows)
    for lb in range(lat_count):
        table = block(lb, 0, planes + 2 * rad_layers)
        spots = iota((rows, blocks), 1).astype(F32)
        own_spots = iota((own_rows, 128), 1).astype(F32)
        loads = jnp.zeros((rows, blocks), F32)
        lift = jnp.zeros((own_rows, 128), F32)
        for k in range(4):
            index, weight = table[:, k : k + 1], table[:, 4 + k : 5 + k]
            loads = loads + jnp.where(spots == index, weight, 0.0)
            right = index[own] >= map_rows
            near = index[own] - jnp.where(right, map_rows, 0) - (lat * tile_rows).astype(F32)
            here = jnp.logical_and(near >= 0, near < tile_rows)
            spot = jnp.where(here, near + jnp.where(right, tile_rows, 0), -1.0)
            lift = lift + jnp.where(own_spots == spot, weight[own], 0.0)
        loads = loads * scale
        high = loads.astype(BF16).astype(F32)
        middle = (loads - high).astype(BF16).astype(F32)
        low = loads - high - middle
        lw_out[lb] = jnp.concatenate([high, middle, low], 1).astype(BF16)
        lift = lift * (1.0 / LAYERS)
        for layer in range(LAYERS):
            first = lb * own_rows * LAYERS + layer
            ut_out[pl.ds(first, own_rows, LAYERS), :] = lift


def krylov_kernel(*refs, loads):
    load_refs = refs[:loads]
    stencil, r_in, coefs, x_own, lw, ut = refs[loads : loads + 6]
    payload, v_out = refs[loads + 6 : loads + 8]
    V, TOP = refs[loads + 8 :]
    lat = lax.axis_index("lat")
    lat_count = lax.axis_size("lat")
    cols = r_in.shape[1]
    width = cols // lat_count
    pairs = x_own.shape[0] // VEC
    own_rows = 2 * pairs
    if loads == 2:
        own, other = load_refs[0][...], load_refs[1][...]
        own, other = own.astype(F32), other.astype(F32)
        tiles = [jnp.where(lat == 0, own, other), jnp.where(lat == 0, other, own)]
        field = jnp.concatenate(tiles, 0)
    else:
        field = load_refs[0][...].astype(F32)
    half = field.shape[1] // 2
    blocks = jnp.concatenate([field[:, :half], field[:, half:]], 0)
    blocks = jnp.concatenate([blocks] * 3, 0).astype(BF16)
    for lb in range(lat_count):
        TOP[lb] = jnp.zeros(TOP.shape[1:], F32)
        top = jnp.dot(lw[lb], blocks, preferred_element_type=F32)
        for q in range(2):
            TOP[lb, pl.ds((1 - q) * PAIR + q * LAYERS, top.shape[0], PAIR), :] = top
    for pair in range(5, 28):
        vector = at(r_in, VEC, pair)[...]
        top = [at(TOP.at[lb], PAIR, pair)[...] for lb in range(lat_count)]
        upright = vector[2 * PAIR :] + jnp.concatenate(top, 1)
        at(V.at[0], VEC, pair)[...] = jnp.concatenate([vector[: 2 * PAIR], upright], 0)
    mask = domain_of(own_rows, cols)
    for n in range(ITERS):

        def store(pair, sums, n=n):
            domain = mask(pair)
            fresh = jnp.concatenate([domain * x for x in sums], 0)
            at(V.at[n + 1], VEC, pair)[...] = fresh - at(V.at[n], VEC, pair)[...]

        apply_rows(V.at[n], coefs, stencil, 6 + n, 27 - n, store)

    own_pairs = [HALO + 1 + 2 * t for t in range(pairs)]
    sums = [None] * (2 * ITERS)
    for pair in own_pairs:
        values = [at(V.at[n], VEC, pair)[...] for n in range(ITERS + 1)]
        for k in range(2 * ITERS):
            product = values[k // 2] * values[(k + 1) // 2]
            for r in range(COMPS):
                for c in range(cols // 128):
                    piece = product[PAIR * r : PAIR * r + PAIR, 128 * c : 128 * c + 128]
                    sums[k] = piece if sums[k] is None else sums[k] + piece
    for k in range(2 * ITERS):
        payload[k : k + 1] = jnp.sum(sums[k], 0, keepdims=True)
    fields = []
    upright = slice(2 * PAIR, VEC)
    for lb in range(lat_count):
        lanes = slice(lb * width, (lb + 1) * width)
        row = [[x_own[t * VEC + 2 * PAIR : (t + 1) * VEC, lanes] for t in range(pairs)]]
        for n in range(ITERS):
            row.append([at(V.at[n], VEC, pair)[upright, lanes] for pair in own_pairs])
        fields.append(jnp.concatenate([jnp.concatenate(x, 0) for x in row], 1))
    fields = jnp.concatenate(fields, 0)
    spots = (payload.shape[0] - 2 * ITERS) // (ITERS + 1)
    lift = lax.dot_general(
        ut[...],
        fields,
        (((0,), (0,)), ((), ())),
        precision=lax.Precision.HIGHEST,
        preferred_element_type=F32,
    )
    for n in range(ITERS + 1):
        payload[2 * ITERS + n * spots : 2 * ITERS + (n + 1) * spots] = lift[
            :spots, n * width : (n + 1) * width
        ]
    own = pl.ds(pl.multiple_of(lat * width, 128), width)
    for n in range(ITERS):
        for t, pair in enumerate(own_pairs):
            v_out[n, t * VEC : (t + 1) * VEC] = V[n, pair * VEC : (pair + 1) * VEC, own]
    v_out[ITERS] = x_own[:, own]


def finish_kernel(payload, theta, v, bed, disp_out, bed_out, X):
    rad = lax.axis_index("rad")
    moment = [
        jnp.broadcast_to(jnp.sum(payload[k : k + 1], 1, keepdims=True), (8, 128))
        for k in range(2 * ITERS)
    ]

    def product(left, right, size=False):
        by_degree = {}
        for i, a in enumerate(left):
            for j, b in enumerate(right):
                term = a * b
                if size:
                    term = jnp.abs(term)
                by_degree[i + j] = by_degree[i + j] + term if i + j in by_degree else term
        total = None
        for k, weight in by_degree.items():
            term = weight * (jnp.abs(moment[k]) if size else moment[k])
            total = term if total is None else total + term
        return total

    def shifted(poly):
        result = list(poly) + [jnp.zeros((8, 128), F32)]
        for i, a in enumerate(poly):
            result[i + 1] = result[i + 1] + a
        return result

    one, zero = jnp.ones((8, 128), F32), jnp.zeros((8, 128), F32)
    residual, direction, answer = [one], [one], [zero] * ITERS
    norm = moment[0]
    live = None
    for n in range(ITERS):
        image = shifted(direction)
        step = norm / product(direction, image)
        if live is not None:
            step = jnp.where(live, step, 0.0)
        for i, a in enumerate(direction):
            answer[i] = answer[i] + step * a
        if n == ITERS - 1:
            break
        residual = [
            (residual[i] if i < len(residual) else zero) - step * a for i, a in enumerate(image)
        ]
        fresh = product(residual, residual)
        above = fresh > 1e-7 * product(residual, residual, True)
        live = above if live is None else jnp.logical_and(live, above)
        ratio = jnp.where(live, fresh / norm, 0.0)
        direction = [
            a + (ratio * direction[i] if i < len(direction) else zero)
            for i, a in enumerate(residual)
        ]
        norm = jnp.where(live, fresh, 1.0)
    raw = [a[0:1] for a in answer]
    answer = [a / theta[0:1] for a in raw]
    total = v[ITERS]
    for n in range(ITERS):
        total = total + answer[n] * v[n]
    X[...] = total
    layers = disp_out.shape[1]
    pairs = disp_out.shape[2] // 2
    for c in range(COMPS):
        for k in range(layers):
            for q in range(2):
                lower = X[pl.ds(c * PAIR + q * LAYERS + k, pairs, VEC), :]
                upper = X[pl.ds(c * PAIR + q * LAYERS + layers + k, pairs, VEC), :]
                disp_out[c, k, pl.ds(q, pairs, 2), :] = jnp.where(rad == 0, lower, upper)
    rows, cols = bed.shape
    spots = 2 * rows
    base = 2 * ITERS
    lift = payload[base : base + spots]
    for n in range(ITERS):
        lift = lift + answer[n] * payload[base + (n + 1) * spots : base + (n + 2) * spots]
    for h in range(2):
        lanes = slice(h * cols // 2, (h + 1) * cols // 2)
        bed_out[:, lanes] = bed[:, lanes] + UPLIFT_SCALE * lift[h * rows : (h + 1) * rows]


def per_device(
    displacement_prev,
    shear_modulus,
    viscosity,
    element_matrix,
    regrid_index,
    regrid_weight,
    ice_thickness,
    bed_elevation,
    basal_friction,
    ice_mask,
    speed_guess,
):
    groups, lats = lax.axis_size("group"), lax.axis_size("lat")
    rad_layers, own_rows, width = shear_modulus.shape
    tile_rows, map_cols = ice_thickness.shape
    cols = lats * width
    blocks = 2 * tile_rows * lats
    planes = COMPS * rad_layers + 2 * rad_layers + 1
    ice_args = (speed_guess, ice_thickness, bed_elevation, basal_friction, ice_mask)

    edges = ice_edges(*ice_args)
    if lats == 2:
        halos = [lax.ppermute(edges[0], "lat", [(0, 1), (1, 0)])]
    else:
        halos = [
            lax.ppermute(edges[1], "lat", [(i, i + 1) for i in range(lats - 1)]),
            lax.ppermute(edges[0], "lat", [(i + 1, i) for i in range(lats - 1)]),
        ]
    low, high = call(
        functools.partial(pack_kernel, map_rows=tile_rows * lats),
        "pack",
        (pltpu.VMEM((planes, HALO, width), F32),) * 2,
        (
            displacement_prev,
            shear_modulus,
            viscosity,
            regrid_index[:, 0].T,
            regrid_weight[:, 0].T,
        ),
        [pltpu.VMEM((8, 128), F32)],
    )
    north = lax.ppermute(high, "group", [(i, (i + 1) % groups) for i in range(groups)])
    south = lax.ppermute(low, "group", [(i, (i - 1) % groups) for i in range(groups)])
    stencil, theta = stencil_of(element_matrix)
    region = call(
        region_kernel,
        "region",
        pltpu.VMEM((planes, 2 * own_rows, width), F32),
        keep(north, low, high, south),
    )
    if lats == 2:
        pieces = [region, lax.ppermute(region, "rad", [(0, 1), (1, 0)])]
        region, halos = lax.optimization_barrier((region, halos))
        pieces.append(lax.ppermute(region, "lat", [(0, 1), (1, 0)]))
        pieces.append(lax.ppermute(pieces[2], "rad", [(0, 1), (1, 0)]))
    else:
        pieces = [lax.all_gather(region, ("lat", "rad"))]
    ice_load = ice_load_of(*ice_args, halos)
    if lats == 2:
        loads = [ice_load, lax.ppermute(ice_load, "lat", [(0, 1), (1, 0)])]
    else:
        loads = [lax.all_gather(ice_load, "lat", axis=0, tiled=True)]
    pairs = own_rows // 2
    r_start, coefs, x_own, lw, ut = call(
        functools.partial(relax_kernel, pieces=len(pieces)),
        "relax",
        (
            pltpu.VMEM((33 * VEC, cols), F32),
            pltpu.VMEM((33 * 4 * PAIR, cols), F32),
            pltpu.VMEM((pairs * VEC, cols), F32),
            pltpu.VMEM((lats, 2 * own_rows, 3 * blocks), BF16),
            pltpu.VMEM((lats * own_rows * LAYERS, 128), F32),
        ),
        keep(*pieces, stencil, theta),
        [
            pltpu.VMEM((33 * VEC, cols), F32),
            pltpu.VMEM((33 * 4 * PAIR, cols), F32),
            pltpu.VMEM((lats, 33 * VEC, width), F32),
            pltpu.VMEM((lats, 33 * PAIR, width), F32),
            pltpu.VMEM((lats, 33 * PAIR, width), F32),
        ],
    )
    spots = 2 * tile_rows
    payload, vectors = call(
        functools.partial(krylov_kernel, loads=len(loads)),
        "krylov",
        (
            pltpu.VMEM((2 * ITERS + (ITERS + 1) * spots, width), F32),
            pltpu.VMEM((ITERS + 1, pairs * VEC, width), F32),
        ),
        keep(*loads, stencil, r_start, coefs, x_own, lw, ut),
        [
            pltpu.VMEM((ITERS + 1, 33 * VEC, cols), F32),
            pltpu.VMEM((lats, 33 * PAIR, width), F32),
        ],
    )
    step = 1
    while step < groups:
        payload = payload + lax.ppermute(
            payload, "group", [(i, i ^ step) for i in range(groups)]
        )
        step *= 2
    return call(
        finish_kernel,
        "finish",
        (
            jax.ShapeDtypeStruct((COMPS, rad_layers, own_rows, width), F32),
            jax.ShapeDtypeStruct((tile_rows, map_cols), F32),
        ),
        (*keep(payload, theta, vectors), bed_elevation),
        [pltpu.VMEM((pairs * VEC, width), F32)],
    )


def solution(mesh):
    in_specs = (
        P(None, "rad", "group", "lat"),
        P("rad", "group", "lat"),
        P("rad", "group", "lat"),
        P(),
        P("group", "lat", None),
        P("group", "lat", None),
        P("lat", None),
        P("lat", None),
        P("lat", None),
        P("lat", None),
        P(None, "lat", None),
    )
    out_specs = (P(None, "rad", "group", "lat"), P("lat", None))
    return jax.shard_map(
        per_device, mesh=mesh, in_specs=in_specs, out_specs=out_specs, check_vma=False
    )
```

time: 78.7 us -> 50.4 us (0.64)
  Pallas kernels: 30.8 us -> 8.81 us
  waiting for transfers between devices: 25.1 us -> 19.2 us
  other arithmetic: 3.93 us -> 0.03 us
  local copies, waits for them, and re-layouts: 6.14 us -> 8.13 us
  starting transfers between devices: 11.2 us -> 12.7 us
    pallas_call x5 -> x8, Pallas kernels: 30.8 us -> 8.81 us  [call(): pl.pallas_call(body, out_shape=out, in_specs=specs or [vmem()] * len(inpu...]
    ppermute x6, waiting for transfers between devices: 10.7 us -> 7.15 us  [the longest x1 5.12 us: per_device(): pieces.append(lax.ppermute(region, 'lat', [(0, 1), (1, 0)]))]
    ppermute x3, starting transfers between devices: 0.6 us -> 4.04 us  [per_device(): lax.ppermute(payload, 'group', [(i, i ^ step) for i in range(groups)])]
    ppermute x3, waiting for transfers between devices: 14.4 us -> 11.4 us  [per_device(): lax.ppermute(payload, 'group', [(i, i ^ step) for i in range(groups)])]
    unnamed x22 -> x32, local copies, waits for them, and re-layouts: 5.21 us -> 8.13 us
    concatenate x3 -> x0, other arithmetic: 1.57 us -> none  [the longest x1 0.84 us: per_device(): jnp.concatenate([displacement_prev.reshape(COMPS * rad_layers, own_rows,...]
    ppermute x6, starting transfers between devices: 9.73 us -> 8.2 us  [the longest x1 3.2 us: per_device(): lax.ppermute(low, 'group', [(i, (i - 1) % groups) for i in range(groups)])]
    add x3, other arithmetic: 1.56 us -> 0.03 us  [per_device(): payload + lax.ppermute(payload, 'group', [(i, i ^ step) for i in range(gr...]
  transfers between devices with their start and end apart: 10 -> 10, of which waited for: 4 -> 6; matrix products, arithmetic and copies ran while one was open for 5% -> 0% of each run, Pallas kernels for 24% -> 11%
where the time goes in v2:
time: 50.4 us; the launch traced here: 49.6 us
  waiting for transfers between devices  19.2 us (38%)
  starting transfers between devices  12.7 us (25%)
  Pallas kernels  8.81 us (17%)
  local copies, waits for them, and re-layouts  8.13 us (16%)
  between operations  0.74 us (1%)
    ppermute x3, waiting for transfers between devices, per_device(): lax.ppermute(payload, 'group', [(i, i ^ step) for i in range(groups)])  11.4 us
    pallas_call x8, Pallas kernels, call(): pl.pallas_call(body, out_shape=out, in_specs=specs or [vmem()] * len(inpu...  8.81 us
    unnamed x32, local copies, waits for them, and re-layouts  8.13 us
    ppermute x1, waiting for transfers between devices, per_device(): pieces.append(lax.ppermute(region, 'lat', [(0, 1), (1, 0)]))  5.12 us
    ppermute x3, starting transfers between devices, per_device(): lax.ppermute(payload, 'group', [(i, i ^ step) for i in range(groups)])  4.04 us
    ppermute x1, starting transfers between devices, per_device(): lax.ppermute(low, 'group', [(i, (i - 1) % groups) for i in range(groups)])  3.2 us
    ppermute x1, starting transfers between devices, per_device(): halos = [lax.ppermute(edges[0], 'lat', [(0, 1), (1, 0)])]  3.03 us
    ppermute x1, waiting for transfers between devices, per_device(): lax.ppermute(high, 'group', [(i, (i + 1) % groups) for i in range(groups)])  2.02 us
  transfers between devices with their start and end apart: 10, of which 6 were waited for; matrix products, arithmetic and copies ran while one was open for 0% of the time, Pallas kernels for 11%

profile of v2, /device:TPU:0, one launch (start us, length us, event | category | flops | bytes accessed | tf_op | source)
XLA Modules:
  0.0 49.6 jit_solution(11251224991594235452)
XLA Ops:
  0.6 0.0 copy-start
  0.6 0.9 %copy-done = f32[16,16,256]{2,1,0:T(8,128)S(1)} copy-done((f32[16,16,256]{2,1,0:T(8,128)S(1)}, f32[16,16,256]{2,1,0:T(8,128)}, u32[]{:S(2)}) %copy-start) | copy-done | bytes 262168
  1.6 0.0 copy-start.3
  1.6 0.7 %copy-done.3 = f32[16,256]{1,0:T(8,128)S(1)} copy-done((f32[16,256]{1,0:T(8,128)S(1)}, f32[16,256]{1,0:T(8,128)}, u32[]{:S(2)}) %copy-start.3) | copy-done | bytes 16408
  2.3 0.0 copy-start.5
  2.3 0.7 %copy-done.5 = f32[16,256]{1,0:T(8,128)S(1)} copy-done((f32[16,256]{1,0:T(8,128)S(1)}, f32[16,256]{1,0:T(8,128)}, u32[]{:S(2)}) %copy-start.5) | copy-done | bytes 16408
  3.0 0.0 copy-start.6
  3.0 0.7 %copy-done.6 = f32[16,256]{1,0:T(8,128)S(1)} copy-done((f32[16,256]{1,0:T(8,128)S(1)}, f32[16,256]{1,0:T(8,128)}, u32[]{:S(2)}) %copy-start.6) | copy-done | bytes 16408
  3.7 0.0 copy-start.7
  3.7 0.7 %copy-done.7 = s32[16,256]{1,0:T(8,128)S(1)} copy-done((s32[16,256]{1,0:T(8,128)S(1)}, s32[16,256]{1,0:T(8,128)}, u32[]{:S(2)}) %copy-start.7) | copy-done | bytes 16408
  4.5 0.1 edge.1
  4.6 3.0 %collective-permute-start.2 = (f32[20,8,256]{2,1,0:T(8,128)S(1)}, f32[20,8,256]{2,1,0:T(8,128)S(1)}, u32[]{:S(2)}, u32[]{:S(2)}) collective-permute-start(f32[20,8,256]{2,1,0:T(8,128)S(1)} %edge.1), channel_id=1, source_target_pairs={{0,2},{2,0},{1,3},{3,1},{4,6},{6,4},{5,7},{7,5},{8,10},{10,8},{9,1... | collective-permute-start | bytes 491528 | tf_op jit(solution)/shard_map/ppermute | solution.py:697
  7.6 0.8 %copy-done.10 = f32[3,2,16,128]{3,2,1,0:T(8,128)S(1)} copy-done((f32[3,2,16,128]{3,2,1,0:T(8,128)S(1)}, f32[3,2,16,128]{3,2,1,0:T(8,128)}, u32[]{:S(2)}) %copy-start.10) | copy-done | bytes 49176
  8.4 0.7 %copy-done.11 = f32[2,16,128]{2,1,0:T(8,128)S(1)} copy-done((f32[2,16,128]{2,1,0:T(8,128)S(1)}, f32[2,16,128]{2,1,0:T(8,128)}, u32[]{:S(2)}) %copy-start.11) | copy-done | bytes 16408
  9.1 0.7 %copy-done.12 = f32[2,16,128]{2,1,0:T(8,128)S(1)} copy-done((f32[2,16,128]{2,1,0:T(8,128)S(1)}, f32[2,16,128]{2,1,0:T(8,128)}, u32[]{:S(2)}) %copy-start.12) | copy-done | bytes 16408
  9.9 0.7 %copy-done.14 = s32[16,1,4]{0,2,1:T(4,128)S(1)} copy-done((s32[16,1,4]{0,2,1:T(4,128)S(1)}, s32[16,1,4]{0,2,1:T(4,128)}, u32[]{:S(2)}) %copy-start.14) | copy-done | bytes 280
  10.5 0.7 %copy-done.15 = f32[16,1,4]{0,2,1:T(4,128)S(1)} copy-done((f32[16,1,4]{0,2,1:T(4,128)S(1)}, f32[16,1,4]{0,2,1:T(4,128)}, u32[]{:S(2)}) %copy-start.15) | copy-done | bytes 280
  11.2 0.1 pack.1
  11.3 1.5 %collective-permute-start = (f32[11,8,128]{2,1,0:T(8,128)S(1)}, f32[11,8,128]{2,1,0:T(8,128)S(1)}, u32[]{:S(2)}, u32[]{:S(2)}) collective-permute-start(f32[11,8,128]{2,1,0:T(8,128)S(1)} %get-tuple-element.15.high), channel_id=1, source_target_pairs={{0,4},{4,8},{8,12},{12,16},{16,20},{20,24},{24,28},{28,0},{1,5},{5... | collective-permute-start | bytes 135176 | tf_op jit(solution)/shard_map/ppermute | solution.py:716
  12.8 3.2 %collective-permute-start.1 = (f32[11,8,128]{2,1,0:T(8,128)S(1)}, f32[11,8,128]{2,1,0:T(8,128)S(1)}, u32[]{:S(2)}, u32[]{:S(2)}) collective-permute-start(f32[11,8,128]{2,1,0:T(8,128)S(1)} %get-tuple-element.16.low), channel_id=1, source_target_pairs={{0,28},{4,0},{8,4},{12,8},{16,12},{20,16},{24,20},{28,24},{1,29},{... | collective-permute-start | bytes 135176 | tf_op jit(solution)/shard_map/ppermute | solution.py:717
  16.0 2.0 %collective-permute-done.north = f32[11,8,128]{2,1,0:T(8,128)S(1)} collective-permute-done((f32[11,8,128]{2,1,0:T(8,128)S(1)}, f32[11,8,128]{2,1,0:T(8,128)S(1)}, u32[]{:S(2)}, u32[]{:S(2)}) %collective-permute-start) | collective-permute-done | bytes 45088 | tf_op jit(solution)/shard_map/ppermute | solution.py:716
  18.0 0.0 collective-permute-done.1.south
  18.1 0.0 collective-permute-done.2.refs_5_
  18.1 0.4 collective-permute-start.5
  18.5 0.0 collective-permute-start.4
  18.5 5.1 %collective-permute-done.5.refs_2_ = f32[11,32,128]{2,1,0:T(8,128)S(1)} collective-permute-done((f32[11,32,128]{2,1,0:T(8,128)S(1)}, f32[11,32,128]{2,1,0:T(8,128)S(1)}, u32[]{:S(2)}, u32[]{:S(2)}) %collective-permute-start.5) | collective-permute-done | bytes 180256 | tf_op jit(solution)/shard_map/ppermute | solution.py:728
  23.6 0.0 collective-permute-start.6
  23.6 0.0 copy-done.1
  23.6 3.5 %ice.1.refs_0_ = bf16[16,256]{1,0:T(8,128)(2,1)S(1)} custom-call(f32[16,16,256]{2,1,0:T(8,128)S(1)} %copy-done.1, f32[16,256]{1,0:T(8,128)S(1)} %copy-done.5, f32[16,256]{1,0:T(8,128)S(1)} %copy-done.3, f32[16,256]{1,0:T(8,128)S(1)} %copy-done.6, s32[16,256]{1,0:T(8,128)S(1)} %copy-done.7, f32[20,8,256]{2,1,0:T(8,128)S(1)} %collective-permute-done.2.refs_5_), custom_call_target="tpu_custom_call" | custom-call | tf_op jit(solution)/shard_map/ice/pallas_call | solution.py:38
  27.2 0.4 collective-permute-start.3
  27.6 0.0 copy-done.2
  27.6 0.0 copy-done.8
  27.6 0.0 copy-done.9
  27.6 0.7 %copy-done.13 = f32[24,24]{1,0:T(8,128)S(1)} copy-done((f32[24,24]{1,0:T(8,128)S(1)}, f32[24,24]{1,0:T(8,128)}, u32[]{:S(2)}) %copy-start.13) | copy-done | bytes 2328
  28.3 0.6 %stencil.1 = (bf16[96,240]{1,0:T(8,128)(2,1)S(1)}, f32[8,128]{1,0:T(8,128)S(1)}) custom-call(f32[24,24]{1,0:T(8,128)S(1)} %copy-done.13, f32[96,24]{1,0:T(8,128)S(1)} %copy-done.9, f32[4,24,72]{2,1,0:T(8,128)S(1)} %copy-done.8, f32[4,96,72]{2,1,0:T(8,128)S(1)} %copy-done.2), custom_call_target="tpu_custom_call" | custom-call | tf_op jit(solution)/shard_map/stencil/pallas_call | solution.py:38
  28.9 0.0 collective-permute-done.4.refs_1_
  28.9 0.0 collective-permute-done.6.refs_3_
  28.9 1.3 %relax.1 = (f32[792,256]{1,0:T(8,128)S(1)}, f32[1056,256]{1,0:T(8,128)S(1)}, f32[192,256]{1,0:T(8,128)S(1)}, bf16[2,32,192]{2,1,0:T(8,128)(2,1)S(1)}, f32[128,128]{1,0:T(8,128)S(1)}) custom-call(f32[11,32,128]{2,1,0:T(8,128)S(1)} %region.1.refs_0_, f32[11,32,128]{2,1,0:T(8,128)S(1)} %collective-permute-done.4.refs_1_, ...), custom_call_target="tpu_custom_call" | custom-call | tf_op jit(solution)/shard_map/relax/pallas_call | solution.py:38
  30.2 0.6 %collective-permute-done.3.refs_1_ = bf16[16,256]{1,0:T(8,128)(2,1)S(1)} collective-permute-done((bf16[16,256]{1,0:T(8,128)(2,1)S(1)}, bf16[16,256]{1,0:T(8,128)(2,1)S(1)}, u32[]{:S(2)}, u32[]{:S(2)}) %collective-permute-start.3) | collective-permute-done | bytes 8224 | tf_op jit(solution)/shard_map/ppermute | solution.py:734
  30.9 2.3 %krylov.1 = (f32[168,128]{1,0:T(8,128)S(1)}, f32[5,192,128]{2,1,0:T(8,128)S(1)}) custom-call(bf16[16,256]{1,0:T(8,128)(2,1)S(1)} %ice.1.refs_0_, bf16[16,256]{1,0:T(8,128)(2,1)S(1)} %collective-permute-done.3.refs_1_, bf16[96,240]{1,0:T(8,128)(2,1)S(1)} %get-tuple-element.18.refs_4_.refs_2_, f32[792,256]{1,0:T(8,128)S(1)} %get-tuple-element.21.refs_3_, ...), custom_call_target="tpu_custom_call" | custom-call | tf_op jit(solution)/shard_map/krylov/pallas_call | solution.py:38
  33.2 1.3 %collective-permute-start.7 = (f32[168,128]{1,0:T(8,128)S(1)}, f32[168,128]{1,0:T(8,128)S(1)}, u32[]{:S(2)}, u32[]{:S(2)}) collective-permute-start(f32[168,128]{1,0:T(8,128)S(1)} %get-tuple-element.26), channel_id=1, source_target_pairs={{0,4},{4,0},{8,12},{12,8},{16,20},{20,16},{24,28},{28,24},{1,5},{5... | collective-permute-start | bytes 258056 | tf_op jit(solution)/shard_map/ppermute | solution.py:773
  34.5 3.2 %collective-permute-done.7 = f32[168,128]{1,0:T(8,128)S(1)} collective-permute-done((f32[168,128]{1,0:T(8,128)S(1)}, f32[168,128]{1,0:T(8,128)S(1)}, u32[]{:S(2)}, u32[]{:S(2)}) %collective-permute-start.7) | collective-permute-done | bytes 86048 | tf_op jit(solution)/shard_map/ppermute | solution.py:773
  37.8 0.9 %collective-permute-start.8 = (f32[168,128]{1,0:T(8,128)S(1)}, f32[168,128]{1,0:T(8,128)S(1)}, u32[]{:S(2)}, u32[]{:S(2)}) collective-permute-start(f32[168,128]{1,0:T(8,128)S(1)} %add.9), channel_id=1, source_target_pairs={{0,8},{4,12},{8,0},{12,4},{16,24},{20,28},{24,16},{28,20},{1,9},{5... | collective-permute-start | bytes 258056 | tf_op jit(solution)/shard_map/ppermute | solution.py:773
  38.6 3.7 %collective-permute-done.8 = f32[168,128]{1,0:T(8,128)S(1)} collective-permute-done((f32[168,128]{1,0:T(8,128)S(1)}, f32[168,128]{1,0:T(8,128)S(1)}, u32[]{:S(2)}, u32[]{:S(2)}) %collective-permute-start.8) | collective-permute-done | bytes 86048 | tf_op jit(solution)/shard_map/ppermute | solution.py:773
  42.3 1.9 %collective-permute-start.9 = (f32[168,128]{1,0:T(8,128)S(1)}, f32[168,128]{1,0:T(8,128)S(1)}, u32[]{:S(2)}, u32[]{:S(2)}) collective-permute-start(f32[168,128]{1,0:T(8,128)S(1)} %add.10), channel_id=1, source_target_pairs={{0,16},{4,20},{8,24},{12,28},{16,0},{20,4},{24,8},{28,12},{1,17},{... | collective-permute-start | bytes 258056 | tf_op jit(solution)/shard_map/ppermute | solution.py:773
  44.2 4.5 %collective-permute-done.9 = f32[168,128]{1,0:T(8,128)S(1)} collective-permute-done((f32[168,128]{1,0:T(8,128)S(1)}, f32[168,128]{1,0:T(8,128)S(1)}, u32[]{:S(2)}, u32[]{:S(2)}) %collective-permute-start.9) | collective-permute-done | bytes 86048 | tf_op jit(solution)/shard_map/ppermute | solution.py:773
  48.7 0.0 copy-done.4
  48.7 0.9 %finish.1 = (f32[3,2,16,128]{3,2,1,0:T(8,128)}, f32[16,256]{1,0:T(8,128)}) custom-call(f32[168,128]{1,0:T(8,128)S(1)} %add.11.payload, f32[8,128]{1,0:T(8,128)S(1)} %get-tuple-element.20.refs_5_.theta, f32[5,192,128]{2,1,0:T(8,128)S(1)} %get-tuple-element.27.v, f32[16,256]{1,0:T(8,128)S(1)} %copy-done.4), custom_call_target="tpu_custom_call" | custom-call | tf_op jit(solution)/shard_map/finish/pallas_call | solution.py:38
  (15 shorter events, 0.1 us)
Async XLA Ops:
  0.6 1.0 %copy-start = (f32[16,16,256]{2,1,0:T(8,128)S(1)}, f32[16,16,256]{2,1,0:T(8,128)}, u32[]{:S(2)}) copy-start(f32[16,16,256]{2,1,0:T(8,128)} %refs_0_.1) | copy-start | bytes 786436
  1.6 0.7 %copy-start.3 = (f32[16,256]{1,0:T(8,128)S(1)}, f32[16,256]{1,0:T(8,128)}, u32[]{:S(2)}) copy-start(f32[16,256]{1,0:T(8,128)} %bed.3) | copy-start | bytes 49156
  2.3 0.7 %copy-start.5 = (f32[16,256]{1,0:T(8,128)S(1)}, f32[16,256]{1,0:T(8,128)}, u32[]{:S(2)}) copy-start(f32[16,256]{1,0:T(8,128)} %refs_1_.1) | copy-start | bytes 49156
  3.0 0.7 %copy-start.6 = (f32[16,256]{1,0:T(8,128)S(1)}, f32[16,256]{1,0:T(8,128)}, u32[]{:S(2)}) copy-start(f32[16,256]{1,0:T(8,128)} %refs_3_.1) | copy-start | bytes 49156
  3.7 0.7 %copy-start.7 = (s32[16,256]{1,0:T(8,128)S(1)}, s32[16,256]{1,0:T(8,128)}, u32[]{:S(2)}) copy-start(s32[16,256]{1,0:T(8,128)} %refs_4_.1) | copy-start | bytes 49156
  4.5 19.2 %copy-start.1 = (f32[16,16,256]{2,1,0:T(8,128)S(1)}, f32[16,16,256]{2,1,0:T(8,128)}, u32[]{:S(2)}) copy-start(f32[16,16,256]{2,1,0:T(8,128)} %refs_0_.1) | copy-start | bytes 786436
  4.5 23.1 %copy-start.2 = (f32[4,96,72]{2,1,0:T(8,128)S(1)}, f32[4,96,72]{2,1,0:T(8,128)}, u32[]{:S(2)}) copy-start(f32[4,96,72]{2,1,0:T(8,128)} %constant.8.clone.keep) | copy-start | bytes 331780
  4.5 23.1 %copy-start.8 = (f32[4,24,72]{2,1,0:T(8,128)S(1)}, f32[4,24,72]{2,1,0:T(8,128)}, u32[]{:S(2)}) copy-start(f32[4,24,72]{2,1,0:T(8,128)} %constant.7.clone.pick_col) | copy-start | bytes 82948
  4.5 23.1 %copy-start.9 = (f32[96,24]{1,0:T(8,128)S(1)}, f32[96,24]{1,0:T(8,128)}, u32[]{:S(2)}) copy-start(f32[96,24]{1,0:T(8,128)} %constant.6.clone.pick_row) | copy-start | bytes 27652
  4.6 13.5 %collective-permute-start.2 = (f32[20,8,256]{2,1,0:T(8,128)S(1)}, f32[20,8,256]{2,1,0:T(8,128)S(1)}, u32[]{:S(2)}, u32[]{:S(2)}) collective-permute-start(f32[20,8,256]{2,1,0:T(8,128)S(1)} %edge.1), channel_id=1, source_target_pairs={{0,2},{2,0},{1,3},{3,1},{4,6},{6,4},{5,7},{7,5},{8,10},{10,8},{9,1... | collective-permute-start | bytes 491528 | tf_op jit(solution)/shard_map/ppermute | solution.py:697
  7.6 0.8 %copy-start.10 = (f32[3,2,16,128]{3,2,1,0:T(8,128)S(1)}, f32[3,2,16,128]{3,2,1,0:T(8,128)}, u32[]{:S(2)}) copy-start(f32[3,2,16,128]{3,2,1,0:T(8,128)} %disp.1) | copy-start | bytes 147460
  8.4 0.7 %copy-start.11 = (f32[2,16,128]{2,1,0:T(8,128)S(1)}, f32[2,16,128]{2,1,0:T(8,128)}, u32[]{:S(2)}) copy-start(f32[2,16,128]{2,1,0:T(8,128)} %shear.1) | copy-start | bytes 49156
  9.1 0.7 %copy-start.12 = (f32[2,16,128]{2,1,0:T(8,128)S(1)}, f32[2,16,128]{2,1,0:T(8,128)}, u32[]{:S(2)}) copy-start(f32[2,16,128]{2,1,0:T(8,128)} %visc.1) | copy-start | bytes 49156
  9.9 0.7 %copy-start.14 = (s32[16,1,4]{0,2,1:T(4,128)S(1)}, s32[16,1,4]{0,2,1:T(4,128)}, u32[]{:S(2)}) copy-start(s32[16,1,4]{0,2,1:T(4,128)} %param.18) | copy-start | bytes 772
  10.5 0.7 %copy-start.15 = (f32[16,1,4]{0,2,1:T(4,128)S(1)}, f32[16,1,4]{0,2,1:T(4,128)}, u32[]{:S(2)}) copy-start(f32[16,1,4]{0,2,1:T(4,128)} %param.19) | copy-start | bytes 772
  11.3 6.7 %collective-permute-start = (f32[11,8,128]{2,1,0:T(8,128)S(1)}, f32[11,8,128]{2,1,0:T(8,128)S(1)}, u32[]{:S(2)}, u32[]{:S(2)}) collective-permute-start(f32[11,8,128]{2,1,0:T(8,128)S(1)} %get-tuple-element.15.high), channel_id=1, source_target_pairs={{0,4},{4,8},{8,12},{12,16},{16,20},{20,24},{24,28},{28,0},{1,5},{5... | collective-permute-start | bytes 135176 | tf_op jit(solution)/shard_map/ppermute | solution.py:716
  12.8 5.2 %collective-permute-start.1 = (f32[11,8,128]{2,1,0:T(8,128)S(1)}, f32[11,8,128]{2,1,0:T(8,128)S(1)}, u32[]{:S(2)}, u32[]{:S(2)}) collective-permute-start(f32[11,8,128]{2,1,0:T(8,128)S(1)} %get-tuple-element.16.low), channel_id=1, source_target_pairs={{0,28},{4,0},{8,4},{12,8},{16,12},{20,16},{24,20},{28,24},{1,29},{... | collective-permute-start | bytes 135176 | tf_op jit(solution)/shard_map/ppermute | solution.py:717
  18.1 5.6 %collective-permute-start.5 = (f32[11,32,128]{2,1,0:T(8,128)S(1)}, f32[11,32,128]{2,1,0:T(8,128)S(1)}, u32[]{:S(2)}, u32[]{:S(2)}) collective-permute-start(f32[11,32,128]{2,1,0:T(8,128)S(1)} %region.1.refs_0_), channel_id=1, source_target_pairs={{0,2},{2,0},{1,3},{3,1},{4,6},{6,4},{5,7},{7,5},{8,10},{10,8},{9,1... | collective-permute-start | bytes 540680 | tf_op jit(solution)/shard_map/ppermute | solution.py:728
  18.5 10.4 %collective-permute-start.4 = (f32[11,32,128]{2,1,0:T(8,128)S(1)}, f32[11,32,128]{2,1,0:T(8,128)S(1)}, u32[]{:S(2)}, u32[]{:S(2)}) collective-permute-start(f32[11,32,128]{2,1,0:T(8,128)S(1)} %region.1.refs_0_), channel_id=1, source_target_pairs={{0,1},{1,0},{2,3},{3,2},{4,5},{5,4},{6,7},{7,6},{8,9},{9,8},{10,11... | collective-permute-start | bytes 540680 | tf_op jit(solution)/shard_map/ppermute | solution.py:726
  23.6 5.3 %collective-permute-start.6 = (f32[11,32,128]{2,1,0:T(8,128)S(1)}, f32[11,32,128]{2,1,0:T(8,128)S(1)}, u32[]{:S(2)}, u32[]{:S(2)}) collective-permute-start(f32[11,32,128]{2,1,0:T(8,128)S(1)} %collective-permute-done.5.refs_2_), channel_id=1, source_target_pairs={{0,1},{1,0},{2,3},{3,2},{4,5},{5,4},{6,7},{7,6},{8,9},{9,8},{10,11... | collective-permute-start | bytes 540680 | tf_op jit(solution)/shard_map/ppermute | solution.py:729
  27.2 3.7 %collective-permute-start.3 = (bf16[16,256]{1,0:T(8,128)(2,1)S(1)}, bf16[16,256]{1,0:T(8,128)(2,1)S(1)}, u32[]{:S(2)}, u32[]{:S(2)}) collective-permute-start(bf16[16,256]{1,0:T(8,128)(2,1)S(1)} %ice.1.refs_0_), channel_id=1, source_target_pairs={{0,2},{2,0},{1,3},{3,1},{4,6},{6,4},{5,7},{7,5},{8,10},{10,8},{9,1... | collective-permute-start | bytes 24584 | tf_op jit(solution)/shard_map/ppermute | solution.py:734
  27.6 0.7 %copy-start.13 = (f32[24,24]{1,0:T(8,128)S(1)}, f32[24,24]{1,0:T(8,128)}, u32[]{:S(2)}) copy-start(f32[24,24]{1,0:T(8,128)} %matrix.1) | copy-start | bytes 6916
  30.9 17.8 %copy-start.4 = (f32[16,256]{1,0:T(8,128)S(1)}, f32[16,256]{1,0:T(8,128)}, u32[]{:S(2)}) copy-start(f32[16,256]{1,0:T(8,128)} %bed.3) | copy-start | bytes 49156
  33.2 4.6 %collective-permute-start.7 = (f32[168,128]{1,0:T(8,128)S(1)}, f32[168,128]{1,0:T(8,128)S(1)}, u32[]{:S(2)}, u32[]{:S(2)}) collective-permute-start(f32[168,128]{1,0:T(8,128)S(1)} %get-tuple-element.26), channel_id=1, source_target_pairs={{0,4},{4,0},{8,12},{12,8},{16,20},{20,16},{24,28},{28,24},{1,5},{5... | collective-permute-start | bytes 258056 | tf_op jit(solution)/shard_map/ppermute | solution.py:773
  37.8 4.6 %collective-permute-start.8 = (f32[168,128]{1,0:T(8,128)S(1)}, f32[168,128]{1,0:T(8,128)S(1)}, u32[]{:S(2)}, u32[]{:S(2)}) collective-permute-start(f32[168,128]{1,0:T(8,128)S(1)} %add.9), channel_id=1, source_target_pairs={{0,8},{4,12},{8,0},{12,4},{16,24},{20,28},{24,16},{28,20},{1,9},{5... | collective-permute-start | bytes 258056 | tf_op jit(solution)/shard_map/ppermute | solution.py:773
  42.3 6.4 %collective-permute-start.9 = (f32[168,128]{1,0:T(8,128)S(1)}, f32[168,128]{1,0:T(8,128)S(1)}, u32[]{:S(2)}, u32[]{:S(2)}) collective-permute-start(f32[168,128]{1,0:T(8,128)S(1)} %add.10), channel_id=1, source_target_pairs={{0,16},{4,20},{8,24},{12,28},{16,0},{20,4},{24,8},{28,12},{1,17},{... | collective-permute-start | bytes 258056 | tf_op jit(solution)/shard_map/ppermute | solution.py:773

commit v3 on v2

--- a/solution.py
+++ b/solution.py
@@ -31,6 +31,10 @@
 
 def keep(*arrays):
     return [pltpu.with_memory_space_constraint(a, pltpu.VMEM) for a in arrays]
+
+
+def leave(*arrays):
+    return [pltpu.with_memory_space_constraint(a, pltpu.HBM) for a in arrays]
 
 
 def call(body, name, out, inputs, scratch=(), specs=None):
@@ -81,12 +85,12 @@
     if masked:
         own_at = HALO
         place(own_at, speed[...], own_four)
-        place(0, before[:levels], [before[levels + n] for n in range(4)])
-        place(HALO + own_rows, after[:levels], [after[levels + n] for n in range(4)])
+        place(0, *read_edge(before, levels))
+        place(HALO + own_rows, *read_edge(after, levels))
     else:
         own_at = lat * HALO
         place(own_at, speed[...], own_four)
-        place((1 - lat) * own_rows, halo[:levels], [halo[levels + n] for n in range(4)])
+        place((1 - lat) * own_rows, *read_edge(halo, levels))
     tiles = range(window // 8)
 
     def rows_of(t):
@@ -204,47 +208,23 @@
     out[...] = PL[1, pl.ds(pl.multiple_of(HALO + own_at, 8), own_rows), :].astype(BF16)
 
 
-def edge_kernel(speed, thick, bed, fric, mask, *rest, masked):
-    outs, sems = rest[:-1], rest[-1]
-    levels, own_rows, cols = speed.shape
-    top = own_rows - HALO
-    if masked:
-        starts = [0, top]
-    else:
-        starts = [jnp.where(lax.axis_index("lat") == 0, top, 0)]
-    copies = []
-    for n, (start, out) in enumerate(zip(starts, outs)):
-        rows = pl.ds(start if masked else pl.multiple_of(start, 8), HALO)
-        copies.append(
-            pltpu.make_async_copy(speed.at[:, rows, :], out.at[0:levels], sems.at[4 * n])
-        )
-        for m, plane in enumerate((thick, bed, fric)):
-            copies.append(
-                pltpu.make_async_copy(
-                    plane.at[rows, :], out.at[levels + m], sems.at[4 * n + 1 + m]
-                )
-            )
-    for copy in copies:
-        copy.start()
-    for start, out in zip(starts, outs):
-        rows = pl.ds(start if masked else pl.multiple_of(start, 8), HALO)
-        out[levels + 3] = mask[rows, :].astype(F32)
-    for copy in copies:
-        copy.wait()
-
-
-def ice_edges(speed, thick, bed, fric, mask):
+def edge_rows(start, speed, thick, bed, fric, mask):
     levels, _, cols = speed.shape
-    masked = lax.axis_size("lat") != 2
-    count = 2 if masked else 1
-    return call(
-        functools.partial(edge_kernel, masked=masked),
-        "edge",
-        (pltpu.VMEM((levels + 4, HALO, cols), F32),) * count,
-        (speed, thick, bed, fric, mask),
-        [pltpu.SemaphoreType.DMA((4 * count,))],
-        [pl.BlockSpec(memory_space=pl.ANY)] * 4 + [vmem()],
-    )
+    rows = pl.ds(start if isinstance(start, int) else pl.multiple_of(start, 8), HALO)
+    parts = [speed[:, rows, :].reshape(levels * HALO, cols)]
+    for plane in (thick, bed, fric):
+        value = plane[rows, :]
+        high = value.astype(BF16).astype(F32)
+        parts += [high, value - high]
+    parts += [mask[rows, :].astype(F32), jnp.zeros((HALO, cols), F32)]
+    return jnp.concatenate(parts, 0).astype(BF16)
+
+
+def read_edge(halo, levels):
+    value = halo[...].astype(F32)
+    planes = [value[(levels + n) * HALO : (levels + n + 1) * HALO] for n in range(7)]
+    four = [planes[2 * n] + planes[2 * n + 1] for n in range(3)] + [planes[6]]
+    return value[: levels * HALO].reshape(levels, HALO, value.shape[1]), four
 
 
 def ice_load_of(speed, thick, bed, fric, mask, halos):
@@ -254,7 +234,7 @@
         functools.partial(ice_kernel, masked=len(halos) != 1),
         "ice",
         pltpu.VMEM((own_rows, cols), BF16),
-        (speed, thick, bed, fric, mask, *keep(*halos)),
+        (*leave(speed, thick, bed, fric, mask), *keep(*halos)),
         [
             pltpu.VMEM((levels, window + 2 * HALO, cols), F32),
             pltpu.VMEM((5, window + 2 * HALO, cols), F32),
@@ -326,11 +306,14 @@
             pltpu.VMEM((32 * COMPS, 3 * (3 * VEC + PAIR)), BF16),
             pltpu.VMEM((8, 128), F32),
         ),
-        (matrix, *tables),
-    )
-
-
-def pack_kernel(disp, shear, visc, index, weight, low, high, TS, *, map_rows):
+        leave(matrix, *tables),
+    )
+
+
+def pack_kernel(*refs, map_rows, masked):
+    ice, (disp, shear, visc, index, weight) = refs[:5], refs[5:10]
+    low, high = refs[10:12]
+    edges, TS = refs[12:-1], refs[-1]
     layers = shear.shape[0]
     count = COMPS * layers
     spot = index[...]
@@ -346,6 +329,12 @@
             out[count + k] = shear[k, rows]
             out[count + layers + k] = visc[k, rows]
         out[count + 2 * layers, :, 0:8] = table[rows]
+    top = ice[0].shape[1] - HALO
+    if masked:
+        edges[0][...] = edge_rows(0, *ice)
+        edges[1][...] = edge_rows(top, *ice)
+    else:
+        edges[0][...] = edge_rows(jnp.where(lax.axis_index("lat") == 0, top, 0), *ice)
 
 
 def region_kernel(north, low, high, south, out):
@@ -692,7 +681,24 @@
     planes = COMPS * rad_layers + 2 * rad_layers + 1
     ice_args = (speed_guess, ice_thickness, bed_elevation, basal_friction, ice_mask)
 
-    edges = ice_edges(*ice_args)
+    levels = speed_guess.shape[0]
+    low, high, *edges = call(
+        functools.partial(pack_kernel, map_rows=tile_rows * lats, masked=lats != 2),
+        "pack",
+        (pltpu.VMEM((planes, HALO, width), F32),) * 2
+        + (pltpu.VMEM(((levels + 8) * HALO, map_cols), BF16),) * (1 if lats == 2 else 2),
+        leave(
+            *ice_args,
+            displacement_prev,
+            shear_modulus,
+            viscosity,
+            regrid_index[:, 0].T,
+            regrid_weight[:, 0].T,
+        ),
+        [pltpu.VMEM((8, 128), F32)],
+    )
+    north = lax.ppermute(high, "group", [(i, (i + 1) % groups) for i in range(groups)])
+    south = lax.ppermute(low, "group", [(i, (i - 1) % groups) for i in range(groups)])
     if lats == 2:
         halos = [lax.ppermute(edges[0], "lat", [(0, 1), (1, 0)])]
     else:
@@ -700,22 +706,8 @@
             lax.ppermute(edges[1], "lat", [(i, i + 1) for i in range(lats - 1)]),
             lax.ppermute(edges[0], "lat", [(i + 1, i) for i in range(lats - 1)]),
         ]
-    low, high = call(
-        functools.partial(pack_kernel, map_rows=tile_rows * lats),
-        "pack",
-        (pltpu.VMEM((planes, HALO, width), F32),) * 2,
-        (
-            displacement_prev,
-            shear_modulus,
-            viscosity,
-            regrid_index[:, 0].T,
-            regrid_weight[:, 0].T,
-        ),
-        [pltpu.VMEM((8, 128), F32)],
-    )
-    north = lax.ppermute(high, "group", [(i, (i + 1) % groups) for i in range(groups)])
-    south = lax.ppermute(low, "group", [(i, (i - 1) % groups) for i in range(groups)])
     stencil, theta = stencil_of(element_matrix)
+    north, south, halos = lax.optimization_barrier((north, south, halos))
     region = call(
         region_kernel,
         "region",
@@ -723,13 +715,14 @@
         keep(north, low, high, south),
     )
     if lats == 2:
-        pieces = [region, lax.ppermute(region, "rad", [(0, 1), (1, 0)])]
-        region, halos = lax.optimization_barrier((region, halos))
-        pieces.append(lax.ppermute(region, "lat", [(0, 1), (1, 0)]))
-        pieces.append(lax.ppermute(pieces[2], "rad", [(0, 1), (1, 0)]))
+        far = lax.ppermute(region, "lat", [(0, 1), (1, 0)])
+        near = lax.ppermute(region, "rad", [(0, 1), (1, 0)])
+        ice_load = ice_load_of(*ice_args, halos)
+        far, ice_load = lax.optimization_barrier((far, ice_load))
+        pieces = [region, near, far, lax.ppermute(far, "rad", [(0, 1), (1, 0)])]
     else:
         pieces = [lax.all_gather(region, ("lat", "rad"))]
-    ice_load = ice_load_of(*ice_args, halos)
+        ice_load = ice_load_of(*ice_args, halos)
     if lats == 2:
         loads = [ice_load, lax.ppermute(ice_load, "lat", [(0, 1), (1, 0)])]
     else:

time: 50.4 us -> 40.6 us (0.81); the launches traced: 49.6 us -> 40.4 us
  local copies, waits for them, and re-layouts: 8.13 us -> 0.01 us
  waiting for transfers between devices: 19.2 us -> 14 us
  Pallas kernels: 8.81 us -> 11.8 us
  starting transfers between devices: 12.7 us -> 13.8 us
    unnamed x32 -> x2, local copies, waits for them, and re-layouts: 8.13 us -> 0.01 us
    ppermute x3, waiting for transfers between devices: 5.12 us -> 0.62 us  [the longest x1 0.62 us: per_device(): far = lax.ppermute(region, 'lat', [(0, 1), (1, 0)])]
    pallas_call x8 -> x7, Pallas kernels: 8.81 us -> 11.8 us  [call(): pl.pallas_call(body, out_shape=out, in_specs=specs or [vmem()] * len(inpu...]
    ppermute x1, starting transfers between devices: 0.44 us -> 1.62 us  [per_device(): loads = [ice_load, lax.ppermute(ice_load, 'lat', [(0, 1), (1, 0)])]]
    ppermute x1, waiting for transfers between devices: 0.63 us -> 0.01 us  [per_device(): loads = [ice_load, lax.ppermute(ice_load, 'lat', [(0, 1), (1, 0)])]]
  transfers between devices with their start and end apart: 10 -> 10, of which waited for: 6 -> 5; matrix products, arithmetic and copies ran while one was open for 0% -> 0% of each run, Pallas kernels for 11% -> 18%
where the time goes in v3:
time: 40.6 us; the launch traced here: 40.4 us
  waiting for transfers between devices  14 us (34%)
  starting transfers between devices  13.8 us (34%)
  Pallas kernels  11.8 us (29%)
  between operations  0.71 us (2%)
    pallas_call x7, Pallas kernels, call(): pl.pallas_call(body, out_shape=out, in_specs=specs or [vmem()] * len(inpu...  11.8 us
    ppermute x3, waiting for transfers between devices, per_device(): lax.ppermute(payload, 'group', [(i, i ^ step) for i in range(groups)])  11.4 us
    ppermute x3, starting transfers between devices, per_device(): lax.ppermute(payload, 'group', [(i, i ^ step) for i in range(groups)])  4.08 us
    ppermute x1, starting transfers between devices, per_device(): lax.ppermute(low, 'group', [(i, (i - 1) % groups) for i in range(groups)])  3.2 us
    ppermute x1, starting transfers between devices, per_device(): halos = [lax.ppermute(edges[0], 'lat', [(0, 1), (1, 0)])]  2.97 us
    ppermute x1, waiting for transfers between devices, per_device(): lax.ppermute(high, 'group', [(i, (i + 1) % groups) for i in range(groups)])  2.02 us
    ppermute x1, starting transfers between devices, per_device(): loads = [ice_load, lax.ppermute(ice_load, 'lat', [(0, 1), (1, 0)])]  1.62 us
    ppermute x1, starting transfers between devices, per_device(): lax.ppermute(high, 'group', [(i, (i + 1) % groups) for i in range(groups)])  1.52 us
  transfers between devices with their start and end apart: 10, of which 5 were waited for; matrix products, arithmetic and copies ran while one was open for 0% of the time, Pallas kernels for 18%

profile of v3, /device:TPU:0, one launch (start us, length us, event | category | flops | bytes accessed | tf_op | source)
XLA Modules:
  0.0 40.4 jit_solution(15060466409450754186)
XLA Ops:
  0.6 1.1 %pack.1 = (f32[11,8,128]{2,1,0:T(8,128)S(1)}, f32[11,8,128]{2,1,0:T(8,128)S(1)}, bf16[192,256]{1,0:T(8,128)(2,1)S(1)}) custom-call(f32[16,16,256]{2,1,0:T(8,128)} %refs_0_.3, f32[16,256]{1,0:T(8,128)} %refs_1_.3, f32[16,256]{1,0:T(8,128)} %bed.1, f32[16,256]{1,0:T(8,128)} %refs_3_.3, s32[16,256]{1,0:T(8,128)} %refs_4_.3, f32[3,2,16,128]{3,2,1,0:T(8,128)} %refs_5_.1, ...), custom_call_target="tpu_custom_call" | custom-call | tf_op jit(solution)/shard_map/pack/pallas_call | solution.py:42
  1.8 3.0 %collective-permute-start.2 = (bf16[192,256]{1,0:T(8,128)(2,1)S(1)}, bf16[192,256]{1,0:T(8,128)(2,1)S(1)}, u32[]{:S(2)}, u32[]{:S(2)}) collective-permute-start(bf16[192,256]{1,0:T(8,128)(2,1)S(1)} %get-tuple-element.21), channel_id=1, source_target_pairs={{0,2},{2,0},{1,3},{3,1},{4,6},{6,4},{5,7},{7,5},{8,10},{10,8},{9,1... | collective-permute-start | bytes 294920 | tf_op jit(solution)/shard_map/ppermute | solution.py:703
  4.7 1.5 %collective-permute-start = (f32[11,8,128]{2,1,0:T(8,128)S(1)}, f32[11,8,128]{2,1,0:T(8,128)S(1)}, u32[]{:S(2)}, u32[]{:S(2)}) collective-permute-start(f32[11,8,128]{2,1,0:T(8,128)S(1)} %get-tuple-element.19.high), channel_id=1, source_target_pairs={{0,4},{4,8},{8,12},{12,16},{16,20},{20,24},{24,28},{28,0},{1,5},{5... | collective-permute-start | bytes 135176 | tf_op jit(solution)/shard_map/ppermute | solution.py:700
  6.3 3.2 %collective-permute-start.1 = (f32[11,8,128]{2,1,0:T(8,128)S(1)}, f32[11,8,128]{2,1,0:T(8,128)S(1)}, u32[]{:S(2)}, u32[]{:S(2)}) collective-permute-start(f32[11,8,128]{2,1,0:T(8,128)S(1)} %get-tuple-element.20.low), channel_id=1, source_target_pairs={{0,28},{4,0},{8,4},{12,8},{16,12},{20,16},{24,20},{28,24},{1,29},{... | collective-permute-start | bytes 135176 | tf_op jit(solution)/shard_map/ppermute | solution.py:701
  9.5 2.0 %collective-permute-done.north = f32[11,8,128]{2,1,0:T(8,128)S(1)} collective-permute-done((f32[11,8,128]{2,1,0:T(8,128)S(1)}, f32[11,8,128]{2,1,0:T(8,128)S(1)}, u32[]{:S(2)}, u32[]{:S(2)}) %collective-permute-start) | collective-permute-done | bytes 45088 | tf_op jit(solution)/shard_map/ppermute | solution.py:700
  11.5 0.0 collective-permute-done.1.south
  11.5 0.0 collective-permute-done.2.refs_5_
  11.5 0.4 %collective-permute-start.3 = (f32[11,32,128]{2,1,0:T(8,128)S(1)}, f32[11,32,128]{2,1,0:T(8,128)S(1)}, u32[]{:S(2)}, u32[]{:S(2)}) collective-permute-start(f32[11,32,128]{2,1,0:T(8,128)S(1)} %region.1.refs_0_), channel_id=1, source_target_pairs={{0,2},{2,0},{1,3},{3,1},{4,6},{6,4},{5,7},{7,5},{8,10},{10,8},{9,1... | collective-permute-start | bytes 540680 | tf_op jit(solution)/shard_map/ppermute | solution.py:718
  11.9 0.0 collective-permute-start.5
  12.0 4.5 %ice.1.refs_0_ = bf16[16,256]{1,0:T(8,128)(2,1)S(1)} custom-call(f32[16,16,256]{2,1,0:T(8,128)} %refs_0_.3, f32[16,256]{1,0:T(8,128)} %refs_1_.3, f32[16,256]{1,0:T(8,128)} %bed.1, f32[16,256]{1,0:T(8,128)} %refs_3_.3, s32[16,256]{1,0:T(8,128)} %refs_4_.3, bf16[192,256]{1,0:T(8,128)(2,1)S(1)} %collective-permute-done.2.refs_5_), custom_call_target="tpu_custom_call" | custom-call | tf_op jit(solution)/shard_map/ice/pallas_call | solution.py:42
  16.5 0.6 %collective-permute-done.3.refs_2_ = f32[11,32,128]{2,1,0:T(8,128)S(1)} collective-permute-done((f32[11,32,128]{2,1,0:T(8,128)S(1)}, f32[11,32,128]{2,1,0:T(8,128)S(1)}, u32[]{:S(2)}, u32[]{:S(2)}) %collective-permute-start.3) | collective-permute-done | bytes 180256 | tf_op jit(solution)/shard_map/ppermute | solution.py:718
  17.1 0.0 collective-permute-start.6
  17.1 1.6 %collective-permute-start.4 = (bf16[16,256]{1,0:T(8,128)(2,1)S(1)}, bf16[16,256]{1,0:T(8,128)(2,1)S(1)}, u32[]{:S(2)}, u32[]{:S(2)}) collective-permute-start(bf16[16,256]{1,0:T(8,128)(2,1)S(1)} %ice.1.refs_0_), channel_id=1, source_target_pairs={{0,2},{2,0},{1,3},{3,1},{4,6},{6,4},{5,7},{7,5},{8,10},{10,8},{9,1... | collective-permute-start | bytes 24584 | tf_op jit(solution)/shard_map/ppermute | solution.py:727
  18.7 1.6 %stencil.1 = (bf16[96,240]{1,0:T(8,128)(2,1)S(1)}, f32[8,128]{1,0:T(8,128)S(1)}) custom-call(f32[24,24]{1,0:T(8,128)} %matrix.1, f32[96,24]{1,0:T(8,128)} %constant.6.clone.pick_row, f32[4,24,72]{2,1,0:T(8,128)} %constant.7.clone.pick_col, f32[4,96,72]{2,1,0:T(8,128)} %constant.8.clone.keep), custom_call_target="tpu_custom_call" | custom-call | tf_op jit(solution)/shard_map/stencil/pallas_call | solution.py:42
  20.3 0.0 collective-permute-done.5.refs_1_
  20.3 0.0 collective-permute-done.6.refs_3_
  20.3 1.3 %relax.1 = (f32[792,256]{1,0:T(8,128)S(1)}, f32[1056,256]{1,0:T(8,128)S(1)}, f32[192,256]{1,0:T(8,128)S(1)}, bf16[2,32,192]{2,1,0:T(8,128)(2,1)S(1)}, f32[128,128]{1,0:T(8,128)S(1)}) custom-call(f32[11,32,128]{2,1,0:T(8,128)S(1)} %region.1.refs_0_, f32[11,32,128]{2,1,0:T(8,128)S(1)} %collective-permute-done.5.refs_1_, ...), custom_call_target="tpu_custom_call" | custom-call | tf_op jit(solution)/shard_map/relax/pallas_call | solution.py:42
  21.6 0.0 collective-permute-done.4.refs_1_
  21.6 0.0 copy-start
  21.6 2.4 %krylov.1 = (f32[168,128]{1,0:T(8,128)S(1)}, f32[5,192,128]{2,1,0:T(8,128)S(1)}) custom-call(bf16[16,256]{1,0:T(8,128)(2,1)S(1)} %ice.1.refs_0_, bf16[16,256]{1,0:T(8,128)(2,1)S(1)} %collective-permute-done.4.refs_1_, bf16[96,240]{1,0:T(8,128)(2,1)S(1)} %get-tuple-element.26.refs_4_.refs_2_, f32[792,256]{1,0:T(8,128)S(1)} %get-tuple-element.29.refs_3_, ...), custom_call_target="tpu_custom_call" | custom-call | tf_op jit(solution)/shard_map/krylov/pallas_call | solution.py:42
  24.0 1.3 %collective-permute-start.7 = (f32[168,128]{1,0:T(8,128)S(1)}, f32[168,128]{1,0:T(8,128)S(1)}, u32[]{:S(2)}, u32[]{:S(2)}) collective-permute-start(f32[168,128]{1,0:T(8,128)S(1)} %get-tuple-element.34), channel_id=1, source_target_pairs={{0,4},{4,0},{8,12},{12,8},{16,20},{20,16},{24,28},{28,24},{1,5},{5... | collective-permute-start | bytes 258056 | tf_op jit(solution)/shard_map/ppermute | solution.py:766
  25.3 3.3 %collective-permute-done.7 = f32[168,128]{1,0:T(8,128)S(1)} collective-permute-done((f32[168,128]{1,0:T(8,128)S(1)}, f32[168,128]{1,0:T(8,128)S(1)}, u32[]{:S(2)}, u32[]{:S(2)}) %collective-permute-start.7) | collective-permute-done | bytes 86048 | tf_op jit(solution)/shard_map/ppermute | solution.py:766
  28.6 0.9 %collective-permute-start.8 = (f32[168,128]{1,0:T(8,128)S(1)}, f32[168,128]{1,0:T(8,128)S(1)}, u32[]{:S(2)}, u32[]{:S(2)}) collective-permute-start(f32[168,128]{1,0:T(8,128)S(1)} %add.9), channel_id=1, source_target_pairs={{0,8},{4,12},{8,0},{12,4},{16,24},{20,28},{24,16},{28,20},{1,9},{5... | collective-permute-start | bytes 258056 | tf_op jit(solution)/shard_map/ppermute | solution.py:766
  29.5 3.7 %collective-permute-done.8 = f32[168,128]{1,0:T(8,128)S(1)} collective-permute-done((f32[168,128]{1,0:T(8,128)S(1)}, f32[168,128]{1,0:T(8,128)S(1)}, u32[]{:S(2)}, u32[]{:S(2)}) %collective-permute-start.8) | collective-permute-done | bytes 86048 | tf_op jit(solution)/shard_map/ppermute | solution.py:766
  33.1 1.9 %collective-permute-start.9 = (f32[168,128]{1,0:T(8,128)S(1)}, f32[168,128]{1,0:T(8,128)S(1)}, u32[]{:S(2)}, u32[]{:S(2)}) collective-permute-start(f32[168,128]{1,0:T(8,128)S(1)} %add.10), channel_id=1, source_target_pairs={{0,16},{4,20},{8,24},{12,28},{16,0},{20,4},{24,8},{28,12},{1,17},{... | collective-permute-start | bytes 258056 | tf_op jit(solution)/shard_map/ppermute | solution.py:766
  35.0 4.5 %collective-permute-done.9 = f32[168,128]{1,0:T(8,128)S(1)} collective-permute-done((f32[168,128]{1,0:T(8,128)S(1)}, f32[168,128]{1,0:T(8,128)S(1)}, u32[]{:S(2)}, u32[]{:S(2)}) %collective-permute-start.9) | collective-permute-done | bytes 86048 | tf_op jit(solution)/shard_map/ppermute | solution.py:766
  39.5 0.0 copy-done
  39.5 0.9 %finish.1 = (f32[3,2,16,128]{3,2,1,0:T(8,128)}, f32[16,256]{1,0:T(8,128)}) custom-call(f32[168,128]{1,0:T(8,128)S(1)} %add.11.payload, f32[8,128]{1,0:T(8,128)S(1)} %get-tuple-element.28.refs_5_.theta, f32[5,192,128]{2,1,0:T(8,128)S(1)} %get-tuple-element.35.v, f32[16,256]{1,0:T(8,128)S(1)} %copy-done), custom_call_target="tpu_custom_call" | custom-call | tf_op jit(solution)/shard_map/finish/pallas_call | solution.py:42
  (4 shorter events, 0.0 us)
Async XLA Ops:
  1.8 9.7 %collective-permute-start.2 = (bf16[192,256]{1,0:T(8,128)(2,1)S(1)}, bf16[192,256]{1,0:T(8,128)(2,1)S(1)}, u32[]{:S(2)}, u32[]{:S(2)}) collective-permute-start(bf16[192,256]{1,0:T(8,128)(2,1)S(1)} %get-tuple-element.21), channel_id=1, source_target_pairs={{0,2},{2,0},{1,3},{3,1},{4,6},{6,4},{5,7},{7,5},{8,10},{10,8},{9,1... | collective-permute-start | bytes 294920 | tf_op jit(solution)/shard_map/ppermute | solution.py:703
  4.7 6.7 %collective-permute-start = (f32[11,8,128]{2,1,0:T(8,128)S(1)}, f32[11,8,128]{2,1,0:T(8,128)S(1)}, u32[]{:S(2)}, u32[]{:S(2)}) collective-permute-start(f32[11,8,128]{2,1,0:T(8,128)S(1)} %get-tuple-element.19.high), channel_id=1, source_target_pairs={{0,4},{4,8},{8,12},{12,16},{16,20},{20,24},{24,28},{28,0},{1,5},{5... | collective-permute-start | bytes 135176 | tf_op jit(solution)/shard_map/ppermute | solution.py:700
  6.3 5.2 %collective-permute-start.1 = (f32[11,8,128]{2,1,0:T(8,128)S(1)}, f32[11,8,128]{2,1,0:T(8,128)S(1)}, u32[]{:S(2)}, u32[]{:S(2)}) collective-permute-start(f32[11,8,128]{2,1,0:T(8,128)S(1)} %get-tuple-element.20.low), channel_id=1, source_target_pairs={{0,28},{4,0},{8,4},{12,8},{16,12},{20,16},{24,20},{28,24},{1,29},{... | collective-permute-start | bytes 135176 | tf_op jit(solution)/shard_map/ppermute | solution.py:701
  11.5 5.6 %collective-permute-start.3 = (f32[11,32,128]{2,1,0:T(8,128)S(1)}, f32[11,32,128]{2,1,0:T(8,128)S(1)}, u32[]{:S(2)}, u32[]{:S(2)}) collective-permute-start(f32[11,32,128]{2,1,0:T(8,128)S(1)} %region.1.refs_0_), channel_id=1, source_target_pairs={{0,2},{2,0},{1,3},{3,1},{4,6},{6,4},{5,7},{7,5},{8,10},{10,8},{9,1... | collective-permute-start | bytes 540680 | tf_op jit(solution)/shard_map/ppermute | solution.py:718
  11.9 8.3 %collective-permute-start.5 = (f32[11,32,128]{2,1,0:T(8,128)S(1)}, f32[11,32,128]{2,1,0:T(8,128)S(1)}, u32[]{:S(2)}, u32[]{:S(2)}) collective-permute-start(f32[11,32,128]{2,1,0:T(8,128)S(1)} %region.1.refs_0_), channel_id=1, source_target_pairs={{0,1},{1,0},{2,3},{3,2},{4,5},{5,4},{6,7},{7,6},{8,9},{9,8},{10,11... | collective-permute-start | bytes 540680 | tf_op jit(solution)/shard_map/ppermute | solution.py:719
  17.1 3.2 %collective-permute-start.6 = (f32[11,32,128]{2,1,0:T(8,128)S(1)}, f32[11,32,128]{2,1,0:T(8,128)S(1)}, u32[]{:S(2)}, u32[]{:S(2)}) collective-permute-start(f32[11,32,128]{2,1,0:T(8,128)S(1)} %collective-permute-done.3.refs_2_), channel_id=1, source_target_pairs={{0,1},{1,0},{2,3},{3,2},{4,5},{5,4},{6,7},{7,6},{8,9},{9,8},{10,11... | collective-permute-start | bytes 540680 | tf_op jit(solution)/shard_map/ppermute | solution.py:722
  17.1 4.6 %collective-permute-start.4 = (bf16[16,256]{1,0:T(8,128)(2,1)S(1)}, bf16[16,256]{1,0:T(8,128)(2,1)S(1)}, u32[]{:S(2)}, u32[]{:S(2)}) collective-permute-start(bf16[16,256]{1,0:T(8,128)(2,1)S(1)} %ice.1.refs_0_), channel_id=1, source_target_pairs={{0,2},{2,0},{1,3},{3,1},{4,6},{6,4},{5,7},{7,5},{8,10},{10,8},{9,1... | collective-permute-start | bytes 24584 | tf_op jit(solution)/shard_map/ppermute | solution.py:727
  21.6 17.9 %copy-start = (f32[16,256]{1,0:T(8,128)S(1)}, f32[16,256]{1,0:T(8,128)}, u32[]{:S(2)}) copy-start(f32[16,256]{1,0:T(8,128)} %bed.1) | copy-start | bytes 49156
  24.0 4.6 %collective-permute-start.7 = (f32[168,128]{1,0:T(8,128)S(1)}, f32[168,128]{1,0:T(8,128)S(1)}, u32[]{:S(2)}, u32[]{:S(2)}) collective-permute-start(f32[168,128]{1,0:T(8,128)S(1)} %get-tuple-element.34), channel_id=1, source_target_pairs={{0,4},{4,0},{8,12},{12,8},{16,20},{20,16},{24,28},{28,24},{1,5},{5... | collective-permute-start | bytes 258056 | tf_op jit(solution)/shard_map/ppermute | solution.py:766
  28.6 4.6 %collective-permute-start.8 = (f32[168,128]{1,0:T(8,128)S(1)}, f32[168,128]{1,0:T(8,128)S(1)}, u32[]{:S(2)}, u32[]{:S(2)}) collective-permute-start(f32[168,128]{1,0:T(8,128)S(1)} %add.9), channel_id=1, source_target_pairs={{0,8},{4,12},{8,0},{12,4},{16,24},{20,28},{24,16},{28,20},{1,9},{5... | collective-permute-start | bytes 258056 | tf_op jit(solution)/shard_map/ppermute | solution.py:766
  33.1 6.4 %collective-permute-start.9 = (f32[168,128]{1,0:T(8,128)S(1)}, f32[168,128]{1,0:T(8,128)S(1)}, u32[]{:S(2)}, u32[]{:S(2)}) collective-permute-start(f32[168,128]{1,0:T(8,128)S(1)} %add.10), channel_id=1, source_target_pairs={{0,16},{4,20},{8,24},{12,28},{16,0},{20,4},{24,8},{28,12},{1,17},{... | collective-permute-start | bytes 258056 | tf_op jit(solution)/shard_map/ppermute | solution.py:766

commit v4 on v3

--- a/solution.py
+++ b/solution.py
@@ -37,7 +37,7 @@
     return [pltpu.with_memory_space_constraint(a, pltpu.HBM) for a in arrays]
 
 
-def call(body, name, out, inputs, scratch=(), specs=None):
+def call(body, out, inputs, scratch=(), specs=None):
     lats = lax.axis_size("lat")
     return pl.pallas_call(
         body,
@@ -46,7 +46,6 @@
         out_specs=jax.tree.map(lambda _: vmem(), out),
         scratch_shapes=list(scratch),
         compiler_params=pltpu.CompilerParams(vmem_limit_bytes=(8 if lats == 2 else 40) << 20),
-        name=name,
     )(*inputs)
 
 
@@ -69,7 +68,6 @@
     levels, own_rows, cols = speed.shape
     lat = lax.axis_index("lat")
     window = ST.shape[1]
-    planes = (thick, bed, fric, mask)
     S[:, 0:HALO, :] = jnp.zeros((levels, HALO, cols), F32)
     S[:, HALO + window :, :] = jnp.zeros((levels, HALO, cols), F32)
     PL[:, 0:HALO, :] = jnp.zeros((5, HALO, cols), F32)
@@ -81,7 +79,7 @@
         for n in range(4):
             PL[n, rows, :] = four[n]
 
-    own_four = [thick[...], bed[...], fric[...], mask[...].astype(F32)]
+    own_four = [thick[...], bed[...], fric[...], mask[...]]
     if masked:
         own_at = HALO
         place(own_at, speed[...], own_four)
@@ -159,7 +157,7 @@
                     (north + south) + (east + west)
                 )
         scale = [(0.5 * ASPECT) * inverse_of(t) * inverse_of(t) for t in tiles]
-        upper, value, vertical, stiff, rest = {}, {}, {}, {}, {}
+        value, vertical, stiff, rest = {}, {}, {}, {}
         for k in range(levels):
             for t in tiles:
                 rows = slice(8 * t, 8 * t + 8)
@@ -232,9 +230,8 @@
     window = own_rows + HALO * (1 if len(halos) == 1 else 2)
     return call(
         functools.partial(ice_kernel, masked=len(halos) != 1),
-        "ice",
         pltpu.VMEM((own_rows, cols), BF16),
-        (*leave(speed, thick, bed, fric, mask), *keep(*halos)),
+        keep(speed, thick, bed, fric, mask, *halos),
         [
             pltpu.VMEM((levels, window + 2 * HALO, cols), F32),
             pltpu.VMEM((5, window + 2 * HALO, cols), F32),
@@ -301,7 +298,6 @@
     tables = [jnp.asarray(t) for t in stencil_tables()]
     return call(
         stencil_kernel,
-        "stencil",
         (
             pltpu.VMEM((32 * COMPS, 3 * (3 * VEC + PAIR)), BF16),
             pltpu.VMEM((8, 128), F32),
@@ -313,7 +309,10 @@
 def pack_kernel(*refs, map_rows, masked):
     ice, (disp, shear, visc, index, weight) = refs[:5], refs[5:10]
     low, high = refs[10:12]
-    edges, TS = refs[12:-1], refs[-1]
+    copies = refs[12:17]
+    edges, TS = refs[17:-1], refs[-1]
+    for source, copy in zip(ice, copies):
+        copy[...] = source[...].astype(F32)
     layers = shear.shape[0]
     count = COMPS * layers
     spot = index[...]
@@ -337,8 +336,9 @@
         edges[0][...] = edge_rows(jnp.where(lax.axis_index("lat") == 0, top, 0), *ice)
 
 
-def region_kernel(north, low, high, south, out):
-    for n, piece in enumerate((north, low, high, south)):
+def region_kernel(*pieces):
+    out = pieces[-1]
+    for n, piece in enumerate(pieces[:-1]):
         out[:, n * HALO : (n + 1) * HALO] = piece[...]
 
 
@@ -402,7 +402,7 @@
     XP, CR, XS, SH, VI = refs[pieces + 7 :]
     group, lat, rad = (lax.axis_index(n) for n in ("group", "lat", "rad"))
     lat_count = lax.axis_size("lat")
-    rows, width = E[0].shape[-2:]
+    rows, _ = E[0].shape[-2:]
     own_rows = rows - 2 * HALO
     cols = XP.shape[1]
     rad_layers = LAYERS // 2
@@ -434,8 +434,7 @@
     mask = domain_of(own_rows, cols)
     layer8 = iota((PAIR, cols), 0) % LAYERS
     top_layer, last_layer = layer8 == 0, layer8 == LAYERS - 1
-    shrink = 1.0 / theta[0:1, 0:1]
-    eighth = 0.125 * shrink
+    eighth = jnp.concatenate([0.125 / theta[...]] * (cols // 128), 1)
 
     def corner_means(nodal, scale):
         both = nodal + pltpu.roll(nodal, LAYERS, 0)
@@ -489,7 +488,8 @@
             right = index[own] >= map_rows
             near = index[own] - jnp.where(right, map_rows, 0) - (lat * tile_rows).astype(F32)
             here = jnp.logical_and(near >= 0, near < tile_rows)
-            spot = jnp.where(here, near + jnp.where(right, tile_rows, 0), -1.0)
+            mine = jnp.where(right, 1.0, 0.0) == rad.astype(F32)
+            spot = jnp.where(jnp.logical_and(here, mine), near, -1.0)
             lift = lift + jnp.where(own_spots == spot, weight[own], 0.0)
         loads = loads * scale
         high = loads.astype(BF16).astype(F32)
@@ -566,7 +566,7 @@
     fields = jnp.concatenate(fields, 0)
     spots = (payload.shape[0] - 2 * ITERS) // (ITERS + 1)
     lift = lax.dot_general(
-        ut[...],
+        ut[:, :spots],
         fields,
         (((0,), (0,)), ((), ())),
         precision=lax.Precision.HIGHEST,
@@ -574,7 +574,7 @@
     )
     for n in range(ITERS + 1):
         payload[2 * ITERS + n * spots : 2 * ITERS + (n + 1) * spots] = lift[
-            :spots, n * width : (n + 1) * width
+            :, n * width : (n + 1) * width
         ]
     own = pl.ds(pl.multiple_of(lat * width, 128), width)
     for n in range(ITERS):
@@ -583,8 +583,7 @@
     v_out[ITERS] = x_own[:, own]
 
 
-def finish_kernel(payload, theta, v, bed, disp_out, bed_out, X):
-    rad = lax.axis_index("rad")
+def scalar_kernel(payload, theta, gamma, lift_out):
     moment = [
         jnp.broadcast_to(jnp.sum(payload[k : k + 1], 1, keepdims=True), (8, 128))
         for k in range(2 * ITERS)
@@ -635,11 +634,23 @@
             for i, a in enumerate(residual)
         ]
         norm = jnp.where(live, fresh, 1.0)
-    raw = [a[0:1] for a in answer]
-    answer = [a / theta[0:1] for a in raw]
+    answer = [a / theta[...] for a in answer]
+    for n in range(ITERS):
+        gamma[n * 8 : (n + 1) * 8] = answer[n]
+    rows = lift_out.shape[0]
+    base = 2 * ITERS
+    lift = payload[base : base + rows]
+    for n in range(ITERS):
+        first = base + (n + 1) * rows
+        lift = lift + answer[n][0:1] * payload[first : first + rows]
+    lift_out[...] = lift
+
+
+def finish_kernel(gamma, v, disp_out, X):
+    rad = lax.axis_index("rad")
     total = v[ITERS]
     for n in range(ITERS):
-        total = total + answer[n] * v[n]
+        total = total + gamma[n * 8 : n * 8 + 1] * v[n]
     X[...] = total
     layers = disp_out.shape[1]
     pairs = disp_out.shape[2] // 2
@@ -649,15 +660,15 @@
                 lower = X[pl.ds(c * PAIR + q * LAYERS + k, pairs, VEC), :]
                 upper = X[pl.ds(c * PAIR + q * LAYERS + layers + k, pairs, VEC), :]
                 disp_out[c, k, pl.ds(q, pairs, 2), :] = jnp.where(rad == 0, lower, upper)
-    rows, cols = bed.shape
-    spots = 2 * rows
-    base = 2 * ITERS
-    lift = payload[base : base + spots]
-    for n in range(ITERS):
-        lift = lift + answer[n] * payload[base + (n + 1) * spots : base + (n + 2) * spots]
+
+
+def bed_kernel(own, other, bed, bed_out):
+    rad = lax.axis_index("rad")
+    half = bed.shape[1] // 2
     for h in range(2):
-        lanes = slice(h * cols // 2, (h + 1) * cols // 2)
-        bed_out[:, lanes] = bed[:, lanes] + UPLIFT_SCALE * lift[h * rows : (h + 1) * rows]
+        lanes = slice(h * half, (h + 1) * half)
+        lift = jnp.where(rad == h, own[...], other[...])
+        bed_out[:, lanes] = bed[:, lanes] + UPLIFT_SCALE * lift
 
 
 def per_device(
@@ -682,10 +693,11 @@
     ice_args = (speed_guess, ice_thickness, bed_elevation, basal_friction, ice_mask)
 
     levels = speed_guess.shape[0]
-    low, high, *edges = call(
+    low, high, *kept = call(
         functools.partial(pack_kernel, map_rows=tile_rows * lats, masked=lats != 2),
-        "pack",
         (pltpu.VMEM((planes, HALO, width), F32),) * 2
+        + (pltpu.VMEM(speed_guess.shape, F32),)
+        + (pltpu.VMEM((tile_rows, map_cols), F32),) * 4
         + (pltpu.VMEM(((levels + 8) * HALO, map_cols), BF16),) * (1 if lats == 2 else 2),
         leave(
             *ice_args,
@@ -697,6 +709,8 @@
         ),
         [pltpu.VMEM((8, 128), F32)],
     )
+    ice_args, edges = kept[:5], kept[5:]
+    bed_kept = ice_args[2]
     north = lax.ppermute(high, "group", [(i, (i + 1) % groups) for i in range(groups)])
     south = lax.ppermute(low, "group", [(i, (i - 1) % groups) for i in range(groups)])
     if lats == 2:
@@ -707,18 +721,20 @@
             lax.ppermute(edges[0], "lat", [(i + 1, i) for i in range(lats - 1)]),
         ]
     stencil, theta = stencil_of(element_matrix)
-    north, south, halos = lax.optimization_barrier((north, south, halos))
+    north, south, halos, stencil, theta = lax.optimization_barrier(
+        (north, south, halos, stencil, theta)
+    )
     region = call(
         region_kernel,
-        "region",
         pltpu.VMEM((planes, 2 * own_rows, width), F32),
         keep(north, low, high, south),
     )
     if lats == 2:
         far = lax.ppermute(region, "lat", [(0, 1), (1, 0)])
+        ice_load = ice_load_of(*ice_args, halos)
+        region, _ = lax.optimization_barrier((region, ice_load))
         near = lax.ppermute(region, "rad", [(0, 1), (1, 0)])
-        ice_load = ice_load_of(*ice_args, halos)
-        far, ice_load = lax.optimization_barrier((far, ice_load))
+        far, _ = lax.optimization_barrier((far, ice_load))
         pieces = [region, near, far, lax.ppermute(far, "rad", [(0, 1), (1, 0)])]
     else:
         pieces = [lax.all_gather(region, ("lat", "rad"))]
@@ -730,7 +746,6 @@
     pairs = own_rows // 2
     r_start, coefs, x_own, lw, ut = call(
         functools.partial(relax_kernel, pieces=len(pieces)),
-        "relax",
         (
             pltpu.VMEM((33 * VEC, cols), F32),
             pltpu.VMEM((33 * 4 * PAIR, cols), F32),
@@ -747,10 +762,9 @@
             pltpu.VMEM((lats, 33 * PAIR, width), F32),
         ],
     )
-    spots = 2 * tile_rows
+    spots = tile_rows
     payload, vectors = call(
         functools.partial(krylov_kernel, loads=len(loads)),
-        "krylov",
         (
             pltpu.VMEM((2 * ITERS + (ITERS + 1) * spots, width), F32),
             pltpu.VMEM((ITERS + 1, pairs * VEC, width), F32),
@@ -767,16 +781,24 @@
             payload, "group", [(i, i ^ step) for i in range(groups)]
         )
         step *= 2
-    return call(
+    gamma, lift = call(
+        scalar_kernel,
+        (pltpu.VMEM((8 * ITERS, 128), F32), pltpu.VMEM((tile_rows, width), F32)),
+        keep(payload, theta),
+    )
+    other = lax.ppermute(lift, "rad", [(0, 1), (1, 0)])
+    displacement = call(
         finish_kernel,
-        "finish",
-        (
-            jax.ShapeDtypeStruct((COMPS, rad_layers, own_rows, width), F32),
-            jax.ShapeDtypeStruct((tile_rows, map_cols), F32),
-        ),
-        (*keep(payload, theta, vectors), bed_elevation),
+        jax.ShapeDtypeStruct((COMPS, rad_layers, own_rows, width), F32),
+        keep(gamma, vectors),
         [pltpu.VMEM((pairs * VEC, width), F32)],
     )
+    bed_new = call(
+        bed_kernel,
+        jax.ShapeDtypeStruct((tile_rows, map_cols), F32),
+        keep(lift, other, bed_kept),
+    )
+    return displacement, bed_new
 
 
 def solution(mesh):
@@ -794,6 +816,7 @@
         P(None, "lat", None),
     )
     out_specs = (P(None, "rad", "group", "lat"), P("lat", None))
+
     return jax.shard_map(
         per_device, mesh=mesh, in_specs=in_specs, out_specs=out_specs, check_vma=False
     )

time: 40.6 us -> 38.9 us (0.958)
  starting transfers between devices: 13.8 us -> 12.9 us
  Pallas kernels: 11.8 us -> 11.3 us
    ppermute x3, waiting for transfers between devices: 11.4 us -> 9.68 us  [per_device(): lax.ppermute(payload, 'group', [(i, i ^ step) for i in range(groups)])]
    ppermute x1, waiting for transfers between devices: 2.02 us -> 0.43 us  [per_device(): lax.ppermute(high, 'group', [(i, (i + 1) % groups) for i in range(groups)])]
    ppermute x1, starting transfers between devices: 1.62 us -> 0.63 us  [per_device(): loads = [ice_load, lax.ppermute(ice_load, 'lat', [(0, 1), (1, 0)])]]
    ppermute x1, waiting for transfers between devices: 0.01 us -> 0.93 us  [per_device(): loads = [ice_load, lax.ppermute(ice_load, 'lat', [(0, 1), (1, 0)])]]
    ppermute x1, waiting for transfers between devices: 0.62 us -> 1.52 us  [per_device(): far = lax.ppermute(region, 'lat', [(0, 1), (1, 0)])]
    ppermute x1, waiting for transfers between devices: 0.01 us -> 0.78 us  [per_device(): pieces = [region, near, far, lax.ppermute(far, 'rad', [(0, 1), (1, 0)])]]
    ppermute x0 -> x1, waiting for transfers between devices: none -> 0.48 us  [per_device(): other = lax.ppermute(lift, 'rad', [(0, 1), (1, 0)])]
    pallas_call x7 -> x9, Pallas kernels: 11.8 us -> 11.3 us  [call(): pl.pallas_call(body, out_shape=out, in_specs=specs or [vmem()] * len(inpu...]
  transfers between devices with their start and end apart: 10 -> 11, of which waited for: 5 -> 8; matrix products, arithmetic and copies ran while one was open for 0% -> 0% of each run, Pallas kernels for 18% -> 18%
where the time goes in v4:
time: 38.9 us; the launch traced here: 38.8 us
  waiting for transfers between devices  13.8 us (35%)
  starting transfers between devices  12.9 us (33%)
  Pallas kernels  11.3 us (29%)
  between operations  0.68 us (2%)
    pallas_call x9, Pallas kernels, call(): pl.pallas_call(body, out_shape=out, in_specs=specs or [vmem()] * len(inpu...  11.3 us
    ppermute x3, waiting for transfers between devices, per_device(): lax.ppermute(payload, 'group', [(i, i ^ step) for i in range(groups)])  9.68 us
    ppermute x3, starting transfers between devices, per_device(): lax.ppermute(payload, 'group', [(i, i ^ step) for i in range(groups)])  3.96 us
    ppermute x1, starting transfers between devices, per_device(): lax.ppermute(low, 'group', [(i, (i - 1) % groups) for i in range(groups)])  3.2 us
    ppermute x1, starting transfers between devices, per_device(): halos = [lax.ppermute(edges[0], 'lat', [(0, 1), (1, 0)])]  2.99 us
    ppermute x1, waiting for transfers between devices, per_device(): far = lax.ppermute(region, 'lat', [(0, 1), (1, 0)])  1.52 us
    ppermute x1, starting transfers between devices, per_device(): lax.ppermute(high, 'group', [(i, (i + 1) % groups) for i in range(groups)])  1.52 us
    ppermute x1, waiting for transfers between devices, per_device(): loads = [ice_load, lax.ppermute(ice_load, 'lat', [(0, 1), (1, 0)])]  0.93 us
  transfers between devices with their start and end apart: 11, of which 8 were waited for; matrix products, arithmetic and copies ran while one was open for 0% of the time, Pallas kernels for 18%

profile of v4, /device:TPU:0, one launch (start us, length us, event | category | flops | bytes accessed | tf_op | source)
XLA Modules:
  0.0 38.8 jit_solution(13462925092693089837)
XLA Ops:
  0.6 1.2 %shard_map.149 = (f32[11,8,128]{2,1,0:T(8,128)S(1)}, f32[11,8,128]{2,1,0:T(8,128)S(1)}, f32[16,16,256]{2,1,0:T(8,128)S(1)}, f32[16,256]{1,0:T(8,128)S(1)}, f32[1...) custom-call(f32[16,16,256]{2,1,0:T(8,128)} %refs_0_.1, ...), custom_call_target="tpu_custom_call" | custom-call | tf_op jit(solution)/shard_map/pallas_call | solution.py:42
  1.8 3.0 %collective-permute-start.2 = (bf16[192,256]{1,0:T(8,128)(2,1)S(1)}, bf16[192,256]{1,0:T(8,128)(2,1)S(1)}, u32[]{:S(2)}, u32[]{:S(2)}) collective-permute-start(bf16[192,256]{1,0:T(8,128)(2,1)S(1)} %get-tuple-element.35), channel_id=1, source_target_pairs={{0,2},{2,0},{1,3},{3,1},{4,6},{6,4},{5,7},{7,5},{8,10},{10,8},{9,1... | collective-permute-start | bytes 294920 | tf_op jit(solution)/shard_map/ppermute | solution.py:717
  4.8 1.5 %collective-permute-start = (f32[11,8,128]{2,1,0:T(8,128)S(1)}, f32[11,8,128]{2,1,0:T(8,128)S(1)}, u32[]{:S(2)}, u32[]{:S(2)}) collective-permute-start(f32[11,8,128]{2,1,0:T(8,128)S(1)} %get-tuple-element.33.pieces_2_), channel_id=1, source_target_pairs={{0,4},{4,8},{8,12},{12,16},{16,20},{20,24},{24,28},{28,0},{1,5},{5... | collective-permute-start | bytes 135176 | tf_op jit(solution)/shard_map/ppermute | solution.py:714
  6.3 3.2 %collective-permute-start.1 = (f32[11,8,128]{2,1,0:T(8,128)S(1)}, f32[11,8,128]{2,1,0:T(8,128)S(1)}, u32[]{:S(2)}, u32[]{:S(2)}) collective-permute-start(f32[11,8,128]{2,1,0:T(8,128)S(1)} %get-tuple-element.34.pieces_1_), channel_id=1, source_target_pairs={{0,28},{4,0},{8,4},{12,8},{16,12},{20,16},{24,20},{28,24},{1,29},{... | collective-permute-start | bytes 135176 | tf_op jit(solution)/shard_map/ppermute | solution.py:715
  9.5 1.6 %shard_map.150 = (bf16[96,240]{1,0:T(8,128)(2,1)S(1)}, f32[8,128]{1,0:T(8,128)S(1)}) custom-call(f32[24,24]{1,0:T(8,128)} %matrix.1, f32[96,24]{1,0:T(8,128)} %constant.6.clone.pick_row, f32[4,24,72]{2,1,0:T(8,128)} %constant.7.clone.pick_col, f32[4,96,72]{2,1,0:T(8,128)} %constant.8.clone.keep), custom_call_target="tpu_custom_call" | custom-call | tf_op jit(solution)/shard_map/pallas_call | solution.py:42
  11.1 0.4 %collective-permute-done.pieces_0_ = f32[11,8,128]{2,1,0:T(8,128)S(1)} collective-permute-done((f32[11,8,128]{2,1,0:T(8,128)S(1)}, f32[11,8,128]{2,1,0:T(8,128)S(1)}, u32[]{:S(2)}, u32[]{:S(2)}) %collective-permute-start) | collective-permute-done | bytes 45088 | tf_op jit(solution)/shard_map/ppermute | solution.py:714
  11.5 0.0 collective-permute-done.1.pieces_3_
  11.5 0.0 collective-permute-done.2.refs_5_
  11.6 0.4 %collective-permute-start.5 = (f32[11,32,128]{2,1,0:T(8,128)S(1)}, f32[11,32,128]{2,1,0:T(8,128)S(1)}, u32[]{:S(2)}, u32[]{:S(2)}) collective-permute-start(f32[11,32,128]{2,1,0:T(8,128)S(1)} %shard_map.152.refs_0_), channel_id=1, source_target_pairs={{0,2},{2,0},{1,3},{3,1},{4,6},{6,4},{5,7},{7,5},{8,10},{10,8},{9,1... | collective-permute-start | bytes 540680 | tf_op jit(solution)/shard_map/ppermute | solution.py:733
  12.0 3.5 %shard_map.151.refs_0_ = bf16[16,256]{1,0:T(8,128)(2,1)S(1)} custom-call(f32[16,16,256]{2,1,0:T(8,128)S(1)} %get-tuple-element.28.refs_0_, f32[16,256]{1,0:T(8,128)S(1)} %get-tuple-element.29.refs_1_, f32[16,256]{1,0:T(8,128)S(1)} %get-tuple-element.30.refs_2_.bed, f32[16,256]{1,0:T(8,128)S(1)} %get-tuple-element.31.refs_3_, ...), custom_call_target="tpu_custom_call" | custom-call | tf_op jit(solution)/shard_map/pallas_call | solution.py:42
  15.5 0.1 collective-permute-start.4
  15.6 1.5 %collective-permute-done.5.refs_2_ = f32[11,32,128]{2,1,0:T(8,128)S(1)} collective-permute-done((f32[11,32,128]{2,1,0:T(8,128)S(1)}, f32[11,32,128]{2,1,0:T(8,128)S(1)}, u32[]{:S(2)}, u32[]{:S(2)}) %collective-permute-start.5) | collective-permute-done | bytes 180256 | tf_op jit(solution)/shard_map/ppermute | solution.py:733
  17.1 0.0 collective-permute-start.6
  17.1 0.6 %collective-permute-start.3 = (bf16[16,256]{1,0:T(8,128)(2,1)S(1)}, bf16[16,256]{1,0:T(8,128)(2,1)S(1)}, u32[]{:S(2)}, u32[]{:S(2)}) collective-permute-start(bf16[16,256]{1,0:T(8,128)(2,1)S(1)} %shard_map.151.refs_0_), channel_id=1, source_target_pairs={{0,2},{2,0},{1,3},{3,1},{4,6},{6,4},{5,7},{7,5},{8,10},{10,8},{9,1... | collective-permute-start | bytes 24584 | tf_op jit(solution)/shard_map/ppermute | solution.py:743
  17.8 0.0 collective-permute-done.4.refs_1_
  17.8 0.8 %collective-permute-done.6.refs_3_ = f32[11,32,128]{2,1,0:T(8,128)S(1)} collective-permute-done((f32[11,32,128]{2,1,0:T(8,128)S(1)}, f32[11,32,128]{2,1,0:T(8,128)S(1)}, u32[]{:S(2)}, u32[]{:S(2)}) %collective-permute-start.6) | collective-permute-done | bytes 180256 | tf_op jit(solution)/shard_map/ppermute | solution.py:738
  18.5 1.3 %shard_map.153 = (f32[792,256]{1,0:T(8,128)S(1)}, f32[1056,256]{1,0:T(8,128)S(1)}, f32[192,256]{1,0:T(8,128)S(1)}, bf16[2,32,192]{2,1,0:T(8,128)(2,1)S(1)}, f32[128,128]{1,0:T(8,128)S(1)}) custom-call(f32[11,32,128]{2,1,0:T(8,128)S(1)} %shard_map.152.refs_0_, f32[11,32,128]{2,1,0:T(8,128)S(1)} %collective-permute-done.4.refs_1_, ...), custom_call_target="tpu_custom_call" | custom-call | tf_op jit(solution)/shard_map/pallas_call | solution.py:42
  19.9 0.9 %collective-permute-done.3.refs_1_ = bf16[16,256]{1,0:T(8,128)(2,1)S(1)} collective-permute-done((bf16[16,256]{1,0:T(8,128)(2,1)S(1)}, bf16[16,256]{1,0:T(8,128)(2,1)S(1)}, u32[]{:S(2)}, u32[]{:S(2)}) %collective-permute-start.3) | collective-permute-done | bytes 8224 | tf_op jit(solution)/shard_map/ppermute | solution.py:743
  20.8 2.3 %shard_map.154 = (f32[88,128]{1,0:T(8,128)S(1)}, f32[5,192,128]{2,1,0:T(8,128)S(1)}) custom-call(bf16[16,256]{1,0:T(8,128)(2,1)S(1)} %shard_map.151.refs_0_, bf16[16,256]{1,0:T(8,128)(2,1)S(1)} %collective-permute-done.3.refs_1_, bf16[96,240]{1,0:T(8,128)(2,1)S(1)} %get-tuple-element.39.refs_4_.refs_2_, f32[792,256]{1,0:T(8,128)S(1)} %get-tuple-element.45.refs_3_, ...), custom_call_target="tpu_custom_call" | custom-call | tf_op jit(solution)/shard_map/pallas_call | solution.py:42
  23.0 1.2 %collective-permute-start.7 = (f32[88,128]{1,0:T(8,128)S(1)}, f32[88,128]{1,0:T(8,128)S(1)}, u32[]{:S(2)}, u32[]{:S(2)}) collective-permute-start(f32[88,128]{1,0:T(8,128)S(1)} %get-tuple-element.50), channel_id=1, source_target_pairs={{0,4},{4,0},{8,12},{12,8},{16,20},{20,16},{24,28},{28,24},{1,5},{5... | collective-permute-start | bytes 135176 | tf_op jit(solution)/shard_map/ppermute | solution.py:780
  24.3 2.8 %collective-permute-done.7 = f32[88,128]{1,0:T(8,128)S(1)} collective-permute-done((f32[88,128]{1,0:T(8,128)S(1)}, f32[88,128]{1,0:T(8,128)S(1)}, u32[]{:S(2)}, u32[]{:S(2)}) %collective-permute-start.7) | collective-permute-done | bytes 45088 | tf_op jit(solution)/shard_map/ppermute | solution.py:780
  27.1 0.8 %collective-permute-start.8 = (f32[88,128]{1,0:T(8,128)S(1)}, f32[88,128]{1,0:T(8,128)S(1)}, u32[]{:S(2)}, u32[]{:S(2)}) collective-permute-start(f32[88,128]{1,0:T(8,128)S(1)} %add.9), channel_id=1, source_target_pairs={{0,8},{4,12},{8,0},{12,4},{16,24},{20,28},{24,16},{28,20},{1,9},{5... | collective-permute-start | bytes 135176 | tf_op jit(solution)/shard_map/ppermute | solution.py:780
  28.0 3.3 %collective-permute-done.8 = f32[88,128]{1,0:T(8,128)S(1)} collective-permute-done((f32[88,128]{1,0:T(8,128)S(1)}, f32[88,128]{1,0:T(8,128)S(1)}, u32[]{:S(2)}, u32[]{:S(2)}) %collective-permute-start.8) | collective-permute-done | bytes 45088 | tf_op jit(solution)/shard_map/ppermute | solution.py:780
  31.2 1.9 %collective-permute-start.9 = (f32[88,128]{1,0:T(8,128)S(1)}, f32[88,128]{1,0:T(8,128)S(1)}, u32[]{:S(2)}, u32[]{:S(2)}) collective-permute-start(f32[88,128]{1,0:T(8,128)S(1)} %add.10), channel_id=1, source_target_pairs={{0,16},{4,20},{8,24},{12,28},{16,0},{20,4},{24,8},{28,12},{1,17},{... | collective-permute-start | bytes 135176 | tf_op jit(solution)/shard_map/ppermute | solution.py:780
  33.1 3.6 %collective-permute-done.9 = f32[88,128]{1,0:T(8,128)S(1)} collective-permute-done((f32[88,128]{1,0:T(8,128)S(1)}, f32[88,128]{1,0:T(8,128)S(1)}, u32[]{:S(2)}, u32[]{:S(2)}) %collective-permute-start.9) | collective-permute-done | bytes 45088 | tf_op jit(solution)/shard_map/ppermute | solution.py:780
  36.7 0.2 shard_map.155
  36.9 0.1 collective-permute-start.10
  37.0 0.7 %shard_map.156 = f32[3,2,16,128]{3,2,1,0:T(8,128)} custom-call(f32[32,128]{1,0:T(8,128)S(1)} %get-tuple-element.51.gamma, f32[5,192,128]{2,1,0:T(8,128)S(1)} %get-tuple-element.52.v), custom_call_target="tpu_custom_call" | custom-call | tf_op jit(solution)/shard_map/pallas_call | solution.py:42
  37.7 0.5 %collective-permute-done.10.other = f32[16,128]{1,0:T(8,128)S(1)} collective-permute-done((f32[16,128]{1,0:T(8,128)S(1)}, f32[16,128]{1,0:T(8,128)S(1)}, u32[]{:S(2)}, u32[]{:S(2)}) %collective-permute-start.10) | collective-permute-done | bytes 8224 | tf_op jit(solution)/shard_map/ppermute | solution.py:789
  38.1 0.6 %shard_map.157 = f32[16,256]{1,0:T(8,128)} custom-call(f32[16,128]{1,0:T(8,128)S(1)} %get-tuple-element.53.own, f32[16,128]{1,0:T(8,128)S(1)} %collective-permute-done.10.other, f32[16,256]{1,0:T(8,128)S(1)} %get-tuple-element.30.refs_2_.bed), custom_call_target="tpu_custom_call" | custom-call | tf_op jit(solution)/shard_map/pallas_call | solution.py:42
  (4 shorter events, 0.0 us)
Async XLA Ops:
  1.8 9.7 %collective-permute-start.2 = (bf16[192,256]{1,0:T(8,128)(2,1)S(1)}, bf16[192,256]{1,0:T(8,128)(2,1)S(1)}, u32[]{:S(2)}, u32[]{:S(2)}) collective-permute-start(bf16[192,256]{1,0:T(8,128)(2,1)S(1)} %get-tuple-element.35), channel_id=1, source_target_pairs={{0,2},{2,0},{1,3},{3,1},{4,6},{6,4},{5,7},{7,5},{8,10},{10,8},{9,1... | collective-permute-start | bytes 294920 | tf_op jit(solution)/shard_map/ppermute | solution.py:717
  4.8 6.7 %collective-permute-start = (f32[11,8,128]{2,1,0:T(8,128)S(1)}, f32[11,8,128]{2,1,0:T(8,128)S(1)}, u32[]{:S(2)}, u32[]{:S(2)}) collective-permute-start(f32[11,8,128]{2,1,0:T(8,128)S(1)} %get-tuple-element.33.pieces_2_), channel_id=1, source_target_pairs={{0,4},{4,8},{8,12},{12,16},{16,20},{20,24},{24,28},{28,0},{1,5},{5... | collective-permute-start | bytes 135176 | tf_op jit(solution)/shard_map/ppermute | solution.py:714
  6.3 5.2 %collective-permute-start.1 = (f32[11,8,128]{2,1,0:T(8,128)S(1)}, f32[11,8,128]{2,1,0:T(8,128)S(1)}, u32[]{:S(2)}, u32[]{:S(2)}) collective-permute-start(f32[11,8,128]{2,1,0:T(8,128)S(1)} %get-tuple-element.34.pieces_1_), channel_id=1, source_target_pairs={{0,28},{4,0},{8,4},{12,8},{16,12},{20,16},{24,20},{28,24},{1,29},{... | collective-permute-start | bytes 135176 | tf_op jit(solution)/shard_map/ppermute | solution.py:715
  11.6 5.6 %collective-permute-start.5 = (f32[11,32,128]{2,1,0:T(8,128)S(1)}, f32[11,32,128]{2,1,0:T(8,128)S(1)}, u32[]{:S(2)}, u32[]{:S(2)}) collective-permute-start(f32[11,32,128]{2,1,0:T(8,128)S(1)} %shard_map.152.refs_0_), channel_id=1, source_target_pairs={{0,2},{2,0},{1,3},{3,1},{4,6},{6,4},{5,7},{7,5},{8,10},{10,8},{9,1... | collective-permute-start | bytes 540680 | tf_op jit(solution)/shard_map/ppermute | solution.py:733
  15.5 2.2 %collective-permute-start.4 = (f32[11,32,128]{2,1,0:T(8,128)S(1)}, f32[11,32,128]{2,1,0:T(8,128)S(1)}, u32[]{:S(2)}, u32[]{:S(2)}) collective-permute-start(f32[11,32,128]{2,1,0:T(8,128)S(1)} %shard_map.152.refs_0_), channel_id=1, source_target_pairs={{0,1},{1,0},{2,3},{3,2},{4,5},{5,4},{6,7},{7,6},{8,9},{9,8},{10,11... | collective-permute-start | bytes 540680 | tf_op jit(solution)/shard_map/ppermute | solution.py:736
  17.1 1.4 %collective-permute-start.6 = (f32[11,32,128]{2,1,0:T(8,128)S(1)}, f32[11,32,128]{2,1,0:T(8,128)S(1)}, u32[]{:S(2)}, u32[]{:S(2)}) collective-permute-start(f32[11,32,128]{2,1,0:T(8,128)S(1)} %collective-permute-done.5.refs_2_), channel_id=1, source_target_pairs={{0,1},{1,0},{2,3},{3,2},{4,5},{5,4},{6,7},{7,6},{8,9},{9,8},{10,11... | collective-permute-start | bytes 540680 | tf_op jit(solution)/shard_map/ppermute | solution.py:738
  17.1 3.7 %collective-permute-start.3 = (bf16[16,256]{1,0:T(8,128)(2,1)S(1)}, bf16[16,256]{1,0:T(8,128)(2,1)S(1)}, u32[]{:S(2)}, u32[]{:S(2)}) collective-permute-start(bf16[16,256]{1,0:T(8,128)(2,1)S(1)} %shard_map.151.refs_0_), channel_id=1, source_target_pairs={{0,2},{2,0},{1,3},{3,1},{4,6},{6,4},{5,7},{7,5},{8,10},{10,8},{9,1... | collective-permute-start | bytes 24584 | tf_op jit(solution)/shard_map/ppermute | solution.py:743
  23.0 4.1 %collective-permute-start.7 = (f32[88,128]{1,0:T(8,128)S(1)}, f32[88,128]{1,0:T(8,128)S(1)}, u32[]{:S(2)}, u32[]{:S(2)}) collective-permute-start(f32[88,128]{1,0:T(8,128)S(1)} %get-tuple-element.50), channel_id=1, source_target_pairs={{0,4},{4,0},{8,12},{12,8},{16,20},{20,16},{24,28},{28,24},{1,5},{5... | collective-permute-start | bytes 135176 | tf_op jit(solution)/shard_map/ppermute | solution.py:780
  27.1 4.1 %collective-permute-start.8 = (f32[88,128]{1,0:T(8,128)S(1)}, f32[88,128]{1,0:T(8,128)S(1)}, u32[]{:S(2)}, u32[]{:S(2)}) collective-permute-start(f32[88,128]{1,0:T(8,128)S(1)} %add.9), channel_id=1, source_target_pairs={{0,8},{4,12},{8,0},{12,4},{16,24},{20,28},{24,16},{28,20},{1,9},{5... | collective-permute-start | bytes 135176 | tf_op jit(solution)/shard_map/ppermute | solution.py:780
  31.2 5.5 %collective-permute-start.9 = (f32[88,128]{1,0:T(8,128)S(1)}, f32[88,128]{1,0:T(8,128)S(1)}, u32[]{:S(2)}, u32[]{:S(2)}) collective-permute-start(f32[88,128]{1,0:T(8,128)S(1)} %add.10), channel_id=1, source_target_pairs={{0,16},{4,20},{8,24},{12,28},{16,0},{20,4},{24,8},{28,12},{1,17},{... | collective-permute-start | bytes 135176 | tf_op jit(solution)/shard_map/ppermute | solution.py:780
  36.9 1.2 %collective-permute-start.10 = (f32[16,128]{1,0:T(8,128)S(1)}, f32[16,128]{1,0:T(8,128)S(1)}, u32[]{:S(2)}, u32[]{:S(2)}) collective-permute-start(f32[16,128]{1,0:T(8,128)S(1)} %get-tuple-element.53.own), channel_id=1, source_target_pairs={{0,1},{1,0},{2,3},{3,2},{4,5},{5,4},{6,7},{7,6},{8,9},{9,8},{10,11... | collective-permute-start | bytes 24584 | tf_op jit(solution)/shard_map/ppermute | solution.py:789
